TPU v7x, 32 devices: a whole 2x2x4 slice. The times are simulated.
32 devices in a mesh: tile: 4 (over y, core), dp: 8 (over z, x).
Axes of the slice: x: 2, y: 2, z: 4, core: 2. Of those that a mesh axis runs over, the one named last changes fastest.
Arguments:
- observed: float32 [8, 2, 8, 32], P('dp', None, 'tile'), may hold values from -6 to 6
- targets: float32 [8, 2, 8, 32], P('dp', None, 'tile'), may hold values from -6 to 6
- pixel_mask: int32 [8, 2, 8, 32], P('dp', None, 'tile'), may hold values 0 or 1
- lengths: int32 [8], P('dp'), may hold values from 1 to 2, as said below
- step_count: int32 [1], replicated, may hold values from 2 to 20
- kernels: float32 [1, 12800, 1024], P(None, 'dp'), may hold values from -0.0546875 to 0.0546875
- kernel_moment: float32 [1, 12800, 1024], P(None, 'dp'), may hold values from -7.6293945e-06 to 7.6293945e-06
- kernel_second: float32 [1, 12800, 1024], P(None, 'dp'), may hold values from 1.9073486e-12 to 7.6293945e-12
- norm_params: float32 [2, 1, 1024], replicated
- norm_moment: float32 [2, 1, 1024], replicated, may hold values from -1.5258789e-05 to 1.5258789e-05
- norm_second: float32 [2, 1, 1024], replicated, may hold values from 7.6293945e-12 to 3.0517578e-11
- end_params: float32 [3, 256], replicated
- end_moment: float32 [3, 256], replicated, may hold values from -7.6293945e-05 to 7.6293945e-05
- end_second: float32 [3, 256], replicated, may hold values from 1.9073486e-10 to 7.6293943e-10
- head_bias: float32 [1], replicated, may hold values from -3 to 3
- head_moment: float32 [1], replicated, may hold values from -0.0546875 to 0.0546875
- head_second: float32 [1], replicated, may hold values from 7.6293945e-05 to 0.00030517578
- hidden_init: float32 [1, 8, 8, 32, 256], P(None, 'dp', 'tile'), may hold values from -0.9 to 0.9
- cells_init: float32 [1, 8, 8, 32, 256], P(None, 'dp', 'tile'), may hold values from -5 to 5
Outputs:
- loss_value: float32 [], replicated
- grad_norm: float32 [], replicated
- kernels_new: float32 [1, 12800, 1024], P(None, 'dp')
- kernel_moment_new: float32 [1, 12800, 1024], P(None, 'dp')
- kernel_second_new: float32 [1, 12800, 1024], P(None, 'dp')
- norm_new: float32 [2, 1, 1024], replicated
- norm_moment_new: float32 [2, 1, 1024], replicated
- norm_second_new: float32 [2, 1, 1024], replicated
- end_new: float32 [3, 256], replicated
- end_moment_new: float32 [3, 256], replicated
- end_second_new: float32 [3, 256], replicated
- head_new: float32 [1], replicated
- head_moment_new: float32 [1], replicated
- head_second_new: float32 [1], replicated
- hidden_final: float32 [1, 8, 8, 32, 256], P(None, 'dp', 'tile')
- cells_final: float32 [1, 8, 8, 32, 256], P(None, 'dp', 'tile')
Inputs may be any that keep to these rules, and one draw needn't show every extreme that they name: `lengths`: some stream has all 2 frames counting and some only one.
All inputs are finite; a program needn't handle non-finite values. No bound on the sum of `pixel_mask` on one device may be relied on, other than what follows from the above.
Results may differ from a plain program's by a relative error of at most 0.0003.
The roundings to bfloat16 on the way count: a program that leaves them out, or rounds other values in their place, can miss the bound.
Values may be sent and summed in bfloat16 or wider, within the bound.
No kernel may reach another device: no remote copies, remote signals or barrier semaphores. Data moves between devices by JAX's collectives and lax.ppermute only.
A program may use at most 192 MiB of HBM per device.

v0:
```python
import jax
import jax.numpy as jnp
from jax import lax
from jax.sharding import PartitionSpec as P

IN_DIM = 512
KERNEL = 5
GROUP_SIZE = 64


clip_limit = 0.005
small_rate = 0.1


def padded_2(cells, sides, width):
    for axis, dim in sides:
        count = lax.axis_size(axis)
        ends = count - 1
        head = lax.slice_in_dim(cells, 0, width, axis=dim)
        tail = lax.slice_in_dim(cells, cells.shape[dim] - width, cells.shape[dim], axis=dim)
        cells = jnp.concatenate(
            [
                lax.ppermute(tail, axis, [(i, (i + 1) % count) for i in range(ends)]),
                cells,
                lax.ppermute(head, axis, [((i + 1) % count, i) for i in range(ends)]),
            ],
            axis=dim,
        )
    return cells


def group_norm(gates, gain, shift):
    full_shape = gates.shape
    grouped = gates.reshape(full_shape[:-1] + (full_shape[-1] // GROUP_SIZE, GROUP_SIZE))
    centred = grouped - jnp.mean(grouped, axis=-1, keepdims=True)
    spread = jnp.mean(centred * centred, axis=-1, keepdims=True)
    return (centred * lax.rsqrt(spread + 1e-05)).reshape(full_shape) * gain + shift


def lstm_cell(gates, cells_prev, gain, shift):
    normed = group_norm(gates, gain, shift)
    quarter = normed.shape[-1] // 4
    input_gate = jax.nn.sigmoid(normed[..., :quarter])
    forget_gate = jax.nn.sigmoid(normed[..., quarter : 2 * quarter])
    candidate = jnp.tanh(normed[..., 2 * quarter : 3 * quarter])
    output_gate = jax.nn.sigmoid(normed[..., 3 * quarter :])
    cells_next = forget_gate * cells_prev + input_gate * candidate
    return (output_gate * jnp.tanh(cells_next), cells_next)


def unfold(padded, rows, columns):
    pieces = []
    for row_off in range(KERNEL):
        for col_off in range(KERNEL):
            pieces.append(padded[:, row_off : row_off + rows, col_off : col_off + columns, :])
    joined = jnp.concatenate(pieces, axis=-1)
    return joined.reshape(-1, joined.shape[-1])


def pad_columns(values):
    margin = KERNEL // 2
    return jnp.pad(values, ((0, 0), (0, 0), (margin, margin), (0, 0)))


def layer_forward(weight_full, gain, shift, inputs_low, hidden_start, cells_start):
    rows, columns = (hidden_start.shape[1], hidden_start.shape[2])
    hidden_low = hidden_start.astype(jnp.bfloat16)
    cells = cells_start
    kept = []
    outputs = []
    outputs_low = []
    hidden = hidden_start
    for frame_no in range(len(inputs_low)):
        joined = jnp.concatenate([inputs_low[frame_no], hidden_low], axis=-1)
        padded = padded_2(joined, (("tile", 1),), KERNEL // 2)
        padded = pad_columns(padded)
        gates = jnp.dot(
            unfold(padded, rows, columns), weight_full, preferred_element_type=jnp.float32
        )
        gates = gates.reshape(hidden_start.shape[:3] + (weight_full.shape[1],))
        kept.append((padded, gates, cells))
        hidden, cells = lstm_cell(gates, cells, gain, shift)
        hidden_low = hidden.astype(jnp.bfloat16)
        outputs.append(hidden)
        outputs_low.append(hidden_low)
    return (outputs, outputs_low, kept, hidden, cells)


def layer_backward(weight_full, gain, shift, kept, grad_above):
    pixel_shape = kept[0][1].shape
    rows, columns, gate_dim = (pixel_shape[1], pixel_shape[2], pixel_shape[3])
    in_dim = weight_full.shape[0] // (KERNEL * KERNEL)
    half = in_dim // 2
    flipped = weight_full.reshape(KERNEL, KERNEL, in_dim, gate_dim)[::-1, ::-1]
    flipped = flipped.transpose(0, 1, 3, 2).reshape(KERNEL * KERNEL * gate_dim, in_dim)
    grad_weight = jnp.zeros(weight_full.shape, jnp.float32)
    grad_gain = jnp.zeros(gain.shape, jnp.float32)
    grad_shift = jnp.zeros(shift.shape, jnp.float32)
    grad_hidden = jnp.zeros(pixel_shape[:3] + (half,), jnp.float32)
    grad_cells = jnp.zeros(pixel_shape[:3] + (half,), jnp.float32)
    grad_inputs = [None] * len(kept)
    for frame_no in reversed(range(len(kept))):
        padded, gates, cells_prev = kept[frame_no]
        unused, pull = jax.vjp(lstm_cell, gates, cells_prev, gain, shift)
        grad_gates, grad_cells, part_gain, part_shift = pull(
            (grad_above[frame_no] + grad_hidden, grad_cells)
        )
        grad_gain = grad_gain + part_gain
        grad_shift = grad_shift + part_shift
        gates_low = grad_gates.astype(jnp.bfloat16)
        grad_weight = grad_weight + lax.dot_general(
            unfold(padded, rows, columns),
            gates_low.reshape(-1, gate_dim),
            (((0,), (0,)), ((), ())),
            preferred_element_type=jnp.float32,
        )
        spread = padded_2(gates_low, (("tile", 1),), KERNEL // 2)
        spread = pad_columns(spread)
        grad_joined = jnp.dot(
            unfold(spread, rows, columns), flipped, preferred_element_type=jnp.float32
        )
        grad_joined = grad_joined.reshape(pixel_shape[:3] + (in_dim,))
        grad_inputs[frame_no] = grad_joined[..., :half]
        grad_hidden = grad_joined[..., half:]
    return (grad_weight, grad_gain, grad_shift, grad_inputs)


def adamw(weight, moment, second, grad, rate, correction):
    moment_new = 0.5 * moment + 0.5 * grad
    second_new = 0.5 * second + 0.5 * grad * grad
    update = moment_new / correction / (jnp.sqrt(second_new / correction) + 1e-08)
    return (weight - rate * (update + 0.01 * weight), moment_new, second_new)


def per_device(
    observed,
    targets,
    pixel_mask,
    lengths,
    step_count,
    kernels,
    kernel_moment,
    kernel_second,
    norm_params,
    norm_moment,
    norm_second,
    end_params,
    end_moment,
    end_second,
    head_bias,
    head_moment,
    head_second,
    hidden_init,
    cells_init,
):
    frame_total = observed.shape[1]
    layers = kernels.shape[0]
    frame_ids = lax.broadcasted_iota(jnp.int32, (1, frame_total), 1)
    counted = (frame_ids < lengths[:, None]).astype(jnp.float32)
    valid = pixel_mask.astype(jnp.float32) * counted[:, :, None, None]
    count = jnp.maximum(lax.psum(jnp.sum(valid), ("tile", "dp")), 1.0)
    inputs_low = [
        (end_params[0] * observed[:, frame_no, :, :, None] + end_params[1]).astype(jnp.bfloat16)
        for frame_no in range(frame_total)
    ]
    outputs = []
    layer_no = 0
    weight_full = lax.all_gather(kernels[layer_no].astype(jnp.bfloat16), "dp", axis=0, tiled=True)
    outputs, outputs_low, kept, hidden, cells = layer_forward(
        weight_full,
        norm_params[0, layer_no],
        norm_params[1, layer_no],
        inputs_low,
        hidden_init[layer_no],
        cells_init[layer_no],
    )
    stored_kept = [kept]
    hidden_list = [hidden]
    cells_list = [cells]
    loss_sum = jnp.zeros((), jnp.float32)
    grad_head_weight = jnp.zeros(end_params.shape[1:], jnp.float32)
    grad_head = jnp.zeros((1,), jnp.float32)
    grad_above = []
    for frame_no in range(frame_total):
        predicted = jnp.sum(outputs[frame_no] * end_params[2], axis=-1) + head_bias[0]
        error = predicted - targets[:, frame_no]
        weighted = valid[:, frame_no] * error
        loss_sum = loss_sum + jnp.sum(weighted * error)
        grad_pred = 2.0 * weighted / count
        grad_head = grad_head + jnp.sum(grad_pred)
        grad_head_weight = grad_head_weight + jnp.sum(
            grad_pred[..., None] * outputs[frame_no], axis=(0, 1, 2)
        )
        grad_above.append(grad_pred[..., None] * end_params[2])
    kernel_grads = [None] * layers
    gain_grads = [None] * layers
    shift_grads = [None] * layers
    for layer_no in reversed(range(layers)):
        weight_full = lax.all_gather(
            kernels[layer_no].astype(jnp.bfloat16), "dp", axis=0, tiled=True
        )
        grad_weight, grad_gain, grad_shift, grad_inputs = layer_backward(
            weight_full,
            norm_params[0, layer_no],
            norm_params[1, layer_no],
            stored_kept[layer_no],
            grad_above,
        )
        kernel_grads[layer_no] = grad_weight
        gain_grads[layer_no] = grad_gain
        shift_grads[layer_no] = grad_shift
        grad_above = grad_inputs
    grad_lift_weight = jnp.zeros(end_params.shape[1:], jnp.float32)
    grad_lift_bias = jnp.zeros(end_params.shape[1:], jnp.float32)
    for frame_no in range(frame_total):
        grad_lift_weight = grad_lift_weight + jnp.sum(
            grad_above[frame_no] * observed[:, frame_no, :, :, None], axis=(0, 1, 2)
        )
        grad_lift_bias = grad_lift_bias + jnp.sum(grad_above[frame_no], axis=(0, 1, 2))
    grad_norms = jnp.stack([jnp.stack(gain_grads), jnp.stack(shift_grads)])
    grad_ends = jnp.stack([grad_lift_weight, grad_lift_bias, grad_head_weight])
    grad_kernels = jnp.stack(kernel_grads)
    shard = lax.psum_scatter(grad_kernels, "dp", scatter_dimension=1, tiled=True)
    shard = lax.psum(shard, "tile")
    local_square = jnp.sum(shard * shard)
    grad_norms, grad_ends, grad_head, loss_sum = lax.psum(
        (grad_norms, grad_ends, grad_head, loss_sum), ("tile", "dp")
    )
    kernel_square = lax.psum(local_square, "dp")
    squares = (
        kernel_square
        + jnp.sum(grad_norms * grad_norms)
        + jnp.sum(grad_ends * grad_ends)
        + jnp.sum(grad_head * grad_head)
    )
    grad_norm = jnp.sqrt(squares)
    factor = clip_limit / jnp.maximum(grad_norm, clip_limit)
    correction = 1.0 - jnp.power(0.5, step_count[0].astype(jnp.float32))
    kernel_rate = (KERNEL * KERNEL * IN_DIM) ** (-0.5)
    kern_out = adamw(kernels, kernel_moment, kernel_second, shard * factor, kernel_rate, correction)
    norm_out = adamw(
        norm_params, norm_moment, norm_second, grad_norms * factor, small_rate, correction
    )
    end_out = adamw(end_params, end_moment, end_second, grad_ends * factor, small_rate, correction)
    head_out = adamw(
        head_bias, head_moment, head_second, grad_head * factor, small_rate, correction
    )
    loss_value = loss_sum / count
    return (
        loss_value,
        grad_norm,
        kern_out[0],
        kern_out[1],
        kern_out[2],
        norm_out[0],
        norm_out[1],
        norm_out[2],
        end_out[0],
        end_out[1],
        end_out[2],
        head_out[0],
        head_out[1],
        head_out[2],
        jnp.stack(hidden_list),
        jnp.stack(cells_list),
    )


def solution(mesh):
    placed = (
        P("dp", None, "tile", None),
        P("dp", None, "tile", None),
        P("dp", None, "tile", None),
        P("dp"),
        P(),
        P(None, "dp", None),
        P(None, "dp", None),
        P(None, "dp", None),
        P(),
        P(),
        P(),
        P(),
        P(),
        P(),
        P(),
        P(),
        P(),
        P(None, "dp", "tile", None, None),
        P(None, "dp", "tile", None, None),
    )
    return jax.shard_map(
        per_device,
        mesh=mesh,
        in_specs=placed,
        out_specs=(
            P(),
            P(),
            P(None, "dp", None),
            P(None, "dp", None),
            P(None, "dp", None),
            P(),
            P(),
            P(),
            P(),
            P(),
            P(),
            P(),
            P(),
            P(),
            P(None, "dp", "tile", None, None),
            P(None, "dp", "tile", None, None),
        ),
        check_vma=False,
    )
```

profile of v0, /device:TPU:0, one launch (start us, length us, event | category | flops | bytes accessed | tf_op | source)
XLA Modules:
  0.0 1688.5 jit_solution(5633768059832277343)
XLA Ops:
  7.2 5.1 convert_element_type.95
  13.2 1.3 collective-permute-start.1
  14.5 3.0 collective-permute-start
  18.2 0.7 fusion.79
  18.9 85.6 %psum.50 = f32[]{:T(128)} all-reduce(f32[]{:T(128)} %get-tuple-element.65), channel_id=1, replica_groups=mesh['tile'=4,'dp'=8] {'tile','dp'}, use_global_device_ids=true, to_apply=%region_10.11 | all-reduce | flops 1 | bytes 8 | tf_op jit(solution)/shard_map/psum | solution.py:161
  107.0 1.2 copy-done.1
  108.5 408.1 %all-gather.3.cloned.1.call-done = bf16[1,12800,1024]{2,1,0:T(8,128)(2,1)} async-done(((bf16[1,1600,1024]{2,1,0:T(8,128)(2,1)}), bf16[1,12800,1024]{2,1,0:T(8,128)(2,1)}) %all-gather.3.cloned.1.call-update) | async-done | bytes 26214416 | tf_op jit(solution)/shard_map/all_gather | solution.py:168
  516.7 10.8 fusion.3
  529.2 0.8 multiply_add_fusion.2
  530.1 1.3 collective-permute-start.3
  531.4 3.0 collective-permute-start.2
  534.4 18.4 %reverse_bitcast_fusion = bf16[5,5,1024,512]{2,3,1,0:T(8,128)(2,1)} fusion(bf16[5,5,512,1024]{3,2,1,0:T(8,128)(2,1)} %bitcast.214), kind=kLoop, calls=%fused_computation.6 | loop fusion | bytes 52428800 | tf_op jit(solution)/shard_map/transpose | solution.py:95
  552.8 33.9 %copy.35 = bf16[5,5,1024,512]{3,2,1,0:T(8,128)(2,1)} copy(bf16[5,5,1024,512]{2,3,1,0:T(8,128)(2,1)} %reverse_bitcast_fusion) | data formatting | bytes 52428800 | tf_op jit(solution)/shard_map/transpose | solution.py:95
  588.0 0.7 copy-done
  588.8 10.8 fusion.1
  601.3 0.8 multiply_add_fusion.1
  602.0 0.7 fusion.74
  605.0 1.0 fusion.25
  606.1 1.3 collective-permute-start.5
  607.4 3.8 collective-permute-start.4
  611.2 21.6 %fusion.11 = f32[12800,1024,1]{1,0,2:T(8,128)} fusion(bf16[1,2,32,12800]{3,2,1,0:T(8,128)(2,1)} %copy-done, bf16[1,2,32,1024]{3,2,1,0:T(8,128)(2,1)S(1)} %fusion.25), kind=kOutput, calls=%fused_computation.17 | convolution fusion | flops 1677721600 | bytes 54198272 | tf_op jit(solution)/shard_map/dot_general | solution.py:111
  633.8 10.8 fusion.13
  646.9 1.0 fusion.27
  647.9 33.5 %fusion = f32[1,12800,1024]{2,1,0:T(8,128)} fusion(f32[12800,1024,1]{1,0,2:T(8,128)} %fusion.11, bf16[1,2,32,12800]{3,2,1,0:T(8,128)(2,1)S(1)} %copy-done.2, bf16[1,2,32,1024]{3,2,1,0:T(8,128)(2,1)S(1)} %fusion.27), kind=kOutput, calls=%fused_computation.1 | convolution fusion | flops 1690828800 | bytes 106627072 | tf_op jit(solution)/shard_map/dot_general | solution.py:111
  683.5 1.3 collective-permute-start.7
  684.8 4.5 collective-permute-start.6
  693.4 0.7 constant_dynamic-update-slice_fusion.152
  694.8 0.7 constant_dynamic-update-slice_fusion.150
  695.5 0.7 constant_dynamic-update-slice_fusion.149
  696.8 0.7 constant_dynamic-update-slice_fusion.147
  698.2 0.7 constant_dynamic-update-slice_fusion.145
  698.9 0.7 constant_dynamic-update-slice_fusion.144
  700.2 0.7 constant_dynamic-update-slice_fusion.142
  701.6 0.7 constant_dynamic-update-slice_fusion.140
  702.3 0.7 constant_dynamic-update-slice_fusion.139
  703.6 0.7 constant_dynamic-update-slice_fusion.137
  705.0 0.7 constant_dynamic-update-slice_fusion.135
  705.7 793.9 %reduce-scatter.2.cloned.1.call-done = f32[1,1600,1024]{2,1,0:T(8,128)} async-done(((f32[1,12800,1024]{2,1,0:T(8,128)}), f32[1,1600,1024]{2,1,0:T(8,128)}) %reduce-scatter.2.cloned.1.call-update) | async-done | bytes 6553616 | tf_op jit(solution)/shard_map/reduce_scatter | solution.py:223
  1499.6 0.7 constant_dynamic-update-slice_fusion.134
  1501.0 0.7 constant_dynamic-update-slice_fusion.132
  1502.4 0.7 constant_dynamic-update-slice_fusion.130
  1503.0 0.7 constant_dynamic-update-slice_fusion.129
  1503.7 12.9 fusion.16
  1516.8 41.4 %all-reduce.12 = (f32[]{:T(128)}, f32[2,1,1024]{2,1,0:T(1,128)S(1)}, f32[3,256]{1,0:T(4,128)S(1)}, f32[1]{0:T(128)}) all-reduce(f32[]{:T(128)S(6)} %add.410, f32[2,1,1024]{2,1,0:T(1,128)S(1)} %pad_maximum_fusion.14, f32[3,256]{1,0:T(4,128)S(1)} %pad_maximum_fusion.15, f32[1]{0:T(128)} %bitcast.95), channel_id=1, replica_groups=mesh['tile'=4,'dp'=8] {'tile','dp'}, use_global_device_ids=true, to_apply=%region_8.9 | all-reduce | flops 2818 | bytes 22544 | tf_op jit(solution)/shard_map/psum | solution.py:226
  1560.1 66.4 %all-reduce.15.cloned.1.call-done = f32[1,1600,1024]{2,1,0:T(8,128)} async-done(((f32[1,1600,1024]{2,1,0:T(8,128)}), f32[1,1600,1024]{2,1,0:T(8,128)}) %all-reduce.15.cloned.1.call-update) | async-done | bytes 6553616 | tf_op jit(solution)/shard_map/psum | solution.py:224
  1626.4 5.1 multiply_reduce_fusion
  1632.9 22.0 %psum.52 = f32[]{:T(128)} all-reduce(f32[]{:T(128)} %multiply_reduce_fusion), channel_id=1, replica_groups=mesh['tile'=4,'dp'=8] {'dp'}, use_global_device_ids=true, to_apply=%region_18.19 | all-reduce | flops 1 | bytes 8 | tf_op jit(solution)/shard_map/psum | solution.py:229
  1659.0 17.3 %multiply_subtract_fusion = (f32[1,1600,1024]{2,1,0:T(8,128)}, f32[1,1600,1024]{2,1,0:T(8,128)}, f32[1,1600,1024]{2,1,0:T(8,128)}) fusion(f32[1,1600,1024]{2,1,0:T(8,128)} %param.24, f32[]{:T(128)} %bitcast.97, f32[1,1600,1024]{2,1,0:T(8,128)} %all-reduce.15.cloned.1.call-done, f32[]{:T(128)} %div.177, f32[1,1600,1024]{2,1,0:T(8,128)} %param.26, ...), kind=kLoop, calls=%fused_computation.10 | loop fusion | flops 24576000 | bytes 45875208 | tf_op jit(solution)/shard_map/sub | solution.py:132
  (265 shorter events, 21.7 us)
Async XLA Ops:
  7.2 509.5 %all-gather.3.cloned.1.call-start = ((), (), s32[]{:S(2)}) async-start(), calls=%async_computation.3 | async-start | bytes 29491200 | tf_op jit(solution)/shard_map/all_gather | solution.py:168
  12.3 0.7 copy-start.18
  12.3 0.7 copy-start.11
  12.3 0.9 copy-start.4
  12.3 5.9 copy-start.7
  12.3 5.9 copy-start.19
  12.4 1487.3 %reduce-scatter.2.cloned.1.call-start = ((), (), s32[]{:S(2)}) async-start(), calls=%async_computation.1 | async-start | bytes 58982400 | tf_op jit(solution)/shard_map/reduce_scatter | solution.py:223
  13.0 93.6 %copy-start.9 = (f32[2,32]{1,0:T(2,128)}, f32[2,32]{1,0:T(2,128)S(1)}, u32[]{:S(2)}) copy-start(f32[2,32]{1,0:T(2,128)S(1)} %get-tuple-element.135) | copy-start | bytes 772
  13.2 92.8 %collective-permute-start.1 = (bf16[1,2,32,512]{3,2,1,0:T(8,128)(2,1)S(1)}, bf16[1,2,32,512]{3,2,1,0:T(8,128)(2,1)S(1)}, u32[]{:S(2)}, u32[]{:S(2)}) collective-permute-start(bf16[1,2,32,512]{3,2,1,0:T(8,128)(2,1)S(1)} %pad_maximum_fusion.12), channel_id=1, source_target_pairs={{8,0},{16,8},{24,16},{9,1},{17,9},{25,17},{10,2},{18,10},{26,18},{... | collective-permute-start | bytes 196616 | tf_op jit(solution)/shard_map/ppermute | solution.py:25
  14.5 91.5 %collective-permute-start = (bf16[1,2,32,512]{3,2,1,0:T(8,128)(2,1)S(1)}, bf16[1,2,32,512]{3,2,1,0:T(8,128)(2,1)S(1)}, u32[]{:S(2)}, u32[]{:S(2)}) collective-permute-start(bf16[1,2,32,512]{3,2,1,0:T(8,128)(2,1)S(1)} %pad_maximum_fusion.12), channel_id=1, source_target_pairs={{0,8},{8,16},{16,24},{1,9},{9,17},{17,25},{2,10},{10,18},{18,26},{... | collective-permute-start | bytes 196616 | tf_op jit(solution)/shard_map/ppermute | solution.py:23
  107.0 1.2 copy-start.1
  528.8 1.2 copy-start.5
  530.1 56.6 %collective-permute-start.3 = (bf16[1,2,32,512]{3,2,1,0:T(8,128)(2,1)S(1)}, bf16[1,2,32,512]{3,2,1,0:T(8,128)(2,1)S(1)}, u32[]{:S(2)}, u32[]{:S(2)}) collective-permute-start(bf16[1,2,32,512]{3,2,1,0:T(8,128)(2,1)S(1)} %pad_maximum_fusion.13), channel_id=1, source_target_pairs={{8,0},{16,8},{24,16},{9,1},{17,9},{25,17},{10,2},{18,10},{26,18},{... | collective-permute-start | bytes 196616 | tf_op jit(solution)/shard_map/ppermute | solution.py:25
  531.4 55.3 %collective-permute-start.2 = (bf16[1,2,32,512]{3,2,1,0:T(8,128)(2,1)S(1)}, bf16[1,2,32,512]{3,2,1,0:T(8,128)(2,1)S(1)}, u32[]{:S(2)}, u32[]{:S(2)}) collective-permute-start(bf16[1,2,32,512]{3,2,1,0:T(8,128)(2,1)S(1)} %pad_maximum_fusion.13), channel_id=1, source_target_pairs={{0,8},{8,16},{16,24},{1,9},{9,17},{17,25},{2,10},{10,18},{18,26},{... | collective-permute-start | bytes 196616 | tf_op jit(solution)/shard_map/ppermute | solution.py:23
  587.6 1.2 copy-start
  601.1 1.8 copy-start.15
  602.8 41.9 %copy-start.3 = (f32[1,2,32,256]{3,2,1,0:T(8,128)}, f32[1,2,32,256]{3,2,1,0:T(8,128)S(1)}, u32[]{:S(2)}) copy-start(f32[1,2,32,256]{3,2,1,0:T(8,128)S(1)} %get-tuple-element.37) | copy-start | bytes 196612
  606.1 26.7 %collective-permute-start.5 = (bf16[1,2,32,1024]{3,2,1,0:T(8,128)(2,1)S(1)}, bf16[1,2,32,1024]{3,2,1,0:T(8,128)(2,1)S(1)}, u32[]{:S(2)}, u32[]{:S(2)}) collective-permute-start(bf16[1,2,32,1024]{3,2,1,0:T(8,128)(2,1)S(1)} %fusion.25), channel_id=1, source_target_pairs={{8,0},{16,8},{24,16},{9,1},{17,9},{25,17},{10,2},{18,10},{26,18},{... | collective-permute-start | bytes 393224 | tf_op jit(solution)/shard_map/ppermute | solution.py:25
  607.4 25.4 %collective-permute-start.4 = (bf16[1,2,32,1024]{3,2,1,0:T(8,128)(2,1)S(1)}, bf16[1,2,32,1024]{3,2,1,0:T(8,128)(2,1)S(1)}, u32[]{:S(2)}, u32[]{:S(2)}) collective-permute-start(bf16[1,2,32,1024]{3,2,1,0:T(8,128)(2,1)S(1)} %fusion.25), channel_id=1, source_target_pairs={{0,8},{8,16},{16,24},{1,9},{9,17},{17,25},{2,10},{10,18},{18,26},{... | collective-permute-start | bytes 393224 | tf_op jit(solution)/shard_map/ppermute | solution.py:23
  633.8 11.0 copy-start.6
  646.3 1.6 copy-start.2
  681.5 944.9 %all-reduce.15.cloned.1.call-start = ((), (), s32[]{:S(2)}) async-start(), calls=%async_computation.2 | async-start | bytes 13107200 | tf_op jit(solution)/shard_map/psum | solution.py:224
  683.5 9.1 collective-permute-start.7
  684.8 7.8 collective-permute-start.6
  1503.7 12.9 copy-start.10
  1560.0 97.7 %copy-start.8 = (f32[2,1,1024]{2,1,0:T(1,128)S(1)}, f32[2,1,1024]{2,1,0:T(1,128)}, u32[]{:S(2)}) copy-start(f32[2,1,1024]{2,1,0:T(1,128)} %param.27) | copy-start | bytes 24580
  1560.0 97.7 %copy-start.13 = (f32[2,1,1024]{2,1,0:T(1,128)S(1)}, f32[2,1,1024]{2,1,0:T(1,128)}, u32[]{:S(2)}) copy-start(f32[2,1,1024]{2,1,0:T(1,128)} %param.29) | copy-start | bytes 24580
  1560.0 97.7 %copy-start.14 = (f32[2,1,1024]{2,1,0:T(1,128)S(1)}, f32[2,1,1024]{2,1,0:T(1,128)}, u32[]{:S(2)}) copy-start(f32[2,1,1024]{2,1,0:T(1,128)} %param.28) | copy-start | bytes 24580
  1560.0 98.3 %copy-start.12 = (f32[3,256]{1,0:T(4,128)S(1)}, f32[3,256]{1,0:T(4,128)}, u32[]{:S(2)}) copy-start(f32[3,256]{1,0:T(4,128)} %param.30) | copy-start | bytes 9220
  1560.0 98.3 %copy-start.16 = (f32[3,256]{1,0:T(4,128)S(1)}, f32[3,256]{1,0:T(4,128)}, u32[]{:S(2)}) copy-start(f32[3,256]{1,0:T(4,128)} %param.32) | copy-start | bytes 9220
  1560.0 98.3 %copy-start.17 = (f32[3,256]{1,0:T(4,128)S(1)}, f32[3,256]{1,0:T(4,128)}, u32[]{:S(2)}) copy-start(f32[3,256]{1,0:T(4,128)} %param.31) | copy-start | bytes 9220
Sparse Core Ops, SparseCore 0:
  12.5 504.1 all-gather.2
  681.6 817.9 reduce-scatter.1
  1502.0 124.3 all-reduce.14
where the time goes:
time: 1690 us
  waiting for transfers between devices  1270 us (75%)
  blocking collectives  149 us (9%)
  matrix products  100 us (6%)
  local copies, waits for them, and re-layouts  76.5 us (5%)
  other arithmetic  41.9 us (2%)
  between operations  32.4 us (2%)
  starting transfers between devices  19.7 us (1%)
    reduce_scatter x1, waiting for transfers between devices, per_device(): lax.psum_scatter(grad_kernels, 'dp', scatter_dimension=1, tiled=True)  794 us
    all_gather x1, waiting for transfers between devices, per_device(): lax.all_gather(kernels[layer_no].astype(jnp.bfloat16), 'dp', axis=0, tile...  408 us
    psum x1, blocking collectives, per_device(): count = jnp.maximum(lax.psum(jnp.sum(valid), ('tile', 'dp')), 1.0)  85.6 us
    psum x1, waiting for transfers between devices, per_device(): shard = lax.psum(shard, 'tile')  66.4 us
    dot_general x2, matrix products, layer_backward(): lax.dot_general(unfold(padded, rows, columns), gates_low.reshape(-1, gate...  55.1 us
    transpose x2, local copies, waits for them, and re-layouts, layer_backward(): flipped.transpose(0, 1, 3, 2).reshape(KERNEL * KERNEL * gate_dim, in_dim)  52.3 us
    psum x1, blocking collectives, per_device(): lax.psum((grad_norms, grad_ends, grad_head, loss_sum), ('tile', 'dp'))  41.4 us
  transfers between devices with their start and end apart: 11, of which 3 were waited for; matrix products, arithmetic and copies ran while one was open for 6% of the time, Pallas kernels for 0%

commit v1 on v0

v1 whole, which is shorter than its diff:
```python
import math

import jax
import jax.numpy as jnp
from jax import lax
from jax.experimental import pallas as pl
from jax.experimental.pallas import tpu as pltpu
from jax.sharding import PartitionSpec as P

IN_DIM = 512
KERNEL = 5
GROUP_SIZE = 64
MARGIN = KERNEL // 2
TAPS = KERNEL * KERNEL
ONES_ROW = 32

clip_limit = 0.005
small_rate = 0.1
BF = jnp.bfloat16
F32 = jnp.float32
I32 = jnp.int32
EXACT = lax.Precision.HIGHEST


def spread(x, axes):
    n = lax.axis_size(axes)
    return lax.all_to_all(jnp.broadcast_to(x[None], (n,) + x.shape), axes, 0, 0)


def shape(dims, kind):
    return jax.ShapeDtypeStruct(dims, kind)


def whole(array):
    dims = array.shape
    return pl.BlockSpec(dims, lambda *unused: (0,) * len(dims))


def columns_kernel(place, first, second, third, fourth, out):
    odd = place[1] == 1
    lower = lax.broadcasted_iota(I32, first.shape, 1) < GROUP_SIZE

    def pair(left, right):
        x, y = left[...], right[...]
        low = jnp.where(odd, pltpu.roll(x, GROUP_SIZE, 1), x)
        high = jnp.where(odd, y, pltpu.roll(y, GROUP_SIZE, 1))
        return jnp.where(lower, low, high).astype(BF)

    out[:, : 2 * GROUP_SIZE] = pair(first, second)
    out[:, 2 * GROUP_SIZE :] = pair(third, fourth)


def own_kernel_columns(kernels, block):
    own, gate_dim = kernels.shape
    lanes = 2 * GROUP_SIZE
    per_quarter = gate_dim // 4 // lanes
    step = own // 5
    place = jnp.stack([block // 2, block % 2]).astype(I32)

    def spec(quarter):
        return pl.BlockSpec((step, lanes), lambda i, where: (i, quarter * per_quarter + where[0]))

    return pl.pallas_call(
        columns_kernel,
        out_shape=shape((own, 4 * GROUP_SIZE), BF),
        grid_spec=pltpu.PrefetchScalarGridSpec(
            num_scalar_prefetch=1,
            grid=(5,),
            in_specs=[spec(q) for q in range(4)],
            out_specs=pl.BlockSpec((step, 4 * GROUP_SIZE), lambda i, where: (i, 0)),
        ),
        name="columns",
    )(place, kernels, kernels, kernels, kernels)


def group_mean(values):
    n = values.shape[1]
    same = (
        lax.broadcasted_iota(I32, (n, n), 0) // GROUP_SIZE
        == lax.broadcasted_iota(I32, (n, n), 1) // GROUP_SIZE
    )
    mixer = jnp.where(same, 1.0 / GROUP_SIZE, 0.0).astype(F32)
    return jnp.dot(values, mixer, precision=EXACT, preferred_element_type=F32)


def fill_bands(bands, image, columns):
    pixels = image.shape[0]
    edge = MARGIN * columns
    column = lax.broadcasted_iota(I32, image.shape, 0) % columns
    blank = jnp.zeros((edge, image.shape[1]), BF)
    for d in range(KERNEL):
        move = d - MARGIN
        moved = image if move == 0 else pltpu.roll(image, (-move) % pixels, 0)
        inside = (column + move >= 0) & (column + move < columns)
        bands[d, edge : edge + pixels, :] = jnp.where(inside, moved, 0.0).astype(BF)
        bands[d, :edge, :] = blank
        bands[d, edge + pixels :, :] = blank


def cell_parts(gates, cells_prev, gain, shift):
    width = cells_prev.shape[1]
    centred = gates - group_mean(gates)
    inverse = lax.rsqrt(group_mean(centred * centred) + 1e-05)
    norm = centred * inverse
    normed = norm * gain + shift
    input_gate = jax.nn.sigmoid(normed[:, :width])
    forget_gate = jax.nn.sigmoid(normed[:, width : 2 * width])
    candidate = jnp.tanh(normed[:, 2 * width : 3 * width])
    output_gate = jax.nn.sigmoid(normed[:, 3 * width :])
    cells = forget_gate * cells_prev + input_gate * candidate
    return norm, inverse, input_gate, forget_gate, candidate, output_gate, cells


def forward_kernel(
    columns, first_row, obs, hid, ends, weight, cells_prev, norms, head,
    gates_out, cells_out, hidden_out, low_out, turned_out, seen_out, bands, total,
):
    step = pl.program_id(0)
    pixels = total.shape[0]

    @pl.when(step == 0)
    def start():
        lifted = (ends[0:1, :] * obs[...] + ends[1:2, :]).astype(BF).astype(F32)
        fill_bands(bands, jnp.concatenate([lifted, hid[...].astype(F32)], axis=1), columns)
        total[...] = jnp.zeros_like(total)

    begin = pl.multiple_of((first_row[0] + step) * columns, columns)
    part = total[...]
    for d in range(KERNEL):
        part = part + jnp.dot(
            bands[d, pl.ds(begin, pixels), :], weight[d], preferred_element_type=F32
        )
    total[...] = part

    @pl.when(step == KERNEL - 1)
    def finish():
        gates = total[...]
        parts = cell_parts(gates, cells_prev[...], norms[0:1, :], norms[1:2, :])
        output_gate, cells = parts[5], parts[6]
        hidden = output_gate * jnp.tanh(cells)
        gates_out[...] = gates
        cells_out[...] = cells
        hidden_out[...] = hidden
        low_out[...] = hidden.astype(BF)
        turned_out[...] = jnp.transpose(hidden).astype(BF)
        seen_out[...] = lax.dot_general(
            head[...], hidden, (((1,), (1,)), ((), ())), precision=EXACT,
            preferred_element_type=F32,
        )


def forward_frame(columns, rows, first_row, obs, hid, ends, weight, cells_prev, norms, head):
    pixels, width = cells_prev.shape
    image = hid.shape[0]
    gate = 4 * width
    outs = (
        shape((pixels, gate), F32),
        shape((pixels, width), F32),
        shape((pixels, width), F32),
        shape((pixels, width), BF),
        shape((width, pixels), BF),
        shape((8, pixels), F32),
    )

    def body(*refs):
        forward_kernel(columns, *refs)

    return pl.pallas_call(
        body,
        out_shape=outs,
        grid_spec=pltpu.PrefetchScalarGridSpec(
            num_scalar_prefetch=1,
            grid=(KERNEL,),
            in_specs=[
                whole(obs),
                whole(hid),
                whole(ends),
                pl.BlockSpec((KERNEL, IN_DIM, gate), lambda i, first: (i, 0, 0)),
                whole(cells_prev),
                whole(norms),
                whole(head),
            ],
            out_specs=[whole(o) for o in outs],
            scratch_shapes=[
                pltpu.VMEM((KERNEL, image + 2 * MARGIN * columns, IN_DIM), BF),
                pltpu.VMEM((pixels, gate), F32),
            ],
        ),
        name="forward_frame",
    )(first_row, obs, hid, ends, weight, cells_prev, norms, head)


def backward_kernel(last, *refs):
    (scalars, seen, target, valid, gates, cells_prev, norms, head, looks) = refs[:9]
    grad_next, pieces = (None, ()) if last else (refs[9], refs[10:-6])
    low_out, cells_grad, sums_out, echo_out, rows_out, head_out = refs[-6:]
    pixels, width = cells_prev.shape
    gain = norms[0:1, :]
    error = jnp.sum(seen[...], axis=0, keepdims=True) + scalars[0] - target[...]
    weighted = valid[...] * error
    grad_row = 2.0 * weighted / scalars[1]
    rows_out[0:1, :] = grad_row
    rows_out[1:2, :] = weighted * error
    rows_out[2:8, :] = jnp.zeros((6, pixels), F32)
    grad_pred = jnp.transpose(jnp.broadcast_to(grad_row, (2 * GROUP_SIZE, pixels)))[:, :width]

    norm, inverse, input_gate, forget_gate, candidate, output_gate, cells = cell_parts(
        gates[...], cells_prev[...], gain, norms[1:2, :]
    )
    squashed = jnp.tanh(cells)
    grad_hidden = grad_pred * head[0:1, :]
    for piece in pieces:
        grad_hidden = grad_hidden + piece[...]
    head_out[...] = jnp.broadcast_to(
        jnp.sum(grad_pred * (output_gate * squashed), axis=0, keepdims=True), head_out.shape
    )
    grad_cells = grad_hidden * output_gate * (1.0 - squashed * squashed)
    if not last:
        grad_cells = grad_cells + grad_next[...]
    cells_grad[...] = grad_cells * forget_gate
    grad_normed = jnp.concatenate(
        [
            grad_cells * candidate * input_gate * (1.0 - input_gate),
            grad_cells * cells_prev[...] * forget_gate * (1.0 - forget_gate),
            grad_cells * input_gate * (1.0 - candidate * candidate),
            grad_hidden * squashed * output_gate * (1.0 - output_gate),
        ],
        axis=1,
    )
    sums_out[0:1, :] = jnp.sum(grad_normed * norm, axis=0, keepdims=True)
    sums_out[1:2, :] = jnp.sum(grad_normed, axis=0, keepdims=True)
    sums_out[2:8, :] = jnp.zeros((6, 4 * width), F32)
    scaled = grad_normed * gain
    grad_gates = inverse * (scaled - group_mean(scaled) - norm * group_mean(scaled * norm))
    low = grad_gates.astype(BF)
    low_out[...] = low
    echo_out[...] = jnp.dot(
        looks[...], low.astype(F32), precision=EXACT, preferred_element_type=F32
    )


def backward_frame(scalars, seen, target, valid, gates, cells_prev, norms, head, looks, later):
    pixels, width = cells_prev.shape
    gate = 4 * width
    outs = (
        shape((pixels, gate), BF),
        shape((pixels, width), F32),
        shape((8, gate), F32),
        shape((looks.shape[0], gate), F32),
        shape((8, pixels), F32),
        shape((8, width), F32),
    )
    args = [seen, target, valid, gates, cells_prev, norms, head, looks] + list(later)
    last = not later

    def body(*refs):
        backward_kernel(last, *refs)

    return pl.pallas_call(
        body,
        out_shape=outs,
        in_specs=[pl.BlockSpec(memory_space=pltpu.SMEM)] + [whole(a) for a in args],
        out_specs=[whole(o) for o in outs],
        grid=(1,),
        name="backward_cell",
    )(scalars, *args)


def hidden_kernel(columns, me, above, low, below, weight, *refs):
    outs, (bands, total, held) = refs[:-3], refs[-3:]
    step = pl.program_id(0)
    pixels = low.shape[0]
    blocks, unused, width = held.shape

    @pl.when(step == 0)
    def start():
        fill_bands(bands, low[...].astype(F32), columns)
        edge = MARGIN * columns
        if above is not None:
            for side, place in ((above, 0), (below, edge + pixels)):
                image = side[...].astype(F32)
                column = lax.broadcasted_iota(I32, image.shape, 0) % columns
                for d in range(KERNEL):
                    move = d - MARGIN
                    moved = image if move == 0 else pltpu.roll(image, (-move) % edge, 0)
                    inside = (column + move >= 0) & (column + move < columns)
                    bands[d, place : place + edge, :] = jnp.where(inside, moved, 0.0).astype(BF)
        total[...] = jnp.zeros_like(total)

    begin = pl.multiple_of((KERNEL - 1 - step) * columns, columns)
    part = total[...]
    for d in range(KERNEL):
        part = part + lax.dot_general(
            bands[KERNEL - 1 - d, pl.ds(begin, pixels), :],
            weight[d, 0],
            (((1,), (1,)), ((), ())),
            preferred_element_type=F32,
        )
    total[...] = part

    @pl.when(step == KERNEL - 1)
    def finish():
        for b in range(blocks):
            held[jnp.bitwise_xor(b, me[0])] = total[:, b * width : (b + 1) * width]
        for k in range(blocks):
            outs[k][...] = held[k]


def hidden_gradient(columns, blocks, me, sides, low, weight):
    pixels, gate = low.shape
    hidden_dim = weight.shape[1] // 2
    halves = weight.reshape(TAPS, 2, hidden_dim, gate)
    width = hidden_dim // blocks
    outs = (shape((pixels, width), F32),) * blocks
    args = [low] if sides is None else [sides[0], low, sides[1]]

    def body(me_ref, *refs):
        if sides is None:
            hidden_kernel(columns, me_ref, None, refs[0], None, *refs[1:])
        else:
            hidden_kernel(columns, me_ref, *refs)

    return pl.pallas_call(
        body,
        out_shape=outs,
        grid_spec=pltpu.PrefetchScalarGridSpec(
            num_scalar_prefetch=1,
            grid=(KERNEL,),
            in_specs=[whole(a) for a in args]
            + [pl.BlockSpec((KERNEL, 1, hidden_dim, gate), lambda i, where: (i, 1, 0, 0))],
            out_specs=[whole(o) for o in outs],
            scratch_shapes=[
                pltpu.VMEM((KERNEL, pixels + 2 * MARGIN * columns, gate), BF),
                pltpu.VMEM((pixels, hidden_dim), F32),
                pltpu.VMEM((blocks, pixels, width), F32),
            ],
        ),
        name="hidden_gradient",
    )(me, *args, halves)


def patches_kernel(columns, slabs, tiles, places, obs, ends, *refs):
    hid, (out, moves, patches, held) = refs[:tiles], refs[tiles:]
    own, image = out.shape
    span = moves.shape[0]
    for k in range(tiles):
        held[k] = hid[k][0]

    @pl.when(pl.program_id(0) == 0)
    def start():
        source = lax.broadcasted_iota(I32, (image, image), 0)
        target = lax.broadcasted_iota(I32, (image, image), 1)
        for k in range(span):
            row_off, col_off = places[2 + 2 * k], places[3 + 2 * k]
            column = target % columns + col_off
            hit = source == target + row_off * columns + col_off
            hit = hit & (column >= 0) & (column < columns)
            moves[k] = jnp.where(hit, 1.0, 0.0).astype(BF)

    lifted = (ends[:, 0:1] * obs[0] + ends[:, 1:2]).astype(BF)
    blocks = tiles // slabs
    parts = [lifted]
    for b in range(blocks):
        piece = [held[jnp.bitwise_xor(s * blocks + b, places[1])] for s in range(slabs)]
        parts.append(piece[0] if slabs == 1 else jnp.concatenate(piece, axis=1))
    joined = jnp.concatenate(parts, axis=0)
    for k in range(span):
        patches[k * IN_DIM : (k + 1) * IN_DIM, :] = jnp.dot(
            joined, moves[k], preferred_element_type=F32
        ).astype(BF)
    skip = pl.multiple_of(places[0], 16)
    out[...] = patches[pl.ds(skip, own), :]


def owned_patches(columns, slabs, own, span, places, obs, hid, width, row, ends):
    owners, unused, image = obs.shape
    tiles, pixels = len(hid), hid[0].shape[2]

    def body(*refs):
        patches_kernel(columns, slabs, tiles, *refs)

    return pl.pallas_call(
        body,
        out_shape=shape((own, owners * image), BF),
        grid_spec=pltpu.PrefetchScalarGridSpec(
            num_scalar_prefetch=1,
            grid=(owners,),
            in_specs=[
                pl.BlockSpec((1, 1, image), lambda s, where: (s, 0, 0)),
                whole(ends),
            ]
            + [pl.BlockSpec((1, width, pixels), lambda s, where: (s, row, 0))] * tiles,
            out_specs=pl.BlockSpec((own, image), lambda s, where: (0, s)),
            scratch_shapes=[
                pltpu.VMEM((span, image, image), BF),
                pltpu.VMEM((span * IN_DIM, image), BF),
                pltpu.VMEM((tiles, width, pixels), BF),
            ],
        ),
        name="owned_patches",
    )(places, obs, ends, *hid)


def adamw(weight, moment, second, grad, rate, correction):
    moment_new = 0.5 * moment + 0.5 * grad
    second_new = 0.5 * second + 0.5 * grad * grad
    update = moment_new / correction / (jnp.sqrt(second_new / correction) + 1e-08)
    return (weight - rate * (update + 0.01 * weight), moment_new, second_new)


def adamw_kernel(blocks, rate, me, scalars, *refs):
    grads = refs[:blocks]
    weight, moment, second, weight_out, moment_out, second_out, held = refs[blocks:]
    for k in range(blocks):
        held[k] = grads[k][...]
    width = held.shape[2] // 4
    placed = [held[jnp.bitwise_xor(b, me[0])] for b in range(blocks)]
    for q in range(4):
        grad = jnp.concatenate([p[:, q * width : (q + 1) * width] for p in placed], axis=1)
        cols = slice(q * blocks * width, (q + 1) * blocks * width)
        weight_out[:, cols], moment_out[:, cols], second_out[:, cols] = adamw(
            weight[:, cols], moment[:, cols], second[:, cols], grad * scalars[0], rate, scalars[1]
        )


def kernel_update(me, scalars, grads, weight, moment, second, rate):
    own, gate_dim = weight.shape
    blocks = len(grads)
    step = own // 10
    gate = gate_dim // blocks
    wide = pl.BlockSpec((step, gate_dim), lambda i, where: (i, 0))
    thin = pl.BlockSpec((step, gate), lambda i, where: (i, 0))

    def body(*refs):
        adamw_kernel(blocks, rate, *refs)

    return pl.pallas_call(
        body,
        out_shape=(shape((own, gate_dim), F32),) * 3,
        grid_spec=pltpu.PrefetchScalarGridSpec(
            num_scalar_prefetch=1,
            grid=(10,),
            in_specs=[pl.BlockSpec(memory_space=pltpu.SMEM)] + [thin] * blocks + [wide] * 3,
            out_specs=[wide] * 3,
            scratch_shapes=[pltpu.VMEM((blocks, step, gate), F32)],
        ),
        name="kernel_update",
    )(me, scalars, *grads, weight, moment, second)


def split_low(values):
    high = values.astype(BF)
    return high, (values - high.astype(F32)).astype(BF)


def per_device(
    observed,
    targets,
    pixel_mask,
    lengths,
    step_count,
    kernels,
    kernel_moment,
    kernel_second,
    norm_params,
    norm_moment,
    norm_second,
    end_params,
    end_moment,
    end_second,
    head_bias,
    head_moment,
    head_second,
    hidden_init,
    cells_init,
):
    tiles, owners = lax.axis_size("tile"), lax.axis_size("dp")
    streams, frames, tile_rows, columns = observed.shape
    height = tile_rows * tiles
    hidden_dim = end_params.shape[1]
    gate_dim = 4 * hidden_dim
    blocks = math.gcd(tiles, hidden_dim // GROUP_SIZE)
    slabs = tiles // blocks
    rows = height // slabs
    width = hidden_dim // blocks
    gate = 4 * width
    pixels, image = rows * columns, height * columns
    own = kernels.shape[1]
    assert streams == 1 and width == GROUP_SIZE and own % 80 == 0 and pixels == gate
    tile = lax.axis_index("tile")
    owner = lax.axis_index("dp")
    block, slab = tile % blocks, tile // blocks
    first_row = slab * rows
    groups = None
    if slabs > 1:
        groups = [[s * blocks + b for b in range(blocks)] for s in range(slabs)]

    weight = lax.all_gather(own_kernel_columns(kernels[0], block), "dp", axis=0, tiled=True)
    weight = weight.reshape(TAPS, IN_DIM, gate)

    frame_ids = lax.broadcasted_iota(I32, (1, frames), 1)
    counted = (frame_ids < lengths[:, None]).astype(F32)
    valid = pixel_mask.astype(F32) * counted[:, :, None, None]
    small = spread(jnp.stack([observed[0], targets[0], valid[0]]), ("dp", "tile"))
    small = small.reshape(owners, tiles, 3, frames, tile_rows * columns)
    small = small.transpose(2, 3, 0, 1, 4).reshape(3, frames, owners, image)
    count = jnp.maximum(jnp.sum(small[2]), 1.0)
    obs_all = small[0]
    mine = lax.dynamic_slice_in_dim(small, owner, 1, 2)
    mine_rows = lax.dynamic_slice_in_dim(mine, first_row * columns, pixels, 3)

    def own_columns(values):
        shaped = values.reshape(values.shape[:-1] + (4, hidden_dim))
        part = lax.dynamic_slice_in_dim(shaped, block * width, width, values.ndim)
        return part.reshape(values.shape[:-1] + (gate,))

    norms = own_columns(norm_params[:, 0])
    head = lax.dynamic_slice_in_dim(end_params[2], block * width, width, 0)
    head = jnp.broadcast_to(head[None], (8, width))
    ends = end_params[:2]
    ends_turned = ends.T

    me = jnp.reshape(block if slabs == 1 else jnp.zeros_like(block), (1,)).astype(I32)

    def all_tiles(values):
        if slabs > 1:
            got = lax.all_gather(values, "tile")
            return [got[k] for k in range(tiles)]
        held, order, stride = [values], [0], tiles // 2
        while stride:
            pairs = [(j, j ^ stride) for j in range(tiles)]
            held = held + [lax.ppermute(h, "tile", pairs) for h in held]
            order = order + [k ^ stride for k in order]
            stride //= 2
        return [held[order.index(k)] for k in range(tiles)]

    span = max((own * (i + 1) - 1) // IN_DIM - own * i // IN_DIM + 1 for i in range(owners))
    first_tap = jnp.minimum(owner * own // IN_DIM, TAPS - span)
    places = [owner * own - first_tap * IN_DIM, me[0]]
    for k in range(span):
        places += [(first_tap + k) // KERNEL - MARGIN, (first_tap + k) % KERNEL - MARGIN]
    places = jnp.stack(places).astype(I32)

    def patches_of(frame_no, hid, row):
        obs_rows = obs_all[frame_no].reshape(owners, 1, image)
        return owned_patches(
            columns, slabs, own, span, places, obs_rows, hid, width, row, ends_turned
        )

    states = jnp.stack([hidden_init[0, 0], cells_init[0, 0]])
    states = states.reshape(2, tile_rows * columns, blocks, width).transpose(2, 0, 1, 3)
    states = lax.all_to_all(states, "tile", 0, 0, axis_index_groups=groups)
    states = states.transpose(1, 0, 2, 3).reshape(2, pixels, width)
    low = states[0].astype(BF)
    cells = states[1]
    patches = [None] * frames
    patches[0] = patches_of(0, all_tiles(spread(low.T, "dp")), 0)

    def whole_hidden(values):
        got = lax.all_gather(values, "tile").reshape(slabs, blocks, pixels, width)
        return got.transpose(0, 2, 1, 3).reshape(image, hidden_dim)

    weight, patches[0] = lax.optimization_barrier((weight, patches[0]))
    first = jnp.reshape(first_row, (1,)).astype(I32)
    kept, turns, seen, turned = [], [], [], None
    for frame_no in range(frames):
        obs_column = mine[0, frame_no].reshape(image, 1)
        turns.append(turned)
        gates, cells_next, hidden, low_next, turned, seen_part = forward_frame(
            columns, rows, first, obs_column, whole_hidden(low), ends, weight, cells, norms, head
        )
        kept.append((gates, cells))
        cells, low = cells_next, low_next
        seen.append(seen_part[0])
    seen = lax.all_gather(jnp.stack(seen), "tile", axis_index_groups=groups)
    scalars = jnp.stack([head_bias[0], count])

    padded = jnp.pad(
        jnp.stack([mine[0, :, 0], jnp.ones_like(mine[0, :, 0])], axis=1).reshape(
            frames, 2, height, columns
        ),
        ((0, 0), (0, 0), (MARGIN, MARGIN), (MARGIN, MARGIN)),
    )
    padded = lax.dynamic_slice_in_dim(padded, first_row, rows + 2 * MARGIN, 2)
    looks = jnp.stack(
        [
            padded[:, :, a : a + rows, b : b + columns].reshape(frames, 2, pixels)
            for a in range(KERNEL)
            for b in range(KERNEL)
        ],
        axis=2,
    )
    looks = jnp.pad(looks, ((0, 0), (0, 0), (0, ONES_ROW - TAPS), (0, 0)))
    looks = looks.reshape(frames, 2 * ONES_ROW, pixels)

    sums = jnp.zeros((8, gate), F32)
    echo = jnp.zeros((2 * ONES_ROW, gate), F32)
    rows_sum = jnp.zeros((8, pixels), F32)
    head_sum = jnp.zeros((8, width), F32)
    later = ()
    parcels = [None] * frames
    for frame_no in reversed(range(frames)):
        gates, cells_prev = kept[frame_no]
        low, grad_cells, sums_part, echo_part, rows_part, head_part = backward_frame(
            scalars,
            seen[:, frame_no],
            mine_rows[1, frame_no],
            mine_rows[2, frame_no],
            gates,
            cells_prev,
            norms,
            head,
            looks[frame_no],
            later,
        )
        parcel = low if frame_no == 0 else jnp.concatenate([low, turns[frame_no]], axis=0)
        parcels[frame_no] = spread(parcel, "dp")
        sums, echo = sums + sums_part, echo + echo_part
        rows_sum, head_sum = rows_sum + rows_part, head_sum + head_part
        if frame_no > 0:
            sides = None
            if slabs > 1:
                edge = MARGIN * columns
                up = [(s, s - blocks) for s in range(blocks, tiles)]
                down = [(s - blocks, s) for s in range(blocks, tiles)]
                below = lax.ppermute(low[:edge], "tile", up)
                above = lax.ppermute(low[pixels - edge :], "tile", down)
                sides = (above, below)
            pieces = list(
                hidden_gradient(
                    columns, blocks, jnp.reshape(block, (1,)).astype(I32), sides, low, weight
                )
            )
            for k in range(1, blocks):
                pairs = [(j, j ^ k) for j in range(tiles)]
                pieces[k] = lax.ppermute(pieces[k], "tile", pairs)
            later = [grad_cells] + pieces

    hidden, cells, parcels[0] = lax.optimization_barrier((hidden, cells, parcels[0]))
    final = jnp.stack([hidden, cells]).reshape(2, blocks, tile_rows * columns, width)
    final = lax.all_to_all(final.transpose(1, 0, 2, 3), "tile", 0, 0, axis_index_groups=groups)
    final = final.transpose(1, 2, 0, 3).reshape(2, 1, 1, tile_rows, columns, hidden_dim)

    pieces = [None] * frames
    for frame_no in reversed(range(frames)):
        got = all_tiles(parcels[frame_no])
        if frame_no > 0:
            patches[frame_no] = patches_of(frame_no, got, pixels // width)
        pieces[frame_no] = [g[:, :pixels] for g in got]

    def block_gradient(k):
        grad = None
        for frame_no in reversed(range(frames)):
            if slabs == 1:
                piece = pieces[frame_no][k]
            else:
                piece = [pieces[frame_no][s * blocks + k] for s in range(slabs)]
                piece = jnp.stack(piece, axis=1)
            part = jnp.dot(
                patches[frame_no], piece.reshape(owners * image, gate), preferred_element_type=F32
            )
            grad = part if grad is None else grad + part
        return grad

    grads = [block_gradient(k) for k in range(blocks)]
    own_grad = grads[0]
    if slabs > 1:
        for b in range(1, blocks):
            own_grad = jnp.where(block == b, grads[b], own_grad)
    square = jnp.sum(own_grad * own_grad) * (slab == 0).astype(F32)

    lift_kernel = weight[:, :hidden_dim]
    echoes = echo.reshape(2, ONES_ROW, gate)[:, :TAPS]
    lift_grads = sum(
        jnp.einsum("ktg,tcg->kc", part, lift_kernel, preferred_element_type=F32)
        for part in split_low(echoes)
    )

    once = (block == 0).astype(F32)
    norm_part = jnp.zeros((2, 4, hidden_dim), F32)
    norm_part = lax.dynamic_update_slice_in_dim(
        norm_part, sums[:2].reshape(2, 4, width), block * width, 2
    )
    head_part = lax.dynamic_update_slice_in_dim(
        jnp.zeros((hidden_dim,), F32), head_sum[0], block * width, 0
    )
    packed = jnp.concatenate(
        [
            norm_part.reshape(-1),
            lift_grads.reshape(-1),
            head_part,
            jnp.sum(rows_sum[:2], axis=1) * once,
            jnp.reshape(square, (1,)),
        ]
    )
    total = jnp.sum(spread(packed, ("dp", "tile")), axis=0)
    grad_norms = total[: 2 * gate_dim].reshape(2, 1, gate_dim)
    grad_ends = total[2 * gate_dim : 2 * gate_dim + 3 * hidden_dim].reshape(3, hidden_dim)
    grad_head = total[-3:-2]
    loss_sum = total[-2]
    kernel_square = total[-1]

    squares = (
        kernel_square
        + jnp.sum(grad_norms * grad_norms)
        + jnp.sum(grad_ends * grad_ends)
        + jnp.sum(grad_head * grad_head)
    )
    grad_norm = jnp.sqrt(squares)
    factor = clip_limit / jnp.maximum(grad_norm, clip_limit)
    correction = 1.0 - jnp.power(0.5, step_count[0].astype(F32))
    kernel_rate = (TAPS * IN_DIM) ** (-0.5)
    kern_out = kernel_update(
        me,
        jnp.stack([factor, correction]),
        grads,
        kernels[0],
        kernel_moment[0],
        kernel_second[0],
        kernel_rate,
    )
    norm_out = adamw(
        norm_params, norm_moment, norm_second, grad_norms * factor, small_rate, correction
    )
    end_out = adamw(end_params, end_moment, end_second, grad_ends * factor, small_rate, correction)
    head_out = adamw(
        head_bias, head_moment, head_second, grad_head * factor, small_rate, correction
    )
    return (
        (loss_sum / count, grad_norm)
        + tuple(k[None] for k in kern_out)
        + norm_out
        + end_out
        + head_out
        + (final[0], final[1])
    )


def solution(mesh):
    rows = P("dp", None, "tile", None)
    kern = P(None, "dp", None)
    state = P(None, "dp", "tile", None, None)
    placed = (rows, rows, rows, P("dp"), P(), kern, kern, kern) + (P(),) * 9 + (state, state)
    outs = (P(), P(), kern, kern, kern) + (P(),) * 9 + (state, state)
    return jax.shard_map(
        per_device, mesh=mesh, in_specs=placed, out_specs=outs, check_vma=False
    )
```

time: 1690 us -> 372 us (0.22)
  waiting for transfers between devices: 1270 us -> 119 us
  blocking collectives: 149 us -> 16.6 us
  Pallas kernels: 0 us -> 73.2 us
  matrix products: 100 us -> 45.7 us
  local copies, waits for them, and re-layouts: 76.5 us -> 34.4 us
  other arithmetic: 41.9 us -> 11.4 us
  starting transfers between devices: 19.7 us -> 38.6 us
    reduce_scatter x1 -> x0, waiting for transfers between devices: 794 us -> none  [per_device(): lax.psum_scatter(grad_kernels, 'dp', scatter_dimension=1, tiled=True)]
    all_gather x1, waiting for transfers between devices: 408 us -> 37.7 us  [per_device(): lax.all_gather(own_kernel_columns(kernels[0], block), 'dp', axis=0, tiled...]
    psum x3 -> x0, blocking collectives: 149 us -> none  [the longest x1 85.6 us: per_device(): count = jnp.maximum(lax.psum(jnp.sum(valid), ('tile', 'dp')), 1.0)]
    pallas_call x0 -> x9, Pallas kernels: none -> 73.2 us  [the longest x1 19.5 us: kernel_update(): pl.pallas_call(body, out_shape=(shape((own, gate_dim), F32),) * 3, grid_s...]
    all_to_all x0 -> x7, waiting for transfers between devices: none -> 72.5 us  [the longest x5 44.9 us: spread(): return lax.all_to_all(jnp.broadcast_to(x[None], (n,) + x.shape), axes, 0, 0)]
    psum x1 -> x0, waiting for transfers between devices: 66.4 us -> none  [per_device(): shard = lax.psum(shard, 'tile')]
    dot_general x6 -> x10, matrix products: 100 us -> 45.7 us  [the longest x8 39.9 us: block_gradient(): jnp.dot(patches[frame_no], piece.reshape(owners * image, gate), preferred...]
    transpose x2 -> x1, local copies, waits for them, and re-layouts: 52.3 us -> 0.02 us  [per_device(): states.reshape(2, tile_rows * columns, blocks, width).transpose(2, 0, 1, 3)]
  transfers between devices with their start and end apart: 11 -> 20, of which waited for: 3 -> 10; matrix products, arithmetic and copies ran while one was open for 6% -> 19% of each run, Pallas kernels for 0% -> 5%
where the time goes in v1:
time: 372 us; the launch traced here: 369 us
  waiting for transfers between devices  119 us (32%)
  Pallas kernels  73.2 us (20%)
  matrix products  45.7 us (12%)
  starting transfers between devices  38.6 us (10%)
  local copies, waits for them, and re-layouts  34.4 us (9%)
  between operations  29.9 us (8%)
  blocking collectives  16.6 us (4%)
  other arithmetic  11.4 us (3%)
    all_to_all x5, waiting for transfers between devices, spread(): return lax.all_to_all(jnp.broadcast_to(x[None], (n,) + x.shape), axes, 0, 0)  44.9 us
    dot_general x8, matrix products, block_gradient(): jnp.dot(patches[frame_no], piece.reshape(owners * image, gate), preferred...  39.9 us
    all_gather x1, waiting for transfers between devices, per_device(): lax.all_gather(own_kernel_columns(kernels[0], block), 'dp', axis=0, tiled...  37.7 us
    all_to_all x1, waiting for transfers between devices, per_device(): lax.all_to_all(final.transpose(1, 0, 2, 3), 'tile', 0, 0, axis_index_grou...  27.2 us
    all_to_all x5, starting transfers between devices, spread(): return lax.all_to_all(jnp.broadcast_to(x[None], (n,) + x.shape), axes, 0, 0)  24.8 us
    pallas_call x1, Pallas kernels, kernel_update(): pl.pallas_call(body, out_shape=(shape((own, gate_dim), F32),) * 3, grid_s...  19.5 us
    pallas_call x2, Pallas kernels, owned_patches(): pl.pallas_call(body, out_shape=shape((own, owners * image), BF), grid_spe...  18 us
    pallas_call x2, Pallas kernels, forward_frame(): pl.pallas_call(body, out_shape=outs, grid_spec=pltpu.PrefetchScalarGridSp...  16.3 us
  transfers between devices with their start and end apart: 20, of which 10 were waited for; matrix products, arithmetic and copies ran while one was open for 19% of the time, Pallas kernels for 5%

profile of v1, /device:TPU:0, one launch (start us, length us, event | category | flops | bytes accessed | tf_op | source)
XLA Modules:
  0.0 368.6 jit_solution(8035048391440834282)
XLA Ops:
  7.9 5.6 %columns.1 = bf16[1600,256]{1,0:T(8,128)(2,1)} custom-call(s32[2]{0:T(128)} %pad_add_fusion.place, f32[1600,1024]{1,0:T(8,128)} %bitcast.181, f32[1600,1024]{1,0:T(8,128)} %bitcast.182, f32[1600,1024]{1,0:T(8,128)} %bitcast.183, f32[1600,1024]{1,0:T(8,128)} %bitcast.184), custom_call_target="tpu_custom_call" | custom-call | tf_op jit(solution)/shard_map/columns/pallas_call | solution.py:63
  15.2 7.3 %all-to-all-start = ((f32[32,1,384]{2,1,0:T(1,128)}), f32[32,1,384]{2,1,0:T(1,128)S(1)}, u32[]{:S(2)}, u32[]{:S(2)}) async-start(f32[32,1,384]{2,1,0:T(1,128)} %reshape.250), calls=%async_computation | async-start | bytes 98304 | tf_op jit(solution)/shard_map/all_to_all | solution.py:27
  26.9 3.0 all-to-all-done
  29.9 3.3 all-to-all-start.1
  39.8 3.4 all-to-all-start.2
  44.5 15.4 %all-to-all-done.2.refs_3_ = bf16[8,64,256]{2,1,0:T(8,128)(2,1)S(1)} async-done(((bf16[8,64,256]{2,1,0:T(8,128)(2,1)}), bf16[8,64,256]{2,1,0:T(8,128)(2,1)S(1)}, u32[]{:S(2)}, u32[]{:S(2)}) %all-to-all-start.2) | async-done | bytes 262176 | tf_op jit(solution)/shard_map/all_to_all | solution.py:27
  59.9 1.5 collective-permute-start.1
  64.6 3.5 collective-permute-done.1.refs_5_
  70.2 5.4 %all_gather.19 = bf16[4,256,64]{1,2,0:T(8,128)(2,1)S(1)} all-gather(bf16[1,256,64]{1,2,0:T(8,128)(2,1)S(1)} %copy.125), channel_id=1, replica_groups=mesh['tile'=4,'dp'=8] {'tile'}, dimensions={0}, use_global_device_ids=true | all-gather | bytes 163840 | tf_op jit(solution)/shard_map/all_gather | solution.py:560
  77.2 9.0 %owned_patches.2 = bf16[1600,2048]{1,0:T(8,128)(2,1)} custom-call(s32[10]{0:T(128)} %stack.98.refs_0_, f32[8,1,256]{2,1,0:T(1,128)} %reshape_squeeze.16.refs_1_, f32[256,2]{1,0:T(8,128)} %bitcast.197, bf16[8,64,256]{2,1,0:T(8,128)(2,1)} %copy-done.2, bf16[8,64,256]{2,1,0:T(8,128)(2,1)} %copy-done.6, bf16[8,64,256]{2,1,0:T(8,128)(2,1)} %copy-done.5, ...), custom_call_target="tpu_custom_call" | custom-call | tf_op jit(solution)/shard_map/owned_patches/pallas_call | solution.py:382
  86.1 37.7 %all-gather.5.cloned.1.call-done = bf16[12800,256]{1,0:T(8,128)(2,1)} async-done(((bf16[1600,256]{1,0:T(8,128)(2,1)}), bf16[12800,256]{1,0:T(8,128)(2,1)}) %all-gather.5.cloned.1.call-update) | async-done | bytes 6553616 | tf_op jit(solution)/shard_map/all_gather | solution.py:498
  124.4 8.2 %forward_frame.2 = (f32[256,256]{1,0:T(8,128)}, f32[256,64]{1,0:T(8,128)}, f32[256,64]{1,0:T(8,128)}, bf16[256,64]{1,0:T(8,128)(2,1)}, bf16[64,256]{1,0:T(8,128)(2,1)}, /*index=5*/f32[8,256]{1,0:T(8,128)}) custom-call(s32[1]{0:T(128)} %bitcast.3.refs_0_, f32[256,1]{1,0:T(8,128)} %copy.128.refs_1_, bf16[256,256]{1,0:T(8,128)(2,1)} %copy.129.refs_2_, ...), custom_call_target="tpu_custom_call" | custom-call | tf_op jit(solution)/shard_map/forward_frame/pallas_call | solution.py:168
  132.6 6.0 %all-gather = bf16[1024,64]{1,0:T(8,128)(2,1)S(1)} all-gather(bf16[256,64]{1,0:T(8,128)(2,1)} %get-tuple-element.50), channel_id=2, replica_groups=mesh['tile'=4,'dp'=8] {'tile'}, dimensions={0}, use_global_device_ids=true | all-gather | bytes 163840 | tf_op jit(solution)/shard_map/all_gather | solution.py:560
  139.5 8.2 %forward_frame.3 = (f32[256,256]{1,0:T(8,128)}, f32[256,64]{1,0:T(8,128)}, f32[256,64]{1,0:T(8,128)}, bf16[256,64]{1,0:T(8,128)(2,1)}, bf16[64,256]{1,0:T(8,128)(2,1)}, /*index=5*/f32[8,256]{1,0:T(8,128)}) custom-call(s32[1]{0:T(128)} %bitcast.3.refs_0_, f32[256,1]{1,0:T(8,128)} %copy.132.refs_1_, bf16[256,256]{1,0:T(8,128)(2,1)} %copy.133.refs_2_, ...), custom_call_target="tpu_custom_call" | custom-call | tf_op jit(solution)/shard_map/forward_frame/pallas_call | solution.py:168
  149.1 5.2 %all-gather.2 = f32[4,2,256]{2,1,0:T(2,128)S(1)} all-gather(f32[1,2,256]{2,1,0:T(2,128)S(1)} %maximum_bitcast_fusion.2), channel_id=3, replica_groups=mesh['tile'=4,'dp'=8] {'tile'}, dimensions={0}, use_global_device_ids=true | all-gather | bytes 10240 | tf_op jit(solution)/shard_map/all_gather | solution.py:575
  154.9 3.9 %backward_cell.2 = (bf16[256,256]{1,0:T(8,128)(2,1)}, f32[256,64]{1,0:T(8,128)}, f32[8,256]{1,0:T(8,128)}, f32[64,256]{1,0:T(8,128)}, f32[8,256]{1,0:T(8,128)}, /*index=5*/f32[8,64]{1,0:T(8,128)}) custom-call(f32[2]{0:T(128)} %pad_maximum_fusion.2.refs_0_, f32[4,256]{1,0:T(4,128)} %bitcast.227, f32[1,256]{1,0:T(1,128)} %get-tuple-element.94.refs_2_, ...), custom_call_target="tpu_custom_call" | custom-call | tf_op jit(solution)/shard_map/backward_cell/pallas_call | solution.py:259
  159.7 1.1 broadcast_in_dim.30
  160.9 3.9 %all-to-all-start.3 = ((bf16[8,320,256]{2,1,0:T(8,128)(2,1)}), bf16[8,320,256]{2,1,0:T(8,128)(2,1)S(1)}, u32[]{:S(2)}, u32[]{:S(2)}) async-start(bf16[8,320,256]{2,1,0:T(8,128)(2,1)} %broadcast_in_dim.30), calls=%async_computation.3 | async-start | bytes 2621440 | tf_op jit(solution)/shard_map/all_to_all | solution.py:27
  164.7 5.6 %hidden_gradient.1 = (f32[256,64]{1,0:T(8,128)}, f32[256,64]{1,0:T(8,128)}, f32[256,64]{1,0:T(8,128)}, f32[256,64]{1,0:T(8,128)}) custom-call(s32[1]{0:T(128)} %bitcast.16.me_ref.refs_0_, bf16[256,256]{1,0:T(8,128)(2,1)} %get-tuple-element.57.refs_0_, bf16[25,2,256,256]{3,2,1,0:T(8,128)(2,1)} %bitcast.188), custom_call_target="tpu_custom_call" | custom-call | tf_op jit(solution)/shard_map/hidden_gradient/pallas_call | solution.py:323
  170.7 1.5 collective-permute-start.4
  173.5 3.8 %collective-permute-done.4.refs_12_ = f32[256,64]{1,0:T(8,128)S(1)} collective-permute-done((f32[256,64]{1,0:T(8,128)}, f32[256,64]{1,0:T(8,128)S(1)}, u32[]{:S(2)}, u32[]{:S(2)}) %collective-permute-start.4) | collective-permute-done | bytes 65568 | tf_op jit(solution)/shard_map/ppermute | solution.py:636
  177.3 1.2 collective-permute-done.5.refs_13_
  179.2 4.2 %backward_cell.3 = (bf16[256,256]{1,0:T(8,128)(2,1)}, f32[256,64]{1,0:T(8,128)}, f32[8,256]{1,0:T(8,128)}, f32[64,256]{1,0:T(8,128)}, f32[8,256]{1,0:T(8,128)}, /*index=5*/f32[8,64]{1,0:T(8,128)}) custom-call(f32[2]{0:T(128)} %pad_maximum_fusion.2.refs_0_, f32[4,256]{1,0:T(4,128)} %bitcast.226, f32[1,256]{1,0:T(1,128)} %get-tuple-element.93.refs_2_, ...), custom_call_target="tpu_custom_call" | custom-call | tf_op jit(solution)/shard_map/backward_cell/pallas_call | solution.py:259
  183.3 13.3 %all-to-all-done.3.refs_3_ = bf16[8,320,256]{2,1,0:T(8,128)(2,1)S(1)} async-done(((bf16[8,320,256]{2,1,0:T(8,128)(2,1)}), bf16[8,320,256]{2,1,0:T(8,128)(2,1)S(1)}, u32[]{:S(2)}, u32[]{:S(2)}) %all-to-all-start.3) | async-done | bytes 1310752 | tf_op jit(solution)/shard_map/all_to_all | solution.py:27
  196.7 2.1 broadcast_in_dim.62
  198.7 4.3 %all-to-all-start.4 = ((bf16[8,256,256]{2,1,0:T(8,128)(2,1)}), bf16[8,256,256]{2,1,0:T(8,128)(2,1)}, u32[]{:S(2)}, u32[]{:S(2)}) async-start(bf16[8,256,256]{2,1,0:T(8,128)(2,1)} %broadcast_in_dim.62), calls=%async_computation.4 | async-start | bytes 2097152 | tf_op jit(solution)/shard_map/all_to_all | solution.py:27
  208.1 2.9 fusion.7
  210.9 2.9 fusion.13
  213.8 1.5 collective-permute-start.7
  215.5 13.2 %all-to-all-done.4 = bf16[8,256,256]{2,1,0:T(8,128)(2,1)} async-done(((bf16[8,256,256]{2,1,0:T(8,128)(2,1)}), bf16[8,256,256]{2,1,0:T(8,128)(2,1)}, u32[]{:S(2)}, u32[]{:S(2)}) %all-to-all-start.4) | async-done | bytes 1048608 | tf_op jit(solution)/shard_map/all_to_all | solution.py:27
  228.7 1.5 collective-permute-start.10
  231.3 3.3 all-to-all-start.6
  234.6 6.1 %fusion.33 = f32[1600,256]{1,0:T(8,128)} fusion(bf16[1600,2048]{1,0:T(8,128)(2,1)} %owned_patches.2, bf16[2048,256]{1,0:T(8,128)(2,1)} %bitcast.51), kind=kOutput, calls=%fused_computation.119 | convolution fusion | flops 1677721600 | bytes 9240576 | tf_op jit(solution)/shard_map/dot_general | solution.py:659
  240.7 27.2 %all-to-all-done.6 = f32[4,1,8192]{2,1,0:T(1,128)S(1)} async-done(((f32[4,1,8192]{2,1,0:T(1,128)}), f32[4,1,8192]{2,1,0:T(1,128)S(1)}, u32[]{:S(2)}, u32[]{:S(2)}) %all-to-all-start.6) | async-done | bytes 131104 | tf_op jit(solution)/shard_map/all_to_all | solution.py:641
  270.9 1.1 slice.266
  272.6 6.6 %fusion.34 = f32[1600,256]{1,0:T(8,128)} fusion(bf16[1600,2048]{1,0:T(8,128)(2,1)} %owned_patches.2, bf16[2048,256]{1,0:T(8,128)(2,1)} %bitcast.58), kind=kOutput, calls=%fused_computation.120 | convolution fusion | flops 1677721600 | bytes 9240576 | tf_op jit(solution)/shard_map/dot_general | solution.py:659
  279.2 4.4 %fusion.35 = f32[1600,256]{1,0:T(8,128)} fusion(bf16[1600,2048]{1,0:T(8,128)(2,1)S(1)} %bitcast.194, bf16[2048,256]{1,0:T(8,128)(2,1)} %bitcast.60), kind=kOutput, calls=%fused_computation.121 | convolution fusion | flops 1677721600 | bytes 9240576 | tf_op jit(solution)/shard_map/dot_general | solution.py:659
  283.6 1.1 slice.273
  284.6 2.3 slice.272
  287.0 3.1 fusion.36
  290.1 9.0 %owned_patches.3 = bf16[1600,2048]{1,0:T(8,128)(2,1)} custom-call(s32[10]{0:T(128)} %stack.98.refs_0_, f32[8,1,256]{2,1,0:T(1,128)} %reshape_squeeze.19.refs_1_, f32[256,2]{1,0:T(8,128)} %bitcast.198, bf16[8,320,256]{2,1,0:T(8,128)(2,1)} %copy-done, bf16[8,320,256]{2,1,0:T(8,128)(2,1)} %collective-permute-done.6.refs_4_, bf16[8,320,256]{2,1,0:T(8,128)(2,1)} %copy-done.1, ...), custom_call_target="tpu_custom_call" | custom-call | tf_op jit(solution)/shard_map/owned_patches/pallas_call | solution.py:382
  299.1 6.5 %multiply_reduce_fusion = (f32[]{:T(128)}, f32[1600,256]{1,0:T(8,128)}) fusion(f32[1600,256]{1,0:T(8,128)S(1)} %copy-done.28, bf16[1600,2048]{1,0:T(8,128)(2,1)} %owned_patches.3, bf16[2048,256]{1,0:T(8,128)(2,1)S(1)} %bitcast.202), kind=kOutput, calls=%fused_computation.8 | convolution fusion | flops 1678950400 | bytes 10878980 | tf_op jit(solution)/shard_map/dot_general | solution.py:659
  307.3 5.9 %all-to-all-start.5 = ((f32[32,1,2819]{2,1,0:T(1,128)}), f32[32,1,2819]{2,1,0:T(1,128)S(1)}, u32[]{:S(2)}, u32[]{:S(2)}) async-start(f32[32,1,2819]{2,1,0:T(1,128)} %broadcast_in_dim.63), calls=%async_computation.5 | async-start | bytes 753664 | tf_op jit(solution)/shard_map/all_to_all | solution.py:27
  313.3 6.8 %convolution_add_fusion.2.refs_3_ = f32[1600,256]{1,0:T(8,128)} fusion(f32[1600,256]{1,0:T(8,128)} %fusion.34, bf16[1600,2048]{1,0:T(8,128)(2,1)} %owned_patches.3, bf16[2048,256]{1,0:T(8,128)(2,1)} %bitcast.204), kind=kOutput, calls=%fused_computation.6 | convolution fusion | flops 1678131200 | bytes 10878976 | tf_op jit(solution)/shard_map/dot_general | solution.py:659
  320.1 3.2 convolution_add_fusion.1.refs_4_
  323.3 1.3 slice.274
  324.7 3.1 convolution_add_fusion.refs_5_
  336.6 19.5 %kernel_update.1 = (f32[1600,1024]{1,0:T(8,128)}, f32[1600,1024]{1,0:T(8,128)}, f32[1600,1024]{1,0:T(8,128)}) custom-call(s32[1]{0:T(128)} %bitcast.16.me_ref.refs_0_, f32[2]{0:T(128)} %pad_maximum_fusion.3.refs_1_, f32[1600,256]{1,0:T(8,128)} %get-tuple-element.128.refs_2_, f32[1600,256]{1,0:T(8,128)} %convolution_add_fusion.2.refs_3_, ...), custom_call_target="tpu_custom_call" | custom-call | tf_op jit(solution)/shard_map/kernel_update/pallas_call | solution.py:437
  (234 shorter events, 38.5 us)
Async XLA Ops:
  7.2 116.7 %all-gather.5.cloned.1.call-start = ((), (), s32[]{:S(2)}) async-start(), calls=%async_computation.7 | async-start | bytes 7372800 | tf_op jit(solution)/shard_map/all_gather | solution.py:498
  7.9 6.4 %copy-start.26 = (f32[1,2,2,32]{3,2,1,0:T(2,128)S(1)}, f32[1,2,2,32]{3,2,1,0:T(2,128)}, u32[]{:S(2)}) copy-start(f32[1,2,2,32]{3,2,1,0:T(2,128)} %param.20) | copy-start | bytes 1540
  7.9 6.4 %copy-start.27 = (f32[1,2,2,32]{3,2,1,0:T(2,128)S(1)}, f32[1,2,2,32]{3,2,1,0:T(2,128)}, u32[]{:S(2)}) copy-start(f32[1,2,2,32]{3,2,1,0:T(2,128)} %param.19) | copy-start | bytes 1540
  7.9 14.8 %copy-start.19 = (f32[3,256]{1,0:T(4,128)S(1)}, f32[3,256]{1,0:T(4,128)}, u32[]{:S(2)}) copy-start(f32[3,256]{1,0:T(4,128)} %param.30) | copy-start | bytes 9220
  7.9 15.5 %copy-start.13 = (f32[1,1,2,32,256]{4,3,2,1,0:T(8,128)S(1)}, f32[1,1,2,32,256]{4,3,2,1,0:T(8,128)}, u32[]{:S(2)}) copy-start(f32[1,1,2,32,256]{4,3,2,1,0:T(8,128)} %param.37) | copy-start | bytes 196612
  7.9 15.6 %copy-start.14 = (f32[1,1,2,32,256]{4,3,2,1,0:T(8,128)S(1)}, f32[1,1,2,32,256]{4,3,2,1,0:T(8,128)}, u32[]{:S(2)}) copy-start(f32[1,1,2,32,256]{4,3,2,1,0:T(8,128)} %param.36) | copy-start | bytes 196612
  7.9 17.4 %copy-start.18 = (f32[2,1,1024]{2,1,0:T(1,128)S(1)}, f32[2,1,1024]{2,1,0:T(1,128)}, u32[]{:S(2)}) copy-start(f32[2,1,1024]{2,1,0:T(1,128)} %param.27) | copy-start | bytes 24580
  15.2 14.7 %all-to-all-start = ((f32[32,1,384]{2,1,0:T(1,128)}), f32[32,1,384]{2,1,0:T(1,128)S(1)}, u32[]{:S(2)}, u32[]{:S(2)}) async-start(f32[32,1,384]{2,1,0:T(1,128)} %reshape.250), calls=%async_computation | async-start | bytes 98304 | tf_op jit(solution)/shard_map/all_to_all | solution.py:27
  22.6 63.5 %copy-start.16 = (f32[2,256]{1,0:T(2,128)}, f32[2,256]{1,0:T(2,128)S(1)}, u32[]{:S(2)}) copy-start(f32[2,256]{1,0:T(2,128)S(1)} %slice.197.refs_3_) | copy-start | bytes 6148
  29.9 7.9 %all-to-all-start.1 = ((f32[4,1,8192]{2,1,0:T(1,128)}), f32[4,1,8192]{2,1,0:T(1,128)S(1)}, u32[]{:S(2)}, u32[]{:S(2)}) async-start(f32[4,1,8192]{2,1,0:T(1,128)} %reshape.252), calls=%async_computation.1 | async-start | bytes 262144 | tf_op jit(solution)/shard_map/all_to_all | solution.py:552
  39.8 20.1 %all-to-all-start.2 = ((bf16[8,64,256]{2,1,0:T(8,128)(2,1)}), bf16[8,64,256]{2,1,0:T(8,128)(2,1)S(1)}, u32[]{:S(2)}, u32[]{:S(2)}) async-start(bf16[8,64,256]{2,1,0:T(8,128)(2,1)} %broadcast_in_dim.26), calls=%async_computation.2 | async-start | bytes 524288 | tf_op jit(solution)/shard_map/all_to_all | solution.py:27
  59.9 16.5 %copy-start.2 = (bf16[8,64,256]{2,1,0:T(8,128)(2,1)}, bf16[8,64,256]{2,1,0:T(8,128)(2,1)S(1)}, u32[]{:S(2)}) copy-start(bf16[8,64,256]{2,1,0:T(8,128)(2,1)S(1)} %all-to-all-done.2.refs_3_) | copy-start | bytes 786436
  59.9 8.2 %collective-permute-start.1 = (bf16[8,64,256]{2,1,0:T(8,128)(2,1)S(1)}, bf16[8,64,256]{2,1,0:T(8,128)(2,1)S(1)}, u32[]{:S(2)}, u32[]{:S(2)}) collective-permute-start(bf16[8,64,256]{2,1,0:T(8,128)(2,1)S(1)} %all-to-all-done.2.refs_3_), channel_id=1, source_target_pairs={{0,16},{8,24},{16,0},{24,8},{1,17},{9,25},{17,1},{25,9},{2,18},{10... | collective-permute-start | bytes 786440 | tf_op jit(solution)/shard_map/ppermute | solution.py:532
  64.5 11.8 %collective-permute-start = (bf16[8,64,256]{2,1,0:T(8,128)(2,1)S(1)}, bf16[8,64,256]{2,1,0:T(8,128)(2,1)S(1)}, u32[]{:S(2)}, u32[]{:S(2)}) collective-permute-start(bf16[8,64,256]{2,1,0:T(8,128)(2,1)S(1)} %all-to-all-done.2.refs_3_), channel_id=1, source_target_pairs={{0,8},{8,0},{16,24},{24,16},{1,9},{9,1},{17,25},{25,17},{2,10},{10... | collective-permute-start | bytes 786440 | tf_op jit(solution)/shard_map/ppermute | solution.py:532
  68.1 8.3 %copy-start.5 = (bf16[8,64,256]{2,1,0:T(8,128)(2,1)}, bf16[8,64,256]{2,1,0:T(8,128)(2,1)S(1)}, u32[]{:S(2)}) copy-start(bf16[8,64,256]{2,1,0:T(8,128)(2,1)S(1)} %collective-permute-done.1.refs_5_) | copy-start | bytes 786436
  68.1 8.3 %collective-permute-start.2 = (bf16[8,64,256]{2,1,0:T(8,128)(2,1)S(1)}, bf16[8,64,256]{2,1,0:T(8,128)(2,1)S(1)}, u32[]{:S(2)}, u32[]{:S(2)}) collective-permute-start(bf16[8,64,256]{2,1,0:T(8,128)(2,1)S(1)} %collective-permute-done.1.refs_5_), channel_id=1, source_target_pairs={{0,8},{8,0},{16,24},{24,16},{1,9},{9,1},{17,25},{25,17},{2,10},{10... | collective-permute-start | bytes 786440 | tf_op jit(solution)/shard_map/ppermute | solution.py:532
  132.6 26.2 %copy-start.17 = (bf16[64,256]{1,0:T(8,128)(2,1)S(1)}, bf16[64,256]{1,0:T(8,128)(2,1)}, u32[]{:S(2)}) copy-start(bf16[64,256]{1,0:T(8,128)(2,1)} %get-tuple-element.69) | copy-start | bytes 98308
  160.8 44.8 %copy-start.15 = (f32[64,256]{1,0:T(8,128)S(1)}, f32[64,256]{1,0:T(8,128)}, u32[]{:S(2)}) copy-start(f32[64,256]{1,0:T(8,128)} %get-tuple-element.63) | copy-start | bytes 196612
  160.8 45.7 %copy-start.24 = (f32[8,64]{1,0:T(8,128)S(1)}, f32[8,64]{1,0:T(8,128)}, u32[]{:S(2)}) copy-start(f32[8,64]{1,0:T(8,128)} %get-tuple-element.65) | copy-start | bytes 6148
  160.9 35.8 %all-to-all-start.3 = ((bf16[8,320,256]{2,1,0:T(8,128)(2,1)}), bf16[8,320,256]{2,1,0:T(8,128)(2,1)S(1)}, u32[]{:S(2)}, u32[]{:S(2)}) async-start(bf16[8,320,256]{2,1,0:T(8,128)(2,1)} %broadcast_in_dim.30), calls=%async_computation.3 | async-start | bytes 2621440 | tf_op jit(solution)/shard_map/all_to_all | solution.py:27
  170.4 60.0 %copy-start.8 = (f32[256,64]{1,0:T(8,128)S(1)}, f32[256,64]{1,0:T(8,128)}, u32[]{:S(2)}) copy-start(f32[256,64]{1,0:T(8,128)} %get-tuple-element.79) | copy-start | bytes 196612
  170.4 60.0 %copy-start.9 = (f32[256,64]{1,0:T(8,128)S(1)}, f32[256,64]{1,0:T(8,128)}, u32[]{:S(2)}) copy-start(f32[256,64]{1,0:T(8,128)} %get-tuple-element.78) | copy-start | bytes 196612
  170.4 3.1 collective-permute-start.3
  170.7 6.6 %collective-permute-start.4 = (f32[256,64]{1,0:T(8,128)}, f32[256,64]{1,0:T(8,128)S(1)}, u32[]{:S(2)}, u32[]{:S(2)}) collective-permute-start(f32[256,64]{1,0:T(8,128)} %get-tuple-element.60), channel_id=1, source_target_pairs={{0,16},{8,24},{16,0},{24,8},{1,17},{9,25},{17,1},{25,9},{2,18},{10... | collective-permute-start | bytes 196616 | tf_op jit(solution)/shard_map/ppermute | solution.py:636
  172.2 6.3 %collective-permute-start.5 = (f32[256,64]{1,0:T(8,128)}, f32[256,64]{1,0:T(8,128)S(1)}, u32[]{:S(2)}, u32[]{:S(2)}) collective-permute-start(f32[256,64]{1,0:T(8,128)} %get-tuple-element.61), channel_id=1, source_target_pairs={{0,24},{8,16},{16,8},{24,0},{1,25},{9,17},{17,9},{25,1},{2,26},{10... | collective-permute-start | bytes 196616 | tf_op jit(solution)/shard_map/ppermute | solution.py:636
  196.7 74.3 %copy-start = (bf16[8,320,256]{2,1,0:T(8,128)(2,1)}, bf16[8,320,256]{2,1,0:T(8,128)(2,1)S(1)}, u32[]{:S(2)}) copy-start(bf16[8,320,256]{2,1,0:T(8,128)(2,1)S(1)} %all-to-all-done.3.refs_3_) | copy-start | bytes 3932164
  198.7 30.0 %all-to-all-start.4 = ((bf16[8,256,256]{2,1,0:T(8,128)(2,1)}), bf16[8,256,256]{2,1,0:T(8,128)(2,1)}, u32[]{:S(2)}, u32[]{:S(2)}) async-start(bf16[8,256,256]{2,1,0:T(8,128)(2,1)} %broadcast_in_dim.62), calls=%async_computation.4 | async-start | bytes 2097152 | tf_op jit(solution)/shard_map/all_to_all | solution.py:27
  213.8 58.7 %collective-permute-start.7 = (bf16[8,320,256]{2,1,0:T(8,128)(2,1)S(1)}, bf16[8,320,256]{2,1,0:T(8,128)(2,1)S(1)}, u32[]{:S(2)}, u32[]{:S(2)}) collective-permute-start(bf16[8,320,256]{2,1,0:T(8,128)(2,1)S(1)} %all-to-all-done.3.refs_3_), channel_id=1, source_target_pairs={{0,16},{8,24},{16,0},{24,8},{1,17},{9,25},{17,1},{25,9},{2,18},{10... | collective-permute-start | bytes 3932168 | tf_op jit(solution)/shard_map/ppermute | solution.py:532
  228.7 43.9 %collective-permute-start.9 = (bf16[8,256,256]{2,1,0:T(8,128)(2,1)}, bf16[8,256,256]{2,1,0:T(8,128)(2,1)}, u32[]{:S(2)}, u32[]{:S(2)}) collective-permute-start(bf16[8,256,256]{2,1,0:T(8,128)(2,1)} %all-to-all-done.4), channel_id=1, source_target_pairs={{0,8},{8,0},{16,24},{24,16},{1,9},{9,1},{17,25},{25,17},{2,10},{10... | collective-permute-start | bytes 3145736 | tf_op jit(solution)/shard_map/ppermute | solution.py:532
  228.7 43.3 %collective-permute-start.10 = (bf16[8,256,256]{2,1,0:T(8,128)(2,1)}, bf16[8,256,256]{2,1,0:T(8,128)(2,1)}, u32[]{:S(2)}, u32[]{:S(2)}) collective-permute-start(bf16[8,256,256]{2,1,0:T(8,128)(2,1)} %all-to-all-done.4), channel_id=1, source_target_pairs={{0,16},{8,24},{16,0},{24,8},{1,17},{9,25},{17,1},{25,9},{2,18},{10... | collective-permute-start | bytes 3145736 | tf_op jit(solution)/shard_map/ppermute | solution.py:532
  231.3 36.7 %all-to-all-start.6 = ((f32[4,1,8192]{2,1,0:T(1,128)}), f32[4,1,8192]{2,1,0:T(1,128)S(1)}, u32[]{:S(2)}, u32[]{:S(2)}) async-start(f32[4,1,8192]{2,1,0:T(1,128)} %reshape.254), calls=%async_computation.6 | async-start | bytes 262144 | tf_op jit(solution)/shard_map/all_to_all | solution.py:641
  269.1 15.5 %collective-permute-start.6 = (bf16[8,320,256]{2,1,0:T(8,128)(2,1)S(1)}, bf16[8,320,256]{2,1,0:T(8,128)(2,1)}, u32[]{:S(2)}, u32[]{:S(2)}) collective-permute-start(bf16[8,320,256]{2,1,0:T(8,128)(2,1)S(1)} %all-to-all-done.3.refs_3_), channel_id=1, source_target_pairs={{0,8},{8,0},{16,24},{24,16},{1,9},{9,1},{17,25},{25,17},{2,10},{10... | collective-permute-start | bytes 3932168 | tf_op jit(solution)/shard_map/ppermute | solution.py:532
  270.9 8.3 %slice-start = ((s8[6553600]{0:T(1024)(128)(4,1)}), s8[4194304]{0:T(1024)(128)(4,1)S(1)}, s32[]{:S(2)}) async-start(s8[6553600]{0:T(1024)(128)(4,1)} %bitcast.193), calls=%async_computation.8 | async-start | bytes 8388608
  272.0 14.9 %collective-permute-start.11 = (bf16[8,256,256]{2,1,0:T(8,128)(2,1)}, bf16[8,256,256]{2,1,0:T(8,128)(2,1)S(1)}, u32[]{:S(2)}, u32[]{:S(2)}) collective-permute-start(bf16[8,256,256]{2,1,0:T(8,128)(2,1)} %collective-permute-done.10), channel_id=1, source_target_pairs={{0,8},{8,0},{16,24},{24,16},{1,9},{9,1},{17,25},{25,17},{2,10},{10... | collective-permute-start | bytes 3145736 | tf_op jit(solution)/shard_map/ppermute | solution.py:532
  272.5 11.1 %copy-start.1 = (bf16[8,320,256]{2,1,0:T(8,128)(2,1)}, bf16[8,320,256]{2,1,0:T(8,128)(2,1)S(1)}, u32[]{:S(2)}) copy-start(bf16[8,320,256]{2,1,0:T(8,128)(2,1)S(1)} %collective-permute-done.7.refs_5_) | copy-start | bytes 3932164
  272.5 17.6 %collective-permute-start.8 = (bf16[8,320,256]{2,1,0:T(8,128)(2,1)S(1)}, bf16[8,320,256]{2,1,0:T(8,128)(2,1)}, u32[]{:S(2)}, u32[]{:S(2)}) collective-permute-start(bf16[8,320,256]{2,1,0:T(8,128)(2,1)S(1)} %collective-permute-done.7.refs_5_), channel_id=1, source_target_pairs={{0,8},{8,0},{16,24},{24,16},{1,9},{9,1},{17,25},{25,17},{2,10},{10... | collective-permute-start | bytes 3932168 | tf_op jit(solution)/shard_map/ppermute | solution.py:532
  272.6 6.6 %slice-start.1 = ((s8[6553600]{0:T(1024)(128)(4,1)}), s8[2359296]{0:T(1024)(128)(4,1)S(1)}, s32[]{:S(2)}) async-start(s8[6553600]{0:T(1024)(128)(4,1)} %bitcast.193), calls=%async_computation.9 | async-start | bytes 4718592
  290.1 9.0 %copy-start.3 = (bf16[8,256,256]{2,1,0:T(8,128)(2,1)S(1)}, bf16[8,256,256]{2,1,0:T(8,128)(2,1)}, u32[]{:S(2)}) copy-start(bf16[8,256,256]{2,1,0:T(8,128)(2,1)} %slice.266) | copy-start | bytes 3145732
  290.1 9.0 %copy-start.28 = (f32[1600,256]{1,0:T(8,128)S(1)}, f32[1600,256]{1,0:T(8,128)}, u32[]{:S(2)}) copy-start(f32[1600,256]{1,0:T(8,128)} %fusion.33) | copy-start | bytes 4915204
  307.3 12.8 %slice-start.2 = ((s8[6553600]{0:T(1024)(128)(4,1)}), s8[2359296]{0:T(1024)(128)(4,1)S(1)}, s32[]{:S(2)}) async-start(s8[6553600]{0:T(1024)(128)(4,1)} %bitcast.195), calls=%async_computation.10 | async-start | bytes 4718592
  307.3 20.5 %all-to-all-start.5 = ((f32[32,1,2819]{2,1,0:T(1,128)}), f32[32,1,2819]{2,1,0:T(1,128)S(1)}, u32[]{:S(2)}, u32[]{:S(2)}) async-start(f32[32,1,2819]{2,1,0:T(1,128)} %broadcast_in_dim.63), calls=%async_computation.5 | async-start | bytes 753664 | tf_op jit(solution)/shard_map/all_to_all | solution.py:27
  313.2 6.9 %slice-start.3 = ((s8[6553600]{0:T(1024)(128)(4,1)}), s8[4194304]{0:T(1024)(128)(4,1)S(1)}, s32[]{:S(2)}) async-start(s8[6553600]{0:T(1024)(128)(4,1)} %bitcast.195), calls=%async_computation.11 | async-start | bytes 8388608
  313.2 6.9 %copy-start.4 = (bf16[8,256,256]{2,1,0:T(8,128)(2,1)S(1)}, bf16[8,256,256]{2,1,0:T(8,128)(2,1)}, u32[]{:S(2)}) copy-start(bf16[8,256,256]{2,1,0:T(8,128)(2,1)} %slice.273) | copy-start | bytes 3145732
  313.3 6.9 %copy-start.29 = (f32[1600,256]{1,0:T(8,128)S(1)}, f32[1600,256]{1,0:T(8,128)}, u32[]{:S(2)}) copy-start(f32[1600,256]{1,0:T(8,128)} %fusion.35) | copy-start | bytes 4915204
  324.6 10.6 %copy-start.20 = (f32[2,1,1024]{2,1,0:T(1,128)S(1)}, f32[2,1,1024]{2,1,0:T(1,128)}, u32[]{:S(2)}) copy-start(f32[2,1,1024]{2,1,0:T(1,128)} %param.29) | copy-start | bytes 24580
  324.6 10.6 %copy-start.21 = (f32[2,1,1024]{2,1,0:T(1,128)S(1)}, f32[2,1,1024]{2,1,0:T(1,128)}, u32[]{:S(2)}) copy-start(f32[2,1,1024]{2,1,0:T(1,128)} %param.28) | copy-start | bytes 24580
  324.6 11.3 %copy-start.22 = (f32[3,256]{1,0:T(4,128)S(1)}, f32[3,256]{1,0:T(4,128)}, u32[]{:S(2)}) copy-start(f32[3,256]{1,0:T(4,128)} %param.32) | copy-start | bytes 9220
  324.7 11.3 %copy-start.23 = (f32[3,256]{1,0:T(4,128)S(1)}, f32[3,256]{1,0:T(4,128)}, u32[]{:S(2)}) copy-start(f32[3,256]{1,0:T(4,128)} %param.31) | copy-start | bytes 9220
  (7 other events, 19.2 us)
Sparse Core Ops, SparseCore 0:
  13.6 110.1 all-gather.4

commit v2 on v1

--- a/solution.py
+++ b/solution.py
@@ -31,9 +31,30 @@
     return jax.ShapeDtypeStruct(dims, kind)
 
 
+def hint(microseconds):
+    return pl.CostEstimate(
+        flops=int(microseconds * 0.35 * 1e9), bytes_accessed=int(microseconds * 0.35 * 3e6), transcendentals=0
+    )
+
+
 def whole(array):
     dims = array.shape
     return pl.BlockSpec(dims, lambda *unused: (0,) * len(dims))
+
+
+def after(value, *others):
+    def body(*refs):
+        pass
+
+    anywhere = pl.BlockSpec(memory_space=pl.ANY)
+    return pl.pallas_call(
+        body,
+        out_shape=shape(value.shape, value.dtype),
+        in_specs=[anywhere] * (1 + len(others)),
+        out_specs=anywhere,
+        input_output_aliases={0: 0},
+        name="after",
+    )(value, *others)
 
 
 def columns_kernel(place, first, second, third, fourth, out):
@@ -54,7 +75,8 @@
     own, gate_dim = kernels.shape
     lanes = 2 * GROUP_SIZE
     per_quarter = gate_dim // 4 // lanes
-    step = own // 5
+    steps = 2 if own % 32 == 0 else 5
+    step = own // steps
     place = jnp.stack([block // 2, block % 2]).astype(I32)
 
     def spec(quarter):
@@ -65,7 +87,7 @@
         out_shape=shape((own, 4 * GROUP_SIZE), BF),
         grid_spec=pltpu.PrefetchScalarGridSpec(
             num_scalar_prefetch=1,
-            grid=(5,),
+            grid=(steps,),
             in_specs=[spec(q) for q in range(4)],
             out_specs=pl.BlockSpec((step, 4 * GROUP_SIZE), lambda i, where: (i, 0)),
         ),
@@ -83,18 +105,19 @@
     return jnp.dot(values, mixer, precision=EXACT, preferred_element_type=F32)
 
 
-def fill_bands(bands, image, columns):
-    pixels = image.shape[0]
+def fill_bands(bands, image, columns, mirrored=False):
+    pixels, depth = image.shape
     edge = MARGIN * columns
     column = lax.broadcasted_iota(I32, image.shape, 0) % columns
-    blank = jnp.zeros((edge, image.shape[1]), BF)
+    blank = jnp.zeros((edge, depth), BF)
     for d in range(KERNEL):
-        move = d - MARGIN
+        move = (MARGIN - d) if mirrored else (d - MARGIN)
+        lanes = slice(d * depth, (d + 1) * depth)
         moved = image if move == 0 else pltpu.roll(image, (-move) % pixels, 0)
         inside = (column + move >= 0) & (column + move < columns)
-        bands[d, edge : edge + pixels, :] = jnp.where(inside, moved, 0.0).astype(BF)
-        bands[d, :edge, :] = blank
-        bands[d, edge + pixels :, :] = blank
+        bands[edge : edge + pixels, lanes] = jnp.where(inside, moved, 0.0).astype(BF)
+        bands[:edge, lanes] = blank
+        bands[edge + pixels :, lanes] = blank
 
 
 def cell_parts(gates, cells_prev, gain, shift):
@@ -113,43 +136,42 @@
 
 def forward_kernel(
     columns, first_row, obs, hid, ends, weight, cells_prev, norms, head,
-    gates_out, cells_out, hidden_out, low_out, turned_out, seen_out, bands, total,
+    gates_out, cells_out, hidden_out, low_out, turned_out, seen_out, bands, total, near, arrived,
 ):
-    step = pl.program_id(0)
     pixels = total.shape[0]
 
-    @pl.when(step == 0)
-    def start():
-        lifted = (ends[0:1, :] * obs[...] + ends[1:2, :]).astype(BF).astype(F32)
-        fill_bands(bands, jnp.concatenate([lifted, hid[...].astype(F32)], axis=1), columns)
-        total[...] = jnp.zeros_like(total)
-
-    begin = pl.multiple_of((first_row[0] + step) * columns, columns)
-    part = total[...]
-    for d in range(KERNEL):
-        part = part + jnp.dot(
-            bands[d, pl.ds(begin, pixels), :], weight[d], preferred_element_type=F32
+    def fetch(step):
+        return pltpu.make_async_copy(weight.at[step], near.at[step], arrived.at[step])
+
+    for step in range(KERNEL):
+        fetch(step).start()
+    lifted = (ends[0:1, :] * obs[...] + ends[1:2, :]).astype(BF).astype(F32)
+    fill_bands(bands, jnp.concatenate([lifted, hid[...].astype(F32)], axis=1), columns)
+    total[...] = jnp.zeros_like(total)
+
+    @pl.loop(0, KERNEL)
+    def tap_row(step):
+        begin = pl.multiple_of((first_row[0] + step) * columns, columns)
+        fetch(step).wait()
+        total[...] += jnp.dot(
+            bands[pl.ds(begin, pixels), :], near[step], preferred_element_type=F32
         )
-    total[...] = part
-
-    @pl.when(step == KERNEL - 1)
-    def finish():
-        gates = total[...]
-        parts = cell_parts(gates, cells_prev[...], norms[0:1, :], norms[1:2, :])
-        output_gate, cells = parts[5], parts[6]
-        hidden = output_gate * jnp.tanh(cells)
-        gates_out[...] = gates
-        cells_out[...] = cells
-        hidden_out[...] = hidden
-        low_out[...] = hidden.astype(BF)
-        turned_out[...] = jnp.transpose(hidden).astype(BF)
-        seen_out[...] = lax.dot_general(
-            head[...], hidden, (((1,), (1,)), ((), ())), precision=EXACT,
-            preferred_element_type=F32,
-        )
-
-
-def forward_frame(columns, rows, first_row, obs, hid, ends, weight, cells_prev, norms, head):
+
+    gates = total[...]
+    parts = cell_parts(gates, cells_prev[...], norms[0:1, :], norms[1:2, :])
+    output_gate, cells = parts[5], parts[6]
+    hidden = output_gate * jnp.tanh(cells)
+    gates_out[...] = gates
+    cells_out[...] = cells
+    hidden_out[...] = hidden
+    low_out[...] = hidden.astype(BF)
+    turned_out[...] = jnp.broadcast_to(jnp.transpose(hidden).astype(BF)[None], turned_out.shape)
+    seen_out[...] = lax.dot_general(
+        head[...], hidden, (((1,), (1,)), ((), ())), precision=EXACT, preferred_element_type=F32
+    )[0:1, :]
+
+
+def forward_frame(copies, columns, first_row, obs, hid, ends, weight, cells_prev, norms, head):
     pixels, width = cells_prev.shape
     image = hid.shape[0]
     gate = 4 * width
@@ -158,8 +180,8 @@
         shape((pixels, width), F32),
         shape((pixels, width), F32),
         shape((pixels, width), BF),
-        shape((width, pixels), BF),
-        shape((8, pixels), F32),
+        shape((copies, width, pixels), BF),
+        shape((1, pixels), F32),
     )
 
     def body(*refs):
@@ -170,24 +192,30 @@
         out_shape=outs,
         grid_spec=pltpu.PrefetchScalarGridSpec(
             num_scalar_prefetch=1,
-            grid=(KERNEL,),
+            grid=(1,),
             in_specs=[
                 whole(obs),
                 whole(hid),
                 whole(ends),
-                pl.BlockSpec((KERNEL, IN_DIM, gate), lambda i, first: (i, 0, 0)),
+                pl.BlockSpec(memory_space=pl.ANY),
                 whole(cells_prev),
                 whole(norms),
                 whole(head),
             ],
             out_specs=[whole(o) for o in outs],
             scratch_shapes=[
-                pltpu.VMEM((KERNEL, image + 2 * MARGIN * columns, IN_DIM), BF),
+                pltpu.VMEM((image + 2 * MARGIN * columns, KERNEL * IN_DIM), BF),
                 pltpu.VMEM((pixels, gate), F32),
+                pltpu.VMEM((KERNEL, KERNEL * IN_DIM, gate), BF),
+                pltpu.SemaphoreType.DMA((KERNEL,)),
             ],
         ),
+        cost_estimate=hint(4),
         name="forward_frame",
-    )(first_row, obs, hid, ends, weight, cells_prev, norms, head)
+    )(
+        first_row, obs, hid, ends, weight.reshape(KERNEL, KERNEL * IN_DIM, gate), cells_prev,
+        norms, head,
+    )
 
 
 def backward_kernel(last, *refs):
@@ -233,17 +261,19 @@
     scaled = grad_normed * gain
     grad_gates = inverse * (scaled - group_mean(scaled) - norm * group_mean(scaled * norm))
     low = grad_gates.astype(BF)
-    low_out[...] = low
+    low_out[...] = jnp.broadcast_to(low[None], low_out.shape)
     echo_out[...] = jnp.dot(
         looks[...], low.astype(F32), precision=EXACT, preferred_element_type=F32
     )
 
 
-def backward_frame(scalars, seen, target, valid, gates, cells_prev, norms, head, looks, later):
+def backward_frame(
+    copies, scalars, seen, target, valid, gates, cells_prev, norms, head, looks, later
+):
     pixels, width = cells_prev.shape
     gate = 4 * width
     outs = (
-        shape((pixels, gate), BF),
+        shape((copies, pixels, gate), BF),
         shape((pixels, width), F32),
         shape((8, gate), F32),
         shape((looks.shape[0], gate), F32),
@@ -262,57 +292,65 @@
         in_specs=[pl.BlockSpec(memory_space=pltpu.SMEM)] + [whole(a) for a in args],
         out_specs=[whole(o) for o in outs],
         grid=(1,),
+        cost_estimate=hint(4),
         name="backward_cell",
     )(scalars, *args)
 
 
 def hidden_kernel(columns, me, above, low, below, weight, *refs):
-    outs, (bands, total, held) = refs[:-3], refs[-3:]
-    step = pl.program_id(0)
-    pixels = low.shape[0]
+    outs, (bands, total, held, near, arrived) = refs[:-5], refs[-5:]
+    pixels = low.shape[1]
     blocks, unused, width = held.shape
 
-    @pl.when(step == 0)
-    def start():
-        fill_bands(bands, low[...].astype(F32), columns)
-        edge = MARGIN * columns
-        if above is not None:
-            for side, place in ((above, 0), (below, edge + pixels)):
-                image = side[...].astype(F32)
-                column = lax.broadcasted_iota(I32, image.shape, 0) % columns
-                for d in range(KERNEL):
-                    move = d - MARGIN
-                    moved = image if move == 0 else pltpu.roll(image, (-move) % edge, 0)
-                    inside = (column + move >= 0) & (column + move < columns)
-                    bands[d, place : place + edge, :] = jnp.where(inside, moved, 0.0).astype(BF)
-        total[...] = jnp.zeros_like(total)
-
-    begin = pl.multiple_of((KERNEL - 1 - step) * columns, columns)
-    part = total[...]
-    for d in range(KERNEL):
-        part = part + lax.dot_general(
-            bands[KERNEL - 1 - d, pl.ds(begin, pixels), :],
-            weight[d, 0],
+    def fetch(step):
+        return pltpu.make_async_copy(
+            weight.at[pl.ds(step * KERNEL, KERNEL), 1], near.at[step], arrived.at[step]
+        )
+
+    for step in range(KERNEL):
+        fetch(step).start()
+    fill_bands(bands, low[0].astype(F32), columns, mirrored=True)
+    edge = MARGIN * columns
+    if above is not None:
+        for side, place in ((above, 0), (below, edge + pixels)):
+            image = side[...].astype(F32)
+            column = lax.broadcasted_iota(I32, image.shape, 0) % columns
+            depth = image.shape[1]
+            for d in range(KERNEL):
+                move = MARGIN - d
+                moved = image if move == 0 else pltpu.roll(image, (-move) % edge, 0)
+                inside = (column + move >= 0) & (column + move < columns)
+                bands[place : place + edge, d * depth : (d + 1) * depth] = jnp.where(
+                    inside, moved, 0.0
+                ).astype(BF)
+    total[...] = jnp.zeros_like(total)
+
+    @pl.loop(0, KERNEL)
+    def tap_row(step):
+        begin = pl.multiple_of((KERNEL - 1 - step) * columns, columns)
+        fetch(step).wait()
+        taps = jnp.concatenate([near[step, d] for d in range(KERNEL)], axis=1)
+        total[...] += lax.dot_general(
+            bands[pl.ds(begin, pixels), :],
+            taps,
             (((1,), (1,)), ((), ())),
             preferred_element_type=F32,
         )
-    total[...] = part
-
-    @pl.when(step == KERNEL - 1)
-    def finish():
-        for b in range(blocks):
-            held[jnp.bitwise_xor(b, me[0])] = total[:, b * width : (b + 1) * width]
-        for k in range(blocks):
-            outs[k][...] = held[k]
+
+    for b in range(blocks):
+        held[jnp.bitwise_xor(b, me[0])] = total[:, b * width : (b + 1) * width]
+    for k in range(blocks):
+        outs[k][...] = held[k]
 
 
 def hidden_gradient(columns, blocks, me, sides, low, weight):
-    pixels, gate = low.shape
+    unused, pixels, gate = low.shape
     hidden_dim = weight.shape[1] // 2
     halves = weight.reshape(TAPS, 2, hidden_dim, gate)
     width = hidden_dim // blocks
     outs = (shape((pixels, width), F32),) * blocks
     args = [low] if sides is None else [sides[0], low, sides[1]]
+    specs = [pl.BlockSpec((1,) + a.shape[1:], lambda *i: (0, 0, 0)) if a is low else whole(a) for a in args]
 
     def body(me_ref, *refs):
         if sides is None:
@@ -325,16 +363,18 @@
         out_shape=outs,
         grid_spec=pltpu.PrefetchScalarGridSpec(
             num_scalar_prefetch=1,
-            grid=(KERNEL,),
-            in_specs=[whole(a) for a in args]
-            + [pl.BlockSpec((KERNEL, 1, hidden_dim, gate), lambda i, where: (i, 1, 0, 0))],
+            grid=(1,),
+            in_specs=specs + [pl.BlockSpec(memory_space=pl.ANY)],
             out_specs=[whole(o) for o in outs],
             scratch_shapes=[
-                pltpu.VMEM((KERNEL, pixels + 2 * MARGIN * columns, gate), BF),
+                pltpu.VMEM((pixels + 2 * MARGIN * columns, KERNEL * gate), BF),
                 pltpu.VMEM((pixels, hidden_dim), F32),
                 pltpu.VMEM((blocks, pixels, width), F32),
+                pltpu.VMEM((KERNEL, KERNEL, hidden_dim, gate), BF),
+                pltpu.SemaphoreType.DMA((KERNEL,)),
             ],
         ),
+        cost_estimate=hint(4),
         name="hidden_gradient",
     )(me, *args, halves)
 
@@ -372,9 +412,9 @@
     out[...] = patches[pl.ds(skip, own), :]
 
 
-def owned_patches(columns, slabs, own, span, places, obs, hid, width, row, ends):
+def owned_patches(columns, slabs, own, span, places, obs, hid, ends):
     owners, unused, image = obs.shape
-    tiles, pixels = len(hid), hid[0].shape[2]
+    tiles, (unused_too, width, pixels) = len(hid), hid[0].shape
 
     def body(*refs):
         patches_kernel(columns, slabs, tiles, *refs)
@@ -389,7 +429,7 @@
                 pl.BlockSpec((1, 1, image), lambda s, where: (s, 0, 0)),
                 whole(ends),
             ]
-            + [pl.BlockSpec((1, width, pixels), lambda s, where: (s, row, 0))] * tiles,
+            + [pl.BlockSpec((1, width, pixels), lambda s, where: (s, 0, 0))] * tiles,
             out_specs=pl.BlockSpec((own, image), lambda s, where: (0, s)),
             scratch_shapes=[
                 pltpu.VMEM((span, image, image), BF),
@@ -397,6 +437,7 @@
                 pltpu.VMEM((tiles, width, pixels), BF),
             ],
         ),
+        cost_estimate=hint(9),
         name="owned_patches",
     )(places, obs, ends, *hid)
 
@@ -408,44 +449,173 @@
     return (weight - rate * (update + 0.01 * weight), moment_new, second_new)
 
 
-def adamw_kernel(blocks, rate, me, scalars, *refs):
-    grads = refs[:blocks]
-    weight, moment, second, weight_out, moment_out, second_out, held = refs[blocks:]
+def rows_at_once(own):
+    return 16 * math.gcd(own // 16, 20)
+
+
+def patch_dot(patch, pieces):
+    flat = [p[...].reshape(patch.shape[1], p.shape[2]) for p in pieces]
+    signal = flat[0] if len(flat) == 1 else jnp.concatenate(flat, axis=1)
+    return jnp.dot(patch[...], signal, preferred_element_type=F32)
+
+
+def gradient_kernel(blocks, squared, patch, *refs):
+    pieces, refs = refs[:blocks], refs[blocks:]
+    grad = patch_dot(patch, pieces)
+    gate = pieces[0].shape[2]
+    if squared:
+        base, grad_out, square_out = refs
+        grad = grad + base[...]
+
+        @pl.when(pl.program_id(0) == 0)
+        def start():
+            square_out[...] = jnp.zeros_like(square_out)
+
+        lanes = square_out.shape[1]
+        square = grad * grad
+        square = square[:, :lanes] + square[:, lanes:]
+        square_out[...] += jnp.sum(square, axis=0, keepdims=True)
+        grad_out[...] = grad
+    else:
+        for k in range(blocks):
+            refs[k][...] = grad[:, k * gate : (k + 1) * gate]
+
+
+def patch_gradient(patch, pieces, base=None, waits=()):
+    own, gate = patch.shape[0], pieces[0].shape[2]
+    step = own // 2
+    rows = pl.BlockSpec((step, gate), lambda i: (i, 0))
+    outs = [shape((own, gate), F32) for p in pieces]
+    out_specs = [rows] * len(pieces)
+    args = [patch] + list(pieces)
+    in_specs = [pl.BlockSpec((step, patch.shape[1]), lambda i: (i, 0))] + [whole(p) for p in pieces]
+    if base is not None:
+        args, in_specs = args + [base], in_specs + [rows]
+        outs = outs + [shape((1, gate // 2), F32)]
+        out_specs = out_specs + [pl.BlockSpec((1, gate // 2), lambda i: (0, 0))]
+
+    n = len(args)
+    args, in_specs = args + list(waits), in_specs + [pl.BlockSpec(memory_space=pl.ANY)] * len(waits)
+
+    def body(*refs):
+        gradient_kernel(len(pieces), base is not None, *refs[:n], *refs[n + len(waits) :])
+
+    return pl.pallas_call(
+        body,
+        out_shape=tuple(outs),
+        grid=(own // step,),
+        in_specs=in_specs,
+        out_specs=out_specs,
+        compiler_params=pltpu.CompilerParams(vmem_limit_bytes=60 << 20),
+        cost_estimate=hint(3 + 2 * len(pieces)),
+        name="patch_gradient",
+    )(*args)
+
+
+def small_update(scalars, everyone, triples, factor_row, smalls_out, measures_out):
+    total = jnp.sum(everyone[...], axis=0)
+    lanes = total.shape[1]
+    gate_dim, hidden_dim = triples[0].shape[2], triples[3].shape[1]
+    norm_rows = 2 * gate_dim // lanes
+    end_rows = 3 * hidden_dim // lanes
+    last = norm_rows + end_rows
+    row = lax.broadcasted_iota(I32, total.shape, 0)
+    lane = lax.broadcasted_iota(I32, total.shape, 1)
+    wide = (row < last) | ((row == last) & (lane == 0))
+    alone = row == last + 1
+    squares = jnp.where(wide, total * total, jnp.where(alone, total, 0.0))
+    grad_norm = jnp.sqrt(jnp.sum(jnp.sum(squares, axis=0, keepdims=True), axis=1, keepdims=True))
+    factor = clip_limit / jnp.maximum(grad_norm, clip_limit)
+    factor_row[...] = jnp.broadcast_to(factor, factor_row.shape)
+    measures_out[0][...] = total[last : last + 1, 1:2] / scalars[1]
+    measures_out[1][...] = grad_norm
+
+    def line(begin, length):
+        return jnp.concatenate([total[r : r + 1, :] for r in range(begin, begin + length)], axis=1)
+
+    def update(place, grad, index):
+        found = [t[index] for t in triples[place : place + 3]]
+        got = adamw(*found, grad * factor, small_rate, scalars[0])
+        for out, value in zip(smalls_out[place : place + 3], got):
+            out[index] = value
+
+    for r in range(2):
+        update(0, line(r * norm_rows // 2, norm_rows // 2), r)
+    for r in range(3):
+        update(3, line(norm_rows + r * end_rows // 3, end_rows // 3), slice(r, r + 1))
+    update(6, total[last : last + 1, 0:1], slice(0, 1))
+
+
+def last_kernel(blocks, extra, rate, me, scalars, everyone, *refs):
+    triples, refs = refs[:9], refs[9:]
+    bases, refs = refs[:blocks], refs[blocks:]
+    pieces, refs = refs[:extra], refs[extra:]
+    held, factor_row = refs[-2:]
+    weight, moment, second, weight_out, moment_out, second_out = refs[:6]
+    measures_out, smalls_out = refs[6:8], refs[8:17]
+
+    @pl.when(pl.program_id(0) == 0)
+    def start():
+        small_update(scalars, everyone, triples, factor_row, smalls_out, measures_out)
+
     for k in range(blocks):
-        held[k] = grads[k][...]
+        held[k] = bases[k][...]
+    if extra:
+        patch, pieces = pieces[0], pieces[1:]
+        grad = patch_dot(patch, pieces)
+        gate = held.shape[2]
+        for k in range(1, blocks):
+            held[k] += grad[:, (k - 1) * gate : k * gate]
     width = held.shape[2] // 4
     placed = [held[jnp.bitwise_xor(b, me[0])] for b in range(blocks)]
     for q in range(4):
         grad = jnp.concatenate([p[:, q * width : (q + 1) * width] for p in placed], axis=1)
         cols = slice(q * blocks * width, (q + 1) * blocks * width)
         weight_out[:, cols], moment_out[:, cols], second_out[:, cols] = adamw(
-            weight[:, cols], moment[:, cols], second[:, cols], grad * scalars[0], rate, scalars[1]
+            weight[:, cols], moment[:, cols], second[:, cols], grad * factor_row[...], rate,
+            scalars[0],
         )
 
 
-def kernel_update(me, scalars, grads, weight, moment, second, rate):
-    own, gate_dim = weight.shape
-    blocks = len(grads)
-    step = own // 10
+def last_update(me, scalars, everyone, smalls, bases, late, kernel_triple, rate):
+    own, gate_dim = kernel_triple[0].shape
+    blocks = len(bases)
+    step = rows_at_once(own)
     gate = gate_dim // blocks
     wide = pl.BlockSpec((step, gate_dim), lambda i, where: (i, 0))
     thin = pl.BlockSpec((step, gate), lambda i, where: (i, 0))
+    late_specs = []
+    if late:
+        late_specs = [pl.BlockSpec((step, late[0].shape[1]), lambda i, where: (i, 0))]
+        late_specs += [whole(p) for p in late[1:]]
+    measures = [shape((1, 1), F32)] * 2
 
     def body(*refs):
-        adamw_kernel(blocks, rate, *refs)
+        n = 3 + 9 + blocks + len(late)
+        ins, outs = refs[: n + 3], refs[n + 3 :]
+        last_kernel(blocks, len(late), rate, *ins, *outs)
 
     return pl.pallas_call(
         body,
-        out_shape=(shape((own, gate_dim), F32),) * 3,
+        out_shape=tuple([shape((own, gate_dim), F32)] * 3 + measures + [shape(t.shape, F32) for t in smalls]),
         grid_spec=pltpu.PrefetchScalarGridSpec(
             num_scalar_prefetch=1,
-            grid=(10,),
-            in_specs=[pl.BlockSpec(memory_space=pltpu.SMEM)] + [thin] * blocks + [wide] * 3,
-            out_specs=[wide] * 3,
-            scratch_shapes=[pltpu.VMEM((blocks, step, gate), F32)],
+            grid=(own // step,),
+            in_specs=[pl.BlockSpec(memory_space=pltpu.SMEM), whole(everyone)]
+            + [whole(t) for t in smalls]
+            + [thin] * blocks
+            + late_specs
+            + [wide] * 3,
+            out_specs=[wide] * 3 + [whole(m) for m in measures] + [whole(t) for t in smalls],
+            scratch_shapes=[
+                pltpu.VMEM((blocks, step, gate), F32),
+                pltpu.VMEM((1, gate_dim // 4), F32),
+            ],
         ),
-        name="kernel_update",
-    )(me, scalars, *grads, weight, moment, second)
+        compiler_params=pltpu.CompilerParams(vmem_limit_bytes=60 << 20),
+        cost_estimate=hint(22),
+        name="last_update",
+    )(me, scalars, everyone, *smalls, *bases, *late, *kernel_triple)
 
 
 def split_low(values):
@@ -522,7 +692,7 @@
 
     me = jnp.reshape(block if slabs == 1 else jnp.zeros_like(block), (1,)).astype(I32)
 
-    def all_tiles(values):
+    def all_tiles(values, between=()):
         if slabs > 1:
             got = lax.all_gather(values, "tile")
             return [got[k] for k in range(tiles)]
@@ -530,6 +700,8 @@
         while stride:
             pairs = [(j, j ^ stride) for j in range(tiles)]
             held = held + [lax.ppermute(h, "tile", pairs) for h in held]
+            if between and stride > 1:
+                held[1:] = [after(h, *between) for h in held[1:]]
             order = order + [k ^ stride for k in order]
             stride //= 2
         return [held[order.index(k)] for k in range(tiles)]
@@ -541,11 +713,9 @@
         places += [(first_tap + k) // KERNEL - MARGIN, (first_tap + k) % KERNEL - MARGIN]
     places = jnp.stack(places).astype(I32)
 
-    def patches_of(frame_no, hid, row):
+    def patches_of(frame_no, hid):
         obs_rows = obs_all[frame_no].reshape(owners, 1, image)
-        return owned_patches(
-            columns, slabs, own, span, places, obs_rows, hid, width, row, ends_turned
-        )
+        return owned_patches(columns, slabs, own, span, places, obs_rows, hid, ends_turned)
 
     states = jnp.stack([hidden_init[0, 0], cells_init[0, 0]])
     states = states.reshape(2, tile_rows * columns, blocks, width).transpose(2, 0, 1, 3)
@@ -554,7 +724,7 @@
     low = states[0].astype(BF)
     cells = states[1]
     patches = [None] * frames
-    patches[0] = patches_of(0, all_tiles(spread(low.T, "dp")), 0)
+    patches[0] = patches_of(0, all_tiles(spread(low.T, "dp")))
 
     def whole_hidden(values):
         got = lax.all_gather(values, "tile").reshape(slabs, blocks, pixels, width)
@@ -562,17 +732,20 @@
 
     weight, patches[0] = lax.optimization_barrier((weight, patches[0]))
     first = jnp.reshape(first_row, (1,)).astype(I32)
-    kept, turns, seen, turned = [], [], [], None
+    kept, seen, turns = [], [], [None] * frames
     for frame_no in range(frames):
         obs_column = mine[0, frame_no].reshape(image, 1)
-        turns.append(turned)
         gates, cells_next, hidden, low_next, turned, seen_part = forward_frame(
-            columns, rows, first, obs_column, whole_hidden(low), ends, weight, cells, norms, head
+            owners, columns, first, obs_column, whole_hidden(low), ends, weight, cells, norms, head
         )
         kept.append((gates, cells))
         cells, low = cells_next, low_next
         seen.append(seen_part[0])
+        if frame_no + 1 < frames:
+            turns[frame_no + 1] = lax.all_to_all(turned, "dp", 0, 0)
     seen = lax.all_gather(jnp.stack(seen), "tile", axis_index_groups=groups)
+    seen, turns[1:] = lax.optimization_barrier((seen, turns[1:]))
+    turns[1:] = [all_tiles(t) for t in turns[1:]]
     scalars = jnp.stack([head_bias[0], count])
 
     padded = jnp.pad(
@@ -601,7 +774,8 @@
     parcels = [None] * frames
     for frame_no in reversed(range(frames)):
         gates, cells_prev = kept[frame_no]
-        low, grad_cells, sums_part, echo_part, rows_part, head_part = backward_frame(
+        lows, grad_cells, sums_part, echo_part, rows_part, head_part = backward_frame(
+            owners,
             scalars,
             seen[:, frame_no],
             mine_rows[1, frame_no],
@@ -613,8 +787,7 @@
             looks[frame_no],
             later,
         )
-        parcel = low if frame_no == 0 else jnp.concatenate([low, turns[frame_no]], axis=0)
-        parcels[frame_no] = spread(parcel, "dp")
+        parcels[frame_no] = lax.all_to_all(lows, "dp", 0, 0)
         sums, echo = sums + sums_part, echo + echo_part
         rows_sum, head_sum = rows_sum + rows_part, head_sum + head_part
         if frame_no > 0:
@@ -623,52 +796,26 @@
                 edge = MARGIN * columns
                 up = [(s, s - blocks) for s in range(blocks, tiles)]
                 down = [(s - blocks, s) for s in range(blocks, tiles)]
-                below = lax.ppermute(low[:edge], "tile", up)
-                above = lax.ppermute(low[pixels - edge :], "tile", down)
+                below = lax.ppermute(lows[0, :edge], "tile", up)
+                above = lax.ppermute(lows[0, pixels - edge :], "tile", down)
                 sides = (above, below)
             pieces = list(
                 hidden_gradient(
-                    columns, blocks, jnp.reshape(block, (1,)).astype(I32), sides, low, weight
+                    columns, blocks, jnp.reshape(block, (1,)).astype(I32), sides, lows, weight
                 )
             )
             for k in range(1, blocks):
                 pairs = [(j, j ^ k) for j in range(tiles)]
                 pieces[k] = lax.ppermute(pieces[k], "tile", pairs)
+            patches[frame_no] = patches_of(frame_no, turns[frame_no])
             later = [grad_cells] + pieces
 
-    hidden, cells, parcels[0] = lax.optimization_barrier((hidden, cells, parcels[0]))
-    final = jnp.stack([hidden, cells]).reshape(2, blocks, tile_rows * columns, width)
-    final = lax.all_to_all(final.transpose(1, 0, 2, 3), "tile", 0, 0, axis_index_groups=groups)
-    final = final.transpose(1, 2, 0, 3).reshape(2, 1, 1, tile_rows, columns, hidden_dim)
-
-    pieces = [None] * frames
-    for frame_no in reversed(range(frames)):
-        got = all_tiles(parcels[frame_no])
-        if frame_no > 0:
-            patches[frame_no] = patches_of(frame_no, got, pixels // width)
-        pieces[frame_no] = [g[:, :pixels] for g in got]
-
-    def block_gradient(k):
-        grad = None
-        for frame_no in reversed(range(frames)):
-            if slabs == 1:
-                piece = pieces[frame_no][k]
-            else:
-                piece = [pieces[frame_no][s * blocks + k] for s in range(slabs)]
-                piece = jnp.stack(piece, axis=1)
-            part = jnp.dot(
-                patches[frame_no], piece.reshape(owners * image, gate), preferred_element_type=F32
-            )
-            grad = part if grad is None else grad + part
-        return grad
-
-    grads = [block_gradient(k) for k in range(blocks)]
-    own_grad = grads[0]
-    if slabs > 1:
-        for b in range(1, blocks):
-            own_grad = jnp.where(block == b, grads[b], own_grad)
-    square = jnp.sum(own_grad * own_grad) * (slab == 0).astype(F32)
-
+    own_grad = jnp.zeros((8, gate), F32)
+    if slabs == 1:
+        for frame_no in reversed(range(1, frames)):
+            part = patch_gradient(patches[frame_no], [parcels[frame_no]])[0]
+            own_grad = part if frame_no == frames - 1 else own_grad + part
+    echo = after(echo, own_grad)
     lift_kernel = weight[:, :hidden_dim]
     echoes = echo.reshape(2, ONES_ROW, gate)[:, :TAPS]
     lift_grads = sum(
@@ -676,6 +823,19 @@
         for part in split_low(echoes)
     )
 
+    pieces = [None] + [all_tiles(p, [own_grad, lift_grads]) for p in parcels[1:]]
+
+    states = after(jnp.stack([hidden, cells]), own_grad)
+    states = states.reshape(2, blocks, tile_rows * columns, width)
+    final = []
+    for k in range(blocks):
+        part = lax.dynamic_slice_in_dim(states, jnp.bitwise_xor(block, k), 1, 1)
+        if k:
+            part = lax.ppermute(part, "tile", [(j, j ^ k) for j in range(tiles)])
+        final.append(part)
+    final = jnp.concatenate(final, axis=1)
+    final = jnp.take(final, jnp.bitwise_xor(jnp.arange(blocks), block), axis=1)
+    final = final.transpose(0, 2, 1, 3).reshape(2, 1, 1, tile_rows, columns, hidden_dim)
     once = (block == 0).astype(F32)
     norm_part = jnp.zeros((2, 4, hidden_dim), F32)
     norm_part = lax.dynamic_update_slice_in_dim(
@@ -690,48 +850,57 @@
             lift_grads.reshape(-1),
             head_part,
             jnp.sum(rows_sum[:2], axis=1) * once,
-            jnp.reshape(square, (1,)),
         ]
     )
-    total = jnp.sum(spread(packed, ("dp", "tile")), axis=0)
-    grad_norms = total[: 2 * gate_dim].reshape(2, 1, gate_dim)
-    grad_ends = total[2 * gate_dim : 2 * gate_dim + 3 * hidden_dim].reshape(3, hidden_dim)
-    grad_head = total[-3:-2]
-    loss_sum = total[-2]
-    kernel_square = total[-1]
-
-    squares = (
-        kernel_square
-        + jnp.sum(grad_norms * grad_norms)
-        + jnp.sum(grad_ends * grad_ends)
-        + jnp.sum(grad_head * grad_head)
-    )
-    grad_norm = jnp.sqrt(squares)
-    factor = clip_limit / jnp.maximum(grad_norm, clip_limit)
+    lanes = 2 * GROUP_SIZE
+    packed = jnp.pad(packed, (0, -packed.shape[0] % lanes)).reshape(-1, lanes)
+    devices = owners * tiles
+    if slabs == 1:
+        own_grad, square = patch_gradient(patches[0], [parcels[0]], own_grad, waits=[final])
+        packed = jnp.broadcast_to(jnp.concatenate([packed, square])[None], (devices, packed.shape[0] + 1, lanes))
+        bases = [0.0] * (blocks - 1)
+        for frame_no in reversed(range(1, frames)):
+            got = patch_gradient(patches[frame_no], pieces[frame_no][1:], waits=[packed])
+            bases = [b + g for b, g in zip(bases, got)]
+        everyone = lax.all_to_all(packed, ("dp", "tile"), 0, 0)
+        pieces[0] = all_tiles(parcels[0], [everyone] + bases)
+        bases, late = [own_grad] + bases, [patches[0]] + pieces[0][1:]
+    else:
+        pieces[0] = all_tiles(parcels[0])
+        bases, late = [], []
+        for b in range(blocks):
+            grad = 0.0
+            for frame_no in range(frames):
+                piece = [pieces[frame_no][s * blocks + b] for s in range(slabs)]
+                piece = jnp.stack(piece, axis=1).reshape(owners * image, gate)
+                grad = grad + jnp.dot(patches[frame_no], piece, preferred_element_type=F32)
+            bases.append(grad)
+        own_grad = bases[0]
+        for b in range(1, blocks):
+            own_grad = jnp.where(block == b, bases[b], own_grad)
+        square = jnp.sum(own_grad * own_grad, axis=0, keepdims=True) * (slab == 0).astype(F32)
+        square = square[:, : 2 * GROUP_SIZE] + square[:, 2 * GROUP_SIZE :]
+        packed = jnp.broadcast_to(jnp.concatenate([packed, square])[None], (devices, packed.shape[0] + 1, lanes))
+        everyone = lax.all_to_all(packed, ("dp", "tile"), 0, 0)
     correction = 1.0 - jnp.power(0.5, step_count[0].astype(F32))
     kernel_rate = (TAPS * IN_DIM) ** (-0.5)
-    kern_out = kernel_update(
+    heads = [h.reshape(1, 1) for h in (head_bias, head_moment, head_second)]
+    smalls = [norm_params, norm_moment, norm_second, end_params, end_moment, end_second] + heads
+    out = last_update(
         me,
-        jnp.stack([factor, correction]),
-        grads,
-        kernels[0],
-        kernel_moment[0],
-        kernel_second[0],
+        jnp.stack([correction, count]),
+        everyone,
+        smalls,
+        bases,
+        late,
+        (kernels[0], kernel_moment[0], kernel_second[0]),
         kernel_rate,
     )
-    norm_out = adamw(
-        norm_params, norm_moment, norm_second, grad_norms * factor, small_rate, correction
-    )
-    end_out = adamw(end_params, end_moment, end_second, grad_ends * factor, small_rate, correction)
-    head_out = adamw(
-        head_bias, head_moment, head_second, grad_head * factor, small_rate, correction
-    )
     return (
-        (loss_sum / count, grad_norm)
-        + tuple(k[None] for k in kern_out)
-        + norm_out
-        + end_out
-        + head_out
+        (out[3].reshape(()), out[4].reshape(()))
+        + tuple(k[None] for k in out[:3])
+        + tuple(out[5:11])
+        + tuple(h.reshape(1) for h in out[11:14])
         + (final[0], final[1])
     )
 

time: 372 us -> 299 us (0.80)
  matrix products: 45.7 us -> 5.89 us
  waiting for transfers between devices: 119 us -> 80.1 us
  Pallas kernels: 73.2 us -> 94.2 us
  between operations: 29.9 us -> 18.9 us
  local copies, waits for them, and re-layouts: 34.4 us -> 27.8 us
  starting transfers between devices: 38.6 us -> 43.2 us
    dot_general x8 -> x0, matrix products: 39.9 us -> none  [block_gradient(): jnp.dot(patches[frame_no], piece.reshape(owners * image, gate), preferred...]
    all_to_all x5 -> x2, waiting for transfers between devices: 44.9 us -> 18.8 us  [spread(): return lax.all_to_all(jnp.broadcast_to(x[None], (n,) + x.shape), axes, 0, 0)]
    pallas_call x1 -> x8, Pallas kernels: 19.5 us -> 45.3 us  [the longest x1 25 us: last_update(): pl.pallas_call(body, out_shape=tuple([shape((own, gate_dim), F32)] * 3 +...]
    all_to_all x1 -> x4, waiting for transfers between devices: 27.2 us -> 9.79 us  [the longest x1 5.2 us: per_device(): everyone = lax.all_to_all(packed, ('dp', 'tile'), 0, 0)]
    all_to_all x1 -> x4, starting transfers between devices: 3.33 us -> 18.3 us  [the longest x2 9.58 us: per_device(): parcels[frame_no] = lax.all_to_all(lows, 'dp', 0, 0)]
    all_to_all x5 -> x2, starting transfers between devices: 24.8 us -> 10.7 us  [spread(): return lax.all_to_all(jnp.broadcast_to(x[None], (n,) + x.shape), axes, 0, 0)]
    slice x8 -> x0, local copies, waits for them, and re-layouts: 7.71 us -> none  [the longest x4 5.72 us: per_device(): pieces[frame_no] = [g[:, :pixels] for g in got]]
    broadcast_in_dim x5 -> x2, local copies, waits for them, and re-layouts: 4.91 us -> 0.77 us  [spread(): return lax.all_to_all(jnp.broadcast_to(x[None], (n,) + x.shape), axes, 0, 0)]
  transfers between devices with their start and end apart: 20 -> 26, of which waited for: 10 -> 13; matrix products, arithmetic and copies ran while one was open for 19% -> 12% of each run, Pallas kernels for 5% -> 18%
where the time goes in v2:
time: 299 us; the launch traced here: 296 us
  Pallas kernels  94.2 us (32%)
  waiting for transfers between devices  80.1 us (27%)
  starting transfers between devices  43.2 us (14%)
  local copies, waits for them, and re-layouts  27.8 us (9%)
  between operations  18.9 us (6%)
  blocking collectives  16.6 us (6%)
  other arithmetic  9.57 us (3%)
  matrix products  5.89 us (2%)
    all_gather x1, waiting for transfers between devices, per_device(): lax.all_gather(own_kernel_columns(kernels[0], block), 'dp', axis=0, tiled...  38.9 us
    pallas_call x1, Pallas kernels, last_update(): pl.pallas_call(body, out_shape=tuple([shape((own, gate_dim), F32)] * 3 +...  25 us
    pallas_call x3, Pallas kernels, patch_gradient(): pl.pallas_call(body, out_shape=tuple(outs), grid=(own // step,), in_specs...  20.3 us
    all_to_all x2, waiting for transfers between devices, spread(): return lax.all_to_all(jnp.broadcast_to(x[None], (n,) + x.shape), axes, 0, 0)  18.8 us
    pallas_call x2, Pallas kernels, owned_patches(): pl.pallas_call(body, out_shape=shape((own, owners * image), BF), grid_spe...  18 us
    pallas_call x2, Pallas kernels, forward_frame(): pl.pallas_call(body, out_shape=outs, grid_spec=pltpu.PrefetchScalarGridSp...  14 us
    all_gather x2, blocking collectives, whole_hidden(): got = lax.all_gather(values, 'tile').reshape(slabs, blocks, pixels, width)  11.5 us
    all_to_all x2, starting transfers between devices, spread(): return lax.all_to_all(jnp.broadcast_to(x[None], (n,) + x.shape), axes, 0, 0)  10.7 us
  transfers between devices with their start and end apart: 26, of which 13 were waited for; matrix products, arithmetic and copies ran while one was open for 12% of the time, Pallas kernels for 18%

profile of v2, /device:TPU:0, one launch (start us, length us, event | category | flops | bytes accessed | tf_op | source)
XLA Modules:
  0.0 296.3 jit_solution(4062758767934760125)
XLA Ops:
  7.9 3.8 %columns.1 = bf16[1600,256]{1,0:T(8,128)(2,1)} custom-call(s32[2]{0:T(128)} %pad_add_fusion.place, f32[1600,1024]{1,0:T(8,128)} %bitcast.157, f32[1600,1024]{1,0:T(8,128)} %bitcast.158, f32[1600,1024]{1,0:T(8,128)} %bitcast.159, f32[1600,1024]{1,0:T(8,128)} %bitcast.160), custom_call_target="tpu_custom_call" | custom-call | tf_op jit(solution)/shard_map/columns/pallas_call | solution.py:85
  13.4 7.3 %all-to-all-start = ((f32[32,1,384]{2,1,0:T(1,128)}), f32[32,1,384]{2,1,0:T(1,128)S(1)}, u32[]{:S(2)}, u32[]{:S(2)}) async-start(f32[32,1,384]{2,1,0:T(1,128)} %reshape.248), calls=%async_computation | async-start | bytes 98304 | tf_op jit(solution)/shard_map/all_to_all | solution.py:27
  23.6 0.8 reshape.250
  25.1 2.9 all-to-all-done
  28.1 3.3 %all-to-all-start.1 = ((f32[4,1,8192]{2,1,0:T(1,128)}), f32[4,1,8192]{2,1,0:T(1,128)S(1)}, u32[]{:S(2)}, u32[]{:S(2)}) async-start(f32[4,1,8192]{2,1,0:T(1,128)} %reshape.250), calls=%async_computation.1 | async-start | bytes 262144 | tf_op jit(solution)/shard_map/all_to_all | solution.py:722
  36.0 1.0 reduce.3
  38.0 3.4 %all-to-all-start.2 = ((bf16[8,64,256]{2,1,0:T(8,128)(2,1)}), bf16[8,64,256]{2,1,0:T(8,128)(2,1)S(1)}, u32[]{:S(2)}, u32[]{:S(2)}) async-start(bf16[8,64,256]{2,1,0:T(8,128)(2,1)} %broadcast_in_dim.55), calls=%async_computation.2 | async-start | bytes 524288 | tf_op jit(solution)/shard_map/all_to_all | solution.py:27
  42.2 15.9 %all-to-all-done.2.refs_3_ = bf16[8,64,256]{2,1,0:T(8,128)(2,1)S(1)} async-done(((bf16[8,64,256]{2,1,0:T(8,128)(2,1)}), bf16[8,64,256]{2,1,0:T(8,128)(2,1)S(1)}, u32[]{:S(2)}, u32[]{:S(2)}) %all-to-all-start.2) | async-done | bytes 262176 | tf_op jit(solution)/shard_map/all_to_all | solution.py:27
  58.1 1.5 collective-permute-start.1
  61.4 4.7 %collective-permute-done.1.refs_5_ = bf16[8,64,256]{2,1,0:T(8,128)(2,1)S(1)} collective-permute-done((bf16[8,64,256]{2,1,0:T(8,128)(2,1)S(1)}, bf16[8,64,256]{2,1,0:T(8,128)(2,1)S(1)}, u32[]{:S(2)}, u32[]{:S(2)}) %collective-permute-start.1) | collective-permute-done | bytes 262176 | tf_op jit(solution)/shard_map/ppermute | solution.py:702
  67.0 5.5 %all_gather.19 = bf16[4,256,64]{1,2,0:T(8,128)(2,1)S(1)} all-gather(bf16[1,256,64]{1,2,0:T(8,128)(2,1)S(1)} %copy.103), channel_id=1, replica_groups=mesh['tile'=4,'dp'=8] {'tile'}, dimensions={0}, use_global_device_ids=true | all-gather | bytes 163840 | tf_op jit(solution)/shard_map/all_gather | solution.py:730
  74.0 9.1 %owned_patches.2.refs_0_.refs_16_ = bf16[1600,2048]{1,0:T(8,128)(2,1)} custom-call(s32[10]{0:T(128)} %stack.97.refs_0_, f32[8,1,256]{2,1,0:T(1,128)} %reshape_squeeze.16.refs_1_, f32[256,2]{1,0:T(8,128)} %bitcast.185, bf16[8,64,256]{2,1,0:T(8,128)(2,1)} %copy-done.7, bf16[8,64,256]{2,1,0:T(8,128)(2,1)} %copy-done.26, bf16[8,64,256]{2,1,0:T(8,128)(2,1)} %copy-done.24, ...), custom_call_target="tpu_custom_call" | custom-call | flops 3150000128 | bytes 9450000 | tf_op jit(solution)/shard_map/owned_patches/pallas_call | solution.py:422
  83.1 38.9 %all-gather.5.cloned.1.call-done = bf16[12800,256]{1,0:T(8,128)(2,1)} async-done(((bf16[1600,256]{1,0:T(8,128)(2,1)}), bf16[12800,256]{1,0:T(8,128)(2,1)}) %all-gather.5.cloned.1.call-update) | async-done | bytes 6553616 | tf_op jit(solution)/shard_map/all_gather | solution.py:668
  122.7 7.0 %forward_frame.2 = (f32[256,256]{1,0:T(8,128)}, f32[256,64]{1,0:T(8,128)}, f32[256,64]{1,0:T(8,128)}, bf16[256,64]{1,0:T(8,128)(2,1)}, bf16[8,64,256]{2,1,0:T(8,128)(2,1)}, /*index=5*/f32[1,256]{1,0:T(1,128)}) custom-call(s32[1]{0:T(128)} %bitcast.4.refs_0_, f32[256,1]{1,0:T(8,128)} %copy.106.refs_1_, bf16[256,256]{1,0:T(8,128)(2,1)} %copy.107.refs_2_, ...), custom_call_target="tpu_custom_call" | custom-call | flops 1400000000 | bytes 4200000 | tf_op jit(solution)/shard_map/forward_frame/pallas_call | solution.py:190
  129.7 3.4 %all-to-all-start.3 = ((bf16[8,64,256]{2,1,0:T(8,128)(2,1)}), bf16[8,64,256]{2,1,0:T(8,128)(2,1)S(1)}, u32[]{:S(2)}, u32[]{:S(2)}) async-start(bf16[8,64,256]{2,1,0:T(8,128)(2,1)} %get-tuple-element.68), calls=%async_computation.3 | async-start | bytes 524288 | tf_op jit(solution)/shard_map/all_to_all | solution.py:745
  136.4 6.0 %all-gather = bf16[1024,64]{1,0:T(8,128)(2,1)S(1)} all-gather(bf16[256,64]{1,0:T(8,128)(2,1)} %get-tuple-element.65), channel_id=2, replica_groups=mesh['tile'=4,'dp'=8] {'tile'}, dimensions={0}, use_global_device_ids=true | all-gather | bytes 163840 | tf_op jit(solution)/shard_map/all_gather | solution.py:730
  143.3 7.0 %forward_frame.3 = (f32[256,256]{1,0:T(8,128)}, f32[256,64]{1,0:T(8,128)}, f32[256,64]{1,0:T(8,128)}, bf16[256,64]{1,0:T(8,128)(2,1)}, bf16[8,64,256]{2,1,0:T(8,128)(2,1)}, /*index=5*/f32[1,256]{1,0:T(1,128)}) custom-call(s32[1]{0:T(128)} %bitcast.4.refs_0_, f32[256,1]{1,0:T(8,128)} %copy.110.refs_1_, bf16[256,256]{1,0:T(8,128)(2,1)} %copy.111.refs_2_, ...), custom_call_target="tpu_custom_call" | custom-call | flops 1400000000 | bytes 4200000 | tf_op jit(solution)/shard_map/forward_frame/pallas_call | solution.py:190
  151.0 5.2 %all-gather.2 = f32[4,2,256]{2,1,0:T(2,128)S(1)} all-gather(f32[1,2,256]{2,1,0:T(2,128)S(1)} %maximum_bitcast_fusion.1), channel_id=3, replica_groups=mesh['tile'=4,'dp'=8] {'tile'}, dimensions={0}, use_global_device_ids=true | all-gather | bytes 10240 | tf_op jit(solution)/shard_map/all_gather | solution.py:746
  156.8 4.0 %backward_cell.2 = (bf16[8,256,256]{2,1,0:T(8,128)(2,1)}, f32[256,64]{1,0:T(8,128)}, f32[8,256]{1,0:T(8,128)}, f32[64,256]{1,0:T(8,128)}, f32[8,256]{1,0:T(8,128)}, /*index=5*/f32[8,64]{1,0:T(8,128)}) custom-call(f32[2]{0:T(128)} %pad_maximum_fusion.5.refs_0_, f32[4,256]{1,0:T(4,128)} %get-tuple-element.150.refs_1_, f32[1,256]{1,0:T(1,128)} %get-tuple-element.122.refs_2_, ...), custom_call_target="tpu_custom_call" | custom-call | flops 1400000000 | bytes 4200000 | tf_op jit(solution)/shard_map/backward_cell/pallas_call | solution.py:289
  160.9 5.9 %all-to-all-start.4 = ((bf16[8,256,256]{2,1,0:T(8,128)(2,1)}), bf16[8,256,256]{2,1,0:T(8,128)(2,1)}, u32[]{:S(2)}, u32[]{:S(2)}) async-start(bf16[8,256,256]{2,1,0:T(8,128)(2,1)} %get-tuple-element.74.refs_0_), calls=%async_computation.4 | async-start | bytes 2097152 | tf_op jit(solution)/shard_map/all_to_all | solution.py:790
  168.2 4.8 %hidden_gradient.1 = (f32[256,64]{1,0:T(8,128)}, f32[256,64]{1,0:T(8,128)}, f32[256,64]{1,0:T(8,128)}, f32[256,64]{1,0:T(8,128)}) custom-call(s32[1]{0:T(128)} %bitcast.me_ref.refs_0_, bf16[8,256,256]{2,1,0:T(8,128)(2,1)} %get-tuple-element.74.refs_0_, bf16[25,2,256,256]{3,2,1,0:T(8,128)(2,1)} %bitcast.164), custom_call_target="tpu_custom_call" | custom-call | flops 1400000000 | bytes 4200000 | tf_op jit(solution)/shard_map/hidden_gradient/pallas_call | solution.py:361
  173.1 1.5 collective-permute-start.4
  175.7 1.5 collective-permute-start.7
  177.2 2.5 collective-permute-done.4.refs_12_
  179.7 1.9 collective-permute-done.5.refs_13_
  182.3 4.2 %backward_cell.3 = (bf16[8,256,256]{2,1,0:T(8,128)(2,1)}, f32[256,64]{1,0:T(8,128)}, f32[8,256]{1,0:T(8,128)}, f32[64,256]{1,0:T(8,128)}, f32[8,256]{1,0:T(8,128)}, /*index=5*/f32[8,64]{1,0:T(8,128)}) custom-call(f32[2]{0:T(128)} %pad_maximum_fusion.5.refs_0_, f32[4,256]{1,0:T(4,128)} %get-tuple-element.151.refs_1_, f32[1,256]{1,0:T(1,128)} %get-tuple-element.121.refs_2_, ...), custom_call_target="tpu_custom_call" | custom-call | flops 1400000000 | bytes 4200000 | tf_op jit(solution)/shard_map/backward_cell/pallas_call | solution.py:289
  186.5 0.9 fusion.15
  187.6 1.0 collective-permute-start.8
  188.6 4.6 %all-to-all-done.4.refs_1_ = bf16[8,256,256]{2,1,0:T(8,128)(2,1)} async-done(((bf16[8,256,256]{2,1,0:T(8,128)(2,1)}), bf16[8,256,256]{2,1,0:T(8,128)(2,1)}, u32[]{:S(2)}, u32[]{:S(2)}) %all-to-all-start.4) | async-done | bytes 1048608 | tf_op jit(solution)/shard_map/all_to_all | solution.py:790
  193.2 3.6 %all-to-all-start.5 = ((bf16[8,256,256]{2,1,0:T(8,128)(2,1)}), bf16[8,256,256]{2,1,0:T(8,128)(2,1)S(1)}, u32[]{:S(2)}, u32[]{:S(2)}) async-start(bf16[8,256,256]{2,1,0:T(8,128)(2,1)} %get-tuple-element.88), calls=%async_computation.5 | async-start | bytes 2097152 | tf_op jit(solution)/shard_map/all_to_all | solution.py:790
  197.8 1.5 add.119.refs_0_
  199.3 1.5 collective-permute-start.13
  202.2 8.9 %owned_patches.3.refs_0_ = bf16[1600,2048]{1,0:T(8,128)(2,1)} custom-call(s32[10]{0:T(128)} %stack.97.refs_0_, f32[8,1,256]{2,1,0:T(1,128)} %reshape_squeeze.19.refs_1_, f32[256,2]{1,0:T(8,128)} %bitcast.186, bf16[8,64,256]{2,1,0:T(8,128)(2,1)} %copy-done.6, bf16[8,64,256]{2,1,0:T(8,128)(2,1)} %copy-done.23, bf16[8,64,256]{2,1,0:T(8,128)(2,1)} %copy-done.22, ...), custom_call_target="tpu_custom_call" | custom-call | flops 3150000128 | bytes 9450000 | tf_op jit(solution)/shard_map/owned_patches/pallas_call | solution.py:422
  211.1 5.1 %patch_gradient.3.refs_1_.refs_2_ = f32[1600,256]{1,0:T(8,128)} custom-call(bf16[1600,2048]{1,0:T(8,128)(2,1)} %owned_patches.3.refs_0_, bf16[8,256,256]{2,1,0:T(8,128)(2,1)} %all-to-all-done.4.refs_1_), custom_call_target="tpu_custom_call" | custom-call | flops 1750000000 | bytes 5250000 | tf_op jit(solution)/shard_map/patch_gradient/pallas_call | solution.py:503
  216.2 2.9 fusion.7
  219.2 3.0 %fusion.10.refs_2_ = f32[2,256]{1,0:T(2,128)S(1)} fusion(f32[2,256]{1,0:T(2,128)S(1)} %fusion.7, bf16[25,512,256]{2,1,0:T(8,128)(2,1)} %bitcast.166, f32[2,25,256]{2,1,0:T(8,128)} %bitcast.177), kind=kOutput, calls=%fused_computation.7 | convolution fusion | flops 6554112 | bytes 3346432 | tf_op jit(solution)/shard_map/ktg,tcg->kc/dot_general | solution.py:822
  222.3 1.3 collective-permute-start.10
  224.6 1.0 copy-done.4
  225.7 1.0 collective-permute-done.11
  226.7 1.2 collective-permute-done.10
  228.5 1.0 collective-permute-start.16
  229.8 0.9 reshape.222.refs_3_
  230.7 5.7 %patch_gradient.4 = (f32[1600,256]{1,0:T(8,128)}, f32[1,128]{1,0:T(1,128)}) custom-call(bf16[1600,2048]{1,0:T(8,128)(2,1)} %owned_patches.2.refs_0_.refs_16_, bf16[8,256,256]{2,1,0:T(8,128)(2,1)} %copy-done.1, f32[1600,256]{1,0:T(8,128)} %patch_gradient.3.refs_1_.refs_2_, f32[2,1,1,2,32,256]{5,4,3,2,1,0:T(8,128)} %reshape.222.refs_3_), custom_call_target="tpu_custom_call" | custom-call | flops 1750000000 | bytes 5250000 | tf_op jit(solution)/shard_map/patch_gradient/pallas_call | solution.py:503
  237.8 5.3 %all-to-all-start.6 = ((f32[32,24,128]{2,1,0:T(8,128)}), f32[32,24,128]{2,1,0:T(8,128)S(1)}, u32[]{:S(2)}, u32[]{:S(2)}) async-start(f32[32,24,128]{2,1,0:T(8,128)} %broadcast_in_dim.61.refs_4_), calls=%async_computation.6 | async-start | bytes 786432 | tf_op jit(solution)/shard_map/all_to_all | solution.py:865
  243.2 9.5 %patch_gradient.5 = (f32[1600,256]{1,0:T(8,128)}, f32[1600,256]{1,0:T(8,128)}, f32[1600,256]{1,0:T(8,128)}) custom-call(bf16[1600,2048]{1,0:T(8,128)(2,1)} %owned_patches.3.refs_0_, bf16[8,256,256]{2,1,0:T(8,128)(2,1)} %collective-permute-done.12.refs_1_, bf16[8,256,256]{2,1,0:T(8,128)(2,1)} %after.6.refs_2_, ...), custom_call_target="tpu_custom_call" | custom-call | flops 3150000128 | bytes 9450000 | tf_op jit(solution)/shard_map/patch_gradient/pallas_call | solution.py:503
  252.6 5.2 %all-to-all-done.6.refs_1_.refs_2_ = f32[32,24,128]{2,1,0:T(8,128)S(1)} async-done(((f32[32,24,128]{2,1,0:T(8,128)}), f32[32,24,128]{2,1,0:T(8,128)S(1)}, u32[]{:S(2)}, u32[]{:S(2)}) %all-to-all-start.6) | async-done | bytes 393248 | tf_op jit(solution)/shard_map/all_to_all | solution.py:865
  263.4 1.0 copy-done.5
  264.4 25.0 %last_update.1 = (f32[1600,1024]{1,0:T(8,128)}, f32[1600,1024]{1,0:T(8,128)}, f32[1600,1024]{1,0:T(8,128)}, f32[1,1]{1,0:T(1,128)}, f32[1,1]{1,0:T(1,128)}, /*in...) custom-call(s32[1]{0:T(128)} %bitcast.me_ref.refs_0_, ...), custom_call_target="tpu_custom_call" | custom-call | flops 7699999744 | bytes 23100000 | tf_op jit(solution)/shard_map/last_update/pallas_call | solution.py:598
  (223 shorter events, 33.2 us)
Async XLA Ops:
  7.2 114.9 %all-gather.5.cloned.1.call-start = ((), (), s32[]{:S(2)}) async-start(), calls=%async_computation.7 | async-start | bytes 7372800 | tf_op jit(solution)/shard_map/all_gather | solution.py:668
  7.9 4.5 %copy-start.18 = (s32[1,2,2,32]{3,2,1,0:T(2,128)S(1)}, s32[1,2,2,32]{3,2,1,0:T(2,128)}, u32[]{:S(2)}) copy-start(s32[1,2,2,32]{3,2,1,0:T(2,128)} %param.21) | copy-start | bytes 1540
  7.9 4.6 %copy-start.19 = (f32[1,2,2,32]{3,2,1,0:T(2,128)S(1)}, f32[1,2,2,32]{3,2,1,0:T(2,128)}, u32[]{:S(2)}) copy-start(f32[1,2,2,32]{3,2,1,0:T(2,128)} %param.20) | copy-start | bytes 1540
  7.9 4.6 %copy-start.20 = (f32[1,2,2,32]{3,2,1,0:T(2,128)S(1)}, f32[1,2,2,32]{3,2,1,0:T(2,128)}, u32[]{:S(2)}) copy-start(f32[1,2,2,32]{3,2,1,0:T(2,128)} %param.19) | copy-start | bytes 1540
  7.9 13.0 %copy-start.16 = (f32[3,256]{1,0:T(4,128)S(1)}, f32[3,256]{1,0:T(4,128)}, u32[]{:S(2)}) copy-start(f32[3,256]{1,0:T(4,128)} %refs_6_.1) | copy-start | bytes 9220
  7.9 13.8 %copy-start.14 = (f32[2,1,1024]{2,1,0:T(1,128)S(1)}, f32[2,1,1024]{2,1,0:T(1,128)}, u32[]{:S(2)}) copy-start(f32[2,1,1024]{2,1,0:T(1,128)} %refs_3_.1) | copy-start | bytes 24580
  7.9 15.4 %copy-start.10 = (f32[1,1,2,32,256]{4,3,2,1,0:T(8,128)S(1)}, f32[1,1,2,32,256]{4,3,2,1,0:T(8,128)}, u32[]{:S(2)}) copy-start(f32[1,1,2,32,256]{4,3,2,1,0:T(8,128)} %param.36) | copy-start | bytes 196612
  7.9 15.5 %copy-start.11 = (f32[1,1,2,32,256]{4,3,2,1,0:T(8,128)S(1)}, f32[1,1,2,32,256]{4,3,2,1,0:T(8,128)}, u32[]{:S(2)}) copy-start(f32[1,1,2,32,256]{4,3,2,1,0:T(8,128)} %param.37) | copy-start | bytes 196612
  13.4 14.7 %all-to-all-start = ((f32[32,1,384]{2,1,0:T(1,128)}), f32[32,1,384]{2,1,0:T(1,128)S(1)}, u32[]{:S(2)}, u32[]{:S(2)}) async-start(f32[32,1,384]{2,1,0:T(1,128)} %reshape.248), calls=%async_computation | async-start | bytes 98304 | tf_op jit(solution)/shard_map/all_to_all | solution.py:27
  20.9 62.3 %copy-start.13 = (f32[2,256]{1,0:T(2,128)}, f32[2,256]{1,0:T(2,128)S(1)}, u32[]{:S(2)}) copy-start(f32[2,256]{1,0:T(2,128)S(1)} %slice.164.refs_3_) | copy-start | bytes 6148
  28.1 7.9 %all-to-all-start.1 = ((f32[4,1,8192]{2,1,0:T(1,128)}), f32[4,1,8192]{2,1,0:T(1,128)S(1)}, u32[]{:S(2)}, u32[]{:S(2)}) async-start(f32[4,1,8192]{2,1,0:T(1,128)} %reshape.250), calls=%async_computation.1 | async-start | bytes 262144 | tf_op jit(solution)/shard_map/all_to_all | solution.py:722
  38.0 20.1 %all-to-all-start.2 = ((bf16[8,64,256]{2,1,0:T(8,128)(2,1)}), bf16[8,64,256]{2,1,0:T(8,128)(2,1)S(1)}, u32[]{:S(2)}, u32[]{:S(2)}) async-start(bf16[8,64,256]{2,1,0:T(8,128)(2,1)} %broadcast_in_dim.55), calls=%async_computation.2 | async-start | bytes 524288 | tf_op jit(solution)/shard_map/all_to_all | solution.py:27
  58.1 15.2 %copy-start.7 = (bf16[8,64,256]{2,1,0:T(8,128)(2,1)}, bf16[8,64,256]{2,1,0:T(8,128)(2,1)S(1)}, u32[]{:S(2)}) copy-start(bf16[8,64,256]{2,1,0:T(8,128)(2,1)S(1)} %all-to-all-done.2.refs_3_) | copy-start | bytes 786436
  58.1 8.1 %collective-permute-start.1 = (bf16[8,64,256]{2,1,0:T(8,128)(2,1)S(1)}, bf16[8,64,256]{2,1,0:T(8,128)(2,1)S(1)}, u32[]{:S(2)}, u32[]{:S(2)}) collective-permute-start(bf16[8,64,256]{2,1,0:T(8,128)(2,1)S(1)} %all-to-all-done.2.refs_3_), channel_id=1, source_target_pairs={{0,16},{8,24},{16,0},{24,8},{1,17},{9,25},{17,1},{25,9},{2,18},{10... | collective-permute-start | bytes 786440 | tf_op jit(solution)/shard_map/ppermute | solution.py:702
  61.3 11.9 %collective-permute-start = (bf16[8,64,256]{2,1,0:T(8,128)(2,1)S(1)}, bf16[8,64,256]{2,1,0:T(8,128)(2,1)S(1)}, u32[]{:S(2)}, u32[]{:S(2)}) collective-permute-start(bf16[8,64,256]{2,1,0:T(8,128)(2,1)S(1)} %all-to-all-done.2.refs_3_), channel_id=1, source_target_pairs={{0,8},{8,0},{16,24},{24,16},{1,9},{9,1},{17,25},{25,17},{2,10},{10... | collective-permute-start | bytes 786440 | tf_op jit(solution)/shard_map/ppermute | solution.py:702
  66.1 7.1 %copy-start.24 = (bf16[8,64,256]{2,1,0:T(8,128)(2,1)}, bf16[8,64,256]{2,1,0:T(8,128)(2,1)S(1)}, u32[]{:S(2)}) copy-start(bf16[8,64,256]{2,1,0:T(8,128)(2,1)S(1)} %collective-permute-done.1.refs_5_) | copy-start | bytes 786436
  66.1 7.1 %collective-permute-start.2 = (bf16[8,64,256]{2,1,0:T(8,128)(2,1)S(1)}, bf16[8,64,256]{2,1,0:T(8,128)(2,1)S(1)}, u32[]{:S(2)}, u32[]{:S(2)}) collective-permute-start(bf16[8,64,256]{2,1,0:T(8,128)(2,1)S(1)} %collective-permute-done.1.refs_5_), channel_id=1, source_target_pairs={{0,8},{8,0},{16,24},{24,16},{1,9},{9,1},{17,25},{25,17},{2,10},{10... | collective-permute-start | bytes 786440 | tf_op jit(solution)/shard_map/ppermute | solution.py:702
  129.7 20.6 %copy-start.21 = (f32[1,256]{1,0:T(1,128)S(1)}, f32[1,256]{1,0:T(1,128)}, u32[]{:S(2)}) copy-start(f32[1,256]{1,0:T(1,128)} %get-tuple-element.64) | copy-start | bytes 3076
  129.7 26.5 %all-to-all-start.3 = ((bf16[8,64,256]{2,1,0:T(8,128)(2,1)}), bf16[8,64,256]{2,1,0:T(8,128)(2,1)S(1)}, u32[]{:S(2)}, u32[]{:S(2)}) async-start(bf16[8,64,256]{2,1,0:T(8,128)(2,1)} %get-tuple-element.68), calls=%async_computation.3 | async-start | bytes 524288 | tf_op jit(solution)/shard_map/all_to_all | solution.py:745
  156.2 21.0 %copy-start.6 = (bf16[8,64,256]{2,1,0:T(8,128)(2,1)}, bf16[8,64,256]{2,1,0:T(8,128)(2,1)S(1)}, u32[]{:S(2)}) copy-start(bf16[8,64,256]{2,1,0:T(8,128)(2,1)S(1)} %all-to-all-done.3.refs_3_) | copy-start | bytes 786436
  156.8 18.1 %copy-start.8 = (f32[256,64]{1,0:T(8,128)S(1)}, f32[256,64]{1,0:T(8,128)}, u32[]{:S(2)}) copy-start(f32[256,64]{1,0:T(8,128)} %get-tuple-element.90) | copy-start | bytes 196612
  156.8 18.1 %copy-start.9 = (f32[256,64]{1,0:T(8,128)S(1)}, f32[256,64]{1,0:T(8,128)}, u32[]{:S(2)}) copy-start(f32[256,64]{1,0:T(8,128)} %get-tuple-element.89) | copy-start | bytes 196612
  160.9 32.3 %all-to-all-start.4 = ((bf16[8,256,256]{2,1,0:T(8,128)(2,1)}), bf16[8,256,256]{2,1,0:T(8,128)(2,1)}, u32[]{:S(2)}, u32[]{:S(2)}) async-start(bf16[8,256,256]{2,1,0:T(8,128)(2,1)} %get-tuple-element.74.refs_0_), calls=%async_computation.4 | async-start | bytes 2097152 | tf_op jit(solution)/shard_map/all_to_all | solution.py:790
  168.1 28.9 %copy-start.17 = (f32[8,64]{1,0:T(8,128)S(1)}, f32[8,64]{1,0:T(8,128)}, u32[]{:S(2)}) copy-start(f32[8,64]{1,0:T(8,128)} %get-tuple-element.83) | copy-start | bytes 6148
  168.1 29.6 %copy-start.12 = (f32[64,256]{1,0:T(8,128)S(1)}, f32[64,256]{1,0:T(8,128)}, u32[]{:S(2)}) copy-start(f32[64,256]{1,0:T(8,128)} %get-tuple-element.80) | copy-start | bytes 196612
  173.0 4.2 %collective-permute-start.3 = (f32[256,64]{1,0:T(8,128)}, f32[256,64]{1,0:T(8,128)S(1)}, u32[]{:S(2)}, u32[]{:S(2)}) collective-permute-start(f32[256,64]{1,0:T(8,128)} %get-tuple-element.76), channel_id=1, source_target_pairs={{0,8},{8,0},{16,24},{24,16},{1,9},{9,1},{17,25},{25,17},{2,10},{10... | collective-permute-start | bytes 196616 | tf_op jit(solution)/shard_map/ppermute | solution.py:809
  173.1 6.6 %collective-permute-start.4 = (f32[256,64]{1,0:T(8,128)}, f32[256,64]{1,0:T(8,128)S(1)}, u32[]{:S(2)}, u32[]{:S(2)}) collective-permute-start(f32[256,64]{1,0:T(8,128)} %get-tuple-element.77), channel_id=1, source_target_pairs={{0,16},{8,24},{16,0},{24,8},{1,17},{9,25},{17,1},{25,9},{2,18},{10... | collective-permute-start | bytes 196616 | tf_op jit(solution)/shard_map/ppermute | solution.py:809
  174.6 7.0 %collective-permute-start.5 = (f32[256,64]{1,0:T(8,128)}, f32[256,64]{1,0:T(8,128)S(1)}, u32[]{:S(2)}, u32[]{:S(2)}) collective-permute-start(f32[256,64]{1,0:T(8,128)} %get-tuple-element.78), channel_id=1, source_target_pairs={{0,24},{8,16},{16,8},{24,0},{1,25},{9,17},{17,9},{25,1},{2,26},{10... | collective-permute-start | bytes 196616 | tf_op jit(solution)/shard_map/ppermute | solution.py:809
  175.7 11.9 %collective-permute-start.7 = (bf16[8,64,256]{2,1,0:T(8,128)(2,1)S(1)}, bf16[8,64,256]{2,1,0:T(8,128)(2,1)S(1)}, u32[]{:S(2)}, u32[]{:S(2)}) collective-permute-start(bf16[8,64,256]{2,1,0:T(8,128)(2,1)S(1)} %all-to-all-done.3.refs_3_), channel_id=1, source_target_pairs={{0,16},{8,24},{16,0},{24,8},{1,17},{9,25},{17,1},{25,9},{2,18},{10... | collective-permute-start | bytes 786440 | tf_op jit(solution)/shard_map/ppermute | solution.py:702
  177.1 23.6 %collective-permute-start.6 = (bf16[8,64,256]{2,1,0:T(8,128)(2,1)S(1)}, bf16[8,64,256]{2,1,0:T(8,128)(2,1)S(1)}, u32[]{:S(2)}, u32[]{:S(2)}) collective-permute-start(bf16[8,64,256]{2,1,0:T(8,128)(2,1)S(1)} %all-to-all-done.3.refs_3_), channel_id=1, source_target_pairs={{0,8},{8,0},{16,24},{24,16},{1,9},{9,1},{17,25},{25,17},{2,10},{10... | collective-permute-start | bytes 786440 | tf_op jit(solution)/shard_map/ppermute | solution.py:702
  177.2 4.4 %copy-start.28 = (f32[256,64]{1,0:T(8,128)}, f32[256,64]{1,0:T(8,128)S(1)}, u32[]{:S(2)}) copy-start(f32[256,64]{1,0:T(8,128)S(1)} %collective-permute-done.3.refs_11_) | copy-start | bytes 196612
  179.7 1.9 copy-start.29
  187.6 13.2 %copy-start.22 = (bf16[8,64,256]{2,1,0:T(8,128)(2,1)}, bf16[8,64,256]{2,1,0:T(8,128)(2,1)S(1)}, u32[]{:S(2)}) copy-start(bf16[8,64,256]{2,1,0:T(8,128)(2,1)S(1)} %collective-permute-done.7.refs_5_) | copy-start | bytes 786436
  187.6 13.2 %collective-permute-start.8 = (bf16[8,64,256]{2,1,0:T(8,128)(2,1)S(1)}, bf16[8,64,256]{2,1,0:T(8,128)(2,1)S(1)}, u32[]{:S(2)}, u32[]{:S(2)}) collective-permute-start(bf16[8,64,256]{2,1,0:T(8,128)(2,1)S(1)} %collective-permute-done.7.refs_5_), channel_id=1, source_target_pairs={{0,8},{8,0},{16,24},{24,16},{1,9},{9,1},{17,25},{25,17},{2,10},{10... | collective-permute-start | bytes 786440 | tf_op jit(solution)/shard_map/ppermute | solution.py:702
  193.2 35.3 %all-to-all-start.5 = ((bf16[8,256,256]{2,1,0:T(8,128)(2,1)}), bf16[8,256,256]{2,1,0:T(8,128)(2,1)S(1)}, u32[]{:S(2)}, u32[]{:S(2)}) async-start(bf16[8,256,256]{2,1,0:T(8,128)(2,1)} %get-tuple-element.88), calls=%async_computation.5 | async-start | bytes 2097152 | tf_op jit(solution)/shard_map/all_to_all | solution.py:790
  199.3 25.3 %collective-permute-start.13 = (bf16[8,256,256]{2,1,0:T(8,128)(2,1)}, bf16[8,256,256]{2,1,0:T(8,128)(2,1)S(1)}, u32[]{:S(2)}, u32[]{:S(2)}) collective-permute-start(bf16[8,256,256]{2,1,0:T(8,128)(2,1)} %all-to-all-done.4.refs_1_), channel_id=1, source_target_pairs={{0,16},{8,24},{16,0},{24,8},{1,17},{9,25},{17,1},{25,9},{2,18},{10... | collective-permute-start | bytes 3145736 | tf_op jit(solution)/shard_map/ppermute | solution.py:702
  216.2 6.0 %copy-start.3 = (f32[2,256,64]{2,1,0:T(8,128)S(1)}, f32[2,256,64]{2,1,0:T(8,128)}, u32[]{:S(2)}) copy-start(f32[2,256,64]{2,1,0:T(8,128)} %after.5) | copy-start | bytes 393220
  222.1 2.5 copy-start.15
  222.2 4.5 %collective-permute-start.11 = (f32[2,1,64,64]{3,2,1,0:T(8,128)S(1)}, f32[2,1,64,64]{3,2,1,0:T(8,128)S(1)}, u32[]{:S(2)}, u32[]{:S(2)}) collective-permute-start(f32[2,1,64,64]{3,2,1,0:T(8,128)S(1)} %get-tuple-element.113), channel_id=1, source_target_pairs={{0,24},{8,16},{16,8},{24,0},{1,25},{9,17},{17,9},{25,1},{2,26},{10... | collective-permute-start | bytes 98312 | tf_op jit(solution)/shard_map/ppermute | solution.py:834
  222.3 5.6 %collective-permute-start.10 = (f32[2,1,64,64]{3,2,1,0:T(8,128)S(1)}, f32[2,1,64,64]{3,2,1,0:T(8,128)S(1)}, u32[]{:S(2)}, u32[]{:S(2)}) collective-permute-start(f32[2,1,64,64]{3,2,1,0:T(8,128)S(1)} %get-tuple-element.114), channel_id=1, source_target_pairs={{0,16},{8,24},{16,0},{24,8},{1,17},{9,25},{17,1},{25,9},{2,18},{10... | collective-permute-start | bytes 98312 | tf_op jit(solution)/shard_map/ppermute | solution.py:834
  223.6 4.2 %collective-permute-start.9 = (f32[2,1,64,64]{3,2,1,0:T(8,128)S(1)}, f32[2,1,64,64]{3,2,1,0:T(8,128)S(1)}, u32[]{:S(2)}, u32[]{:S(2)}) collective-permute-start(f32[2,1,64,64]{3,2,1,0:T(8,128)S(1)} %get-tuple-element.115), channel_id=1, source_target_pairs={{0,8},{8,0},{16,24},{24,16},{1,9},{9,1},{17,25},{25,17},{2,10},{10... | collective-permute-start | bytes 98312 | tf_op jit(solution)/shard_map/ppermute | solution.py:834
  224.2 19.0 %collective-permute-start.12 = (bf16[8,256,256]{2,1,0:T(8,128)(2,1)}, bf16[8,256,256]{2,1,0:T(8,128)(2,1)}, u32[]{:S(2)}, u32[]{:S(2)}) collective-permute-start(bf16[8,256,256]{2,1,0:T(8,128)(2,1)} %all-to-all-done.4.refs_1_), channel_id=1, source_target_pairs={{0,8},{8,0},{16,24},{24,16},{1,9},{9,1},{17,25},{25,17},{2,10},{10... | collective-permute-start | bytes 3145736 | tf_op jit(solution)/shard_map/ppermute | solution.py:702
  225.6 17.6 %collective-permute-start.14 = (bf16[8,256,256]{2,1,0:T(8,128)(2,1)}, bf16[8,256,256]{2,1,0:T(8,128)(2,1)}, u32[]{:S(2)}, u32[]{:S(2)}) collective-permute-start(bf16[8,256,256]{2,1,0:T(8,128)(2,1)} %after.6.refs_2_), channel_id=1, source_target_pairs={{0,8},{8,0},{16,24},{24,16},{1,9},{9,1},{17,25},{25,17},{2,10},{10... | collective-permute-start | bytes 3145736 | tf_op jit(solution)/shard_map/ppermute | solution.py:702
  228.5 2.2 copy-start.1
  228.5 29.3 %collective-permute-start.16 = (bf16[8,256,256]{2,1,0:T(8,128)(2,1)S(1)}, bf16[8,256,256]{2,1,0:T(8,128)(2,1)S(1)}, u32[]{:S(2)}, u32[]{:S(2)}) collective-permute-start(bf16[8,256,256]{2,1,0:T(8,128)(2,1)S(1)} %all-to-all-done.5.refs_1_), channel_id=1, source_target_pairs={{0,16},{8,24},{16,0},{24,8},{1,17},{9,25},{17,1},{25,9},{2,18},{10... | collective-permute-start | bytes 3145736 | tf_op jit(solution)/shard_map/ppermute | solution.py:702
  237.8 20.0 %all-to-all-start.6 = ((f32[32,24,128]{2,1,0:T(8,128)}), f32[32,24,128]{2,1,0:T(8,128)S(1)}, u32[]{:S(2)}, u32[]{:S(2)}) async-start(f32[32,24,128]{2,1,0:T(8,128)} %broadcast_in_dim.61.refs_4_), calls=%async_computation.6 | async-start | bytes 786432 | tf_op jit(solution)/shard_map/all_to_all | solution.py:865
  243.1 20.3 %collective-permute-start.15 = (bf16[8,256,256]{2,1,0:T(8,128)(2,1)}, bf16[8,256,256]{2,1,0:T(8,128)(2,1)}, u32[]{:S(2)}, u32[]{:S(2)}) collective-permute-start(bf16[8,256,256]{2,1,0:T(8,128)(2,1)} %copy-done.1), channel_id=1, source_target_pairs={{0,8},{8,0},{16,24},{24,16},{1,9},{9,1},{17,25},{25,17},{2,10},{10... | collective-permute-start | bytes 3145736 | tf_op jit(solution)/shard_map/ppermute | solution.py:702
  258.9 4.4 %collective-permute-start.17 = (bf16[8,256,256]{2,1,0:T(8,128)(2,1)}, bf16[8,256,256]{2,1,0:T(8,128)(2,1)S(1)}, u32[]{:S(2)}, u32[]{:S(2)}) collective-permute-start(bf16[8,256,256]{2,1,0:T(8,128)(2,1)} %after.7.refs_18_), channel_id=1, source_target_pairs={{0,8},{8,0},{16,24},{24,16},{1,9},{9,1},{17,25},{25,17},{2,10},{10... | collective-permute-start | bytes 3145736 | tf_op jit(solution)/shard_map/ppermute | solution.py:702
  (9 other events, 7.4 us)
Sparse Core Ops, SparseCore 0:
  11.9 110.1 all-gather.4

commit v3 on v2

--- a/solution.py
+++ b/solution.py
@@ -134,27 +134,78 @@
     return norm, inverse, input_gate, forget_gate, candidate, output_gate, cells
 
 
-def forward_kernel(
-    columns, first_row, obs, hid, ends, weight, cells_prev, norms, head,
-    gates_out, cells_out, hidden_out, low_out, turned_out, seen_out, bands, total, near, arrived,
-):
+def fetch_shards(parts, where, near, arrived):
+    if len(parts) == 1:
+        for k in range(KERNEL):
+            shard_row(parts[0], near, arrived, k).start()
+        return
+    rows = parts[0].shape[0]
+    for k, part in enumerate(parts):
+        @pl.when(where[k] >= 0)
+        def start():
+            begin = pl.multiple_of(where[k] * rows, 16)
+            pltpu.make_async_copy(
+                part, near.at[pl.ds(begin, rows), :], arrived.at[where[k]]
+            ).start()
+
+
+def shard_row(part, near, arrived, step):
+    depth = KERNEL * IN_DIM
+    rows = pl.ds(pl.multiple_of(step * depth, depth), depth)
+    return pltpu.make_async_copy(part.at[rows, :], near.at[rows, :], arrived.at[step])
+
+
+def await_shards(parts, near, arrived):
+    if len(parts) > 1:
+        rows = parts[0].shape[0]
+        for k in range(near.shape[0] // rows):
+            pltpu.make_async_copy(
+                parts[0], near.at[pl.ds(k * rows, rows), :], arrived.at[k]
+            ).wait()
+
+
+def await_row(parts, near, arrived, step):
+    if len(parts) == 1:
+        shard_row(parts[0], near, arrived, step).wait()
+
+
+def shard_scratch(parts):
+    rows, gate = parts[0].shape
+    count = KERNEL if len(parts) == 1 else TAPS * IN_DIM // rows
+    return [pltpu.VMEM((TAPS * IN_DIM, gate), BF), pltpu.SemaphoreType.DMA((count,))]
+
+
+def half_taps(near, step, first, depth):
+    taps = []
+    for d in range(KERNEL):
+        row = (step * KERNEL + d) * IN_DIM + first
+        taps.append(near[pl.ds(pl.multiple_of(row, 16), depth), :])
+    return jnp.concatenate(taps, axis=1)
+
+
+def forward_kernel(columns, count, first_row, where, obs, hid, ends, cells_prev, norms, head, *refs):
+    many = count > 1
+    shards, refs = refs[:count], refs[-12:] if many else refs[-10:]
+    gates_out, cells_out, hidden_out, low_out, turned_out, seen_out = refs[:6]
+    bands, total, near, arrived = refs[7:11] if many else refs[6:]
     pixels = total.shape[0]
-
-    def fetch(step):
-        return pltpu.make_async_copy(weight.at[step], near.at[step], arrived.at[step])
-
-    for step in range(KERNEL):
-        fetch(step).start()
+    fetch_shards(shards, where, near, arrived)
     lifted = (ends[0:1, :] * obs[...] + ends[1:2, :]).astype(BF).astype(F32)
     fill_bands(bands, jnp.concatenate([lifted, hid[...].astype(F32)], axis=1), columns)
     total[...] = jnp.zeros_like(total)
+    await_shards(shards, near, arrived)
+    if many:
+        ordered = pltpu.make_async_copy(near, refs[6], refs[11])
+        ordered.start()
 
     @pl.loop(0, KERNEL)
     def tap_row(step):
         begin = pl.multiple_of((first_row[0] + step) * columns, columns)
-        fetch(step).wait()
+        depth = KERNEL * IN_DIM
+        await_row(shards, near, arrived, step)
+        rows = pl.ds(pl.multiple_of(step * depth, depth), depth)
         total[...] += jnp.dot(
-            bands[pl.ds(begin, pixels), :], near[step], preferred_element_type=F32
+            bands[pl.ds(begin, pixels), :], near[rows, :], preferred_element_type=F32
         )
 
     gates = total[...]
@@ -169,9 +220,13 @@
     seen_out[...] = lax.dot_general(
         head[...], hidden, (((1,), (1,)), ((), ())), precision=EXACT, preferred_element_type=F32
     )[0:1, :]
-
-
-def forward_frame(copies, columns, first_row, obs, hid, ends, weight, cells_prev, norms, head):
+    if many:
+        ordered.wait()
+
+
+def forward_frame(
+    copies, columns, first_row, where, obs, hid, ends, parts, cells_prev, norms, head, waits
+):
     pixels, width = cells_prev.shape
     image = hid.shape[0]
     gate = 4 * width
@@ -183,39 +238,34 @@
         shape((copies, width, pixels), BF),
         shape((1, pixels), F32),
     )
+    args = [obs, hid, ends, cells_prev, norms, head]
+    far = list(parts) + list(waits)
+    out_specs = [whole(o) for o in outs]
+    scratch = [
+        pltpu.VMEM((image + 2 * MARGIN * columns, KERNEL * IN_DIM), BF),
+        pltpu.VMEM((pixels, gate), F32),
+    ] + shard_scratch(parts)
+    if len(parts) > 1:
+        outs += (shape((TAPS * IN_DIM, gate), BF),)
+        out_specs.append(pl.BlockSpec(memory_space=pl.ANY))
+        scratch.append(pltpu.SemaphoreType.DMA)
 
     def body(*refs):
-        forward_kernel(columns, *refs)
+        forward_kernel(columns, len(parts), *refs)
 
     return pl.pallas_call(
         body,
         out_shape=outs,
         grid_spec=pltpu.PrefetchScalarGridSpec(
-            num_scalar_prefetch=1,
+            num_scalar_prefetch=2,
             grid=(1,),
-            in_specs=[
-                whole(obs),
-                whole(hid),
-                whole(ends),
-                pl.BlockSpec(memory_space=pl.ANY),
-                whole(cells_prev),
-                whole(norms),
-                whole(head),
-            ],
-            out_specs=[whole(o) for o in outs],
-            scratch_shapes=[
-                pltpu.VMEM((image + 2 * MARGIN * columns, KERNEL * IN_DIM), BF),
-                pltpu.VMEM((pixels, gate), F32),
-                pltpu.VMEM((KERNEL, KERNEL * IN_DIM, gate), BF),
-                pltpu.SemaphoreType.DMA((KERNEL,)),
-            ],
+            in_specs=[whole(a) for a in args] + [pl.BlockSpec(memory_space=pl.ANY)] * len(far),
+            out_specs=out_specs,
+            scratch_shapes=scratch,
         ),
         cost_estimate=hint(4),
         name="forward_frame",
-    )(
-        first_row, obs, hid, ends, weight.reshape(KERNEL, KERNEL * IN_DIM, gate), cells_prev,
-        norms, head,
-    )
+    )(first_row, where, *args, *far)
 
 
 def backward_kernel(last, *refs):
@@ -297,18 +347,12 @@
     )(scalars, *args)
 
 
-def hidden_kernel(columns, me, above, low, below, weight, *refs):
-    outs, (bands, total, held, near, arrived) = refs[:-5], refs[-5:]
+def hidden_kernel(columns, count, me, where, above, low, below, *refs):
+    shards, outs = refs[:count], refs[count:-5]
+    bands, total, held, near, arrived = refs[-5:]
     pixels = low.shape[1]
     blocks, unused, width = held.shape
-
-    def fetch(step):
-        return pltpu.make_async_copy(
-            weight.at[pl.ds(step * KERNEL, KERNEL), 1], near.at[step], arrived.at[step]
-        )
-
-    for step in range(KERNEL):
-        fetch(step).start()
+    fetch_shards(shards, where, near, arrived)
     fill_bands(bands, low[0].astype(F32), columns, mirrored=True)
     edge = MARGIN * columns
     if above is not None:
@@ -324,12 +368,14 @@
                     inside, moved, 0.0
                 ).astype(BF)
     total[...] = jnp.zeros_like(total)
+    hidden_dim = total.shape[1]
+    await_shards(shards, near, arrived)
 
     @pl.loop(0, KERNEL)
     def tap_row(step):
         begin = pl.multiple_of((KERNEL - 1 - step) * columns, columns)
-        fetch(step).wait()
-        taps = jnp.concatenate([near[step, d] for d in range(KERNEL)], axis=1)
+        await_row(shards, near, arrived, step)
+        taps = half_taps(near, step, IN_DIM - hidden_dim, hidden_dim)
         total[...] += lax.dot_general(
             bands[pl.ds(begin, pixels), :],
             taps,
@@ -343,40 +389,91 @@
         outs[k][...] = held[k]
 
 
-def hidden_gradient(columns, blocks, me, sides, low, weight):
+def hidden_gradient(columns, blocks, me, where, sides, low, parts):
     unused, pixels, gate = low.shape
-    hidden_dim = weight.shape[1] // 2
-    halves = weight.reshape(TAPS, 2, hidden_dim, gate)
+    hidden_dim = IN_DIM // 2
     width = hidden_dim // blocks
     outs = (shape((pixels, width), F32),) * blocks
     args = [low] if sides is None else [sides[0], low, sides[1]]
-    specs = [pl.BlockSpec((1,) + a.shape[1:], lambda *i: (0, 0, 0)) if a is low else whole(a) for a in args]
-
-    def body(me_ref, *refs):
+    specs = [
+        pl.BlockSpec((1,) + a.shape[1:], lambda *i: (0, 0, 0)) if a is low else whole(a)
+        for a in args
+    ]
+
+    def body(me_ref, where_ref, *refs):
         if sides is None:
-            hidden_kernel(columns, me_ref, None, refs[0], None, *refs[1:])
-        else:
-            hidden_kernel(columns, me_ref, *refs)
+            refs = (None, refs[0], None) + refs[1:]
+        hidden_kernel(columns, len(parts), me_ref, where_ref, *refs)
 
     return pl.pallas_call(
         body,
         out_shape=outs,
         grid_spec=pltpu.PrefetchScalarGridSpec(
-            num_scalar_prefetch=1,
+            num_scalar_prefetch=2,
             grid=(1,),
-            in_specs=specs + [pl.BlockSpec(memory_space=pl.ANY)],
+            in_specs=specs + [pl.BlockSpec(memory_space=pl.ANY)] * len(parts),
             out_specs=[whole(o) for o in outs],
             scratch_shapes=[
                 pltpu.VMEM((pixels + 2 * MARGIN * columns, KERNEL * gate), BF),
                 pltpu.VMEM((pixels, hidden_dim), F32),
                 pltpu.VMEM((blocks, pixels, width), F32),
-                pltpu.VMEM((KERNEL, KERNEL, hidden_dim, gate), BF),
-                pltpu.SemaphoreType.DMA((KERNEL,)),
-            ],
+            ]
+            + shard_scratch(parts),
         ),
         cost_estimate=hint(4),
         name="hidden_gradient",
-    )(me, *args, halves)
+    )(me, where, *args, *parts)
+
+
+def lift_kernel(where, echo, *refs):
+    shards, (out, near, arrived) = refs[:-3], refs[-3:]
+    fetch_shards(shards, where, near, arrived)
+    out[...] = jnp.zeros_like(out)
+    await_shards(shards, near, arrived)
+    hidden_dim = out.shape[1]
+
+    @pl.loop(0, KERNEL)
+    def tap_row(step):
+        await_row(shards, near, arrived, step)
+        lanes = []
+        for d in range(KERNEL):
+            rows = []
+            for place in (step * KERNEL + d, step * KERNEL + d + ONES_ROW):
+                value = echo[pl.ds(place, 1), :]
+                high = value.astype(BF).astype(F32)
+                rows += [high, value - high]
+            rows.append(jnp.zeros((12, echo.shape[1]), F32))
+            lanes.append(jnp.concatenate(rows, axis=0).astype(BF))
+        out[...] += lax.dot_general(
+            jnp.concatenate(lanes, axis=1),
+            half_taps(near, step, 0, hidden_dim),
+            (((1,), (1,)), ((), ())),
+            preferred_element_type=F32,
+        )
+
+
+def lift_gradients(where, echo, parts, waits):
+    hidden_dim = IN_DIM // 2
+    count = len(parts)
+
+    def body(where_ref, echo_ref, *refs):
+        lift_kernel(where_ref, echo_ref, *refs[:count], *refs[-3:])
+
+    far = list(parts) + list(waits)
+    got = pl.pallas_call(
+        body,
+        out_shape=shape((16, hidden_dim), F32),
+        grid_spec=pltpu.PrefetchScalarGridSpec(
+            num_scalar_prefetch=1,
+            grid=(1,),
+            in_specs=[whole(echo)] + [pl.BlockSpec(memory_space=pl.ANY)] * len(far),
+            out_specs=pl.BlockSpec((16, hidden_dim), lambda *i: (0, 0)),
+            scratch_shapes=shard_scratch(parts),
+        ),
+        cost_estimate=hint(5),
+        name="lift_gradients",
+    )(where, echo, *far)
+    return jnp.stack([got[0] + got[1], got[2] + got[3]])
 
 
 def patches_kernel(columns, slabs, tiles, places, obs, ends, *refs):
@@ -412,12 +509,14 @@
     out[...] = patches[pl.ds(skip, own), :]
 
 
-def owned_patches(columns, slabs, own, span, places, obs, hid, ends):
+def owned_patches(columns, slabs, own, span, places, obs, hid, ends, waits):
     owners, unused, image = obs.shape
     tiles, (unused_too, width, pixels) = len(hid), hid[0].shape
 
+    n = 3 + tiles
+
     def body(*refs):
-        patches_kernel(columns, slabs, tiles, *refs)
+        patches_kernel(columns, slabs, tiles, *refs[:n], *refs[n + len(waits) :])
 
     return pl.pallas_call(
         body,
@@ -429,7 +528,8 @@
                 pl.BlockSpec((1, 1, image), lambda s, where: (s, 0, 0)),
                 whole(ends),
             ]
-            + [pl.BlockSpec((1, width, pixels), lambda s, where: (s, 0, 0))] * tiles,
+            + [pl.BlockSpec((1, width, pixels), lambda s, where: (s, 0, 0))] * tiles
+            + [pl.BlockSpec(memory_space=pl.ANY)] * len(waits),
             out_specs=pl.BlockSpec((own, image), lambda s, where: (0, s)),
             scratch_shapes=[
                 pltpu.VMEM((span, image, image), BF),
@@ -439,7 +539,7 @@
         ),
         cost_estimate=hint(9),
         name="owned_patches",
-    )(places, obs, ends, *hid)
+    )(places, obs, ends, *hid, *waits)
 
 
 def adamw(weight, moment, second, grad, rate, correction):
@@ -618,9 +718,84 @@
     )(me, scalars, everyone, *smalls, *bases, *late, *kernel_triple)
 
 
-def split_low(values):
-    high = values.astype(BF)
-    return high, (values - high.astype(F32)).astype(BF)
+def split_states(me, blocks, hidden, cells, waits):
+    pixels, width = hidden.shape
+    rows = pixels // blocks
+
+    def body(me_ref, hidden_ref, cells_ref, *refs):
+        for k, out in enumerate(refs[len(waits) :]):
+            begin = pl.multiple_of(jnp.bitwise_xor(me_ref[0], k) * rows, rows)
+            out[0] = hidden_ref[pl.ds(begin, rows), :]
+            out[1] = cells_ref[pl.ds(begin, rows), :]
+
+    outs = (shape((2, rows, width), F32),) * blocks
+    return list(
+        pl.pallas_call(
+            body,
+            out_shape=outs,
+            grid_spec=pltpu.PrefetchScalarGridSpec(
+                num_scalar_prefetch=1,
+                grid=(1,),
+                in_specs=[whole(hidden), whole(cells)]
+                + [pl.BlockSpec(memory_space=pl.ANY)] * len(waits),
+                out_specs=[whole(o) for o in outs],
+            ),
+            name="split_states",
+        )(me, hidden, cells, *waits)
+    )
+
+
+def join_states(me, parts, waits):
+    blocks = len(parts)
+    unused, rows, width = parts[0].shape
+
+    def body(me_ref, *refs):
+        outs, held = refs[-3:-1], refs[-1]
+        for k in range(blocks):
+            held[jnp.bitwise_xor(me_ref[0], k)] = refs[k][...]
+        for n, out in enumerate(outs):
+            out[...] = jnp.concatenate([held[b, n] for b in range(blocks)], axis=1)
+
+    outs = (shape((rows, blocks * width), F32),) * 2
+    return pl.pallas_call(
+        body,
+        out_shape=outs,
+        grid_spec=pltpu.PrefetchScalarGridSpec(
+            num_scalar_prefetch=1,
+            grid=(1,),
+            in_specs=[whole(p) for p in parts]
+            + [pl.BlockSpec(memory_space=pl.ANY)] * len(waits),
+            out_specs=[whole(o) for o in outs],
+            scratch_shapes=[pltpu.VMEM((blocks, 2, rows, width), F32)],
+        ),
+        name="join_states",
+    )(me, *parts, *waits)
+
+
+def looks_kernel(height, columns, obs, out):
+    lane = lax.broadcasted_iota(I32, (1, height * columns), 1)
+    for f in range(out.shape[0]):
+        out[f] = jnp.zeros(out.shape[1:], F32)
+        values = obs[f]
+        for t in range(TAPS):
+            down, right = t // KERNEL - MARGIN, t % KERNEL - MARGIN
+            row, column = lane // columns + down, lane % columns + right
+            inside = (row >= 0) & (row < height) & (column >= 0) & (column < columns)
+            offset = down * columns + right
+            moved = values if offset == 0 else pltpu.roll(values, (-offset) % values.shape[1], 1)
+            out[f, t : t + 1, :] = jnp.where(inside, moved, 0.0)
+            out[f, ONES_ROW + t : ONES_ROW + t + 1, :] = jnp.where(inside, 1.0, 0.0)
+
+
+def tap_looks(height, columns, obs):
+    out = shape((obs.shape[0], 2 * ONES_ROW, height * columns), F32)
+
+    def body(*refs):
+        looks_kernel(height, columns, *refs)
+
+    return pl.pallas_call(
+        body, out_shape=out, grid=(1,), in_specs=[whole(obs)], out_specs=whole(out), name="looks"
+    )(obs)
 
 
 def per_device(
@@ -665,8 +840,7 @@
     if slabs > 1:
         groups = [[s * blocks + b for b in range(blocks)] for s in range(slabs)]
 
-    weight = lax.all_gather(own_kernel_columns(kernels[0], block), "dp", axis=0, tiled=True)
-    weight = weight.reshape(TAPS, IN_DIM, gate)
+    local = own_kernel_columns(kernels[0], block)
 
     frame_ids = lax.broadcasted_iota(I32, (1, frames), 1)
     counted = (frame_ids < lengths[:, None]).astype(F32)
@@ -678,6 +852,10 @@
     obs_all = small[0]
     mine = lax.dynamic_slice_in_dim(small, owner, 1, 2)
     mine_rows = lax.dynamic_slice_in_dim(mine, first_row * columns, pixels, 3)
+
+    looks = tap_looks(height, columns, mine[0])
+    if slabs > 1:
+        looks = lax.dynamic_slice_in_dim(looks, first_row * columns, pixels, 2)
 
     def own_columns(values):
         shaped = values.reshape(values.shape[:-1] + (4, hidden_dim))
@@ -713,9 +891,11 @@
         places += [(first_tap + k) // KERNEL - MARGIN, (first_tap + k) % KERNEL - MARGIN]
     places = jnp.stack(places).astype(I32)
 
-    def patches_of(frame_no, hid):
+    def patches_of(frame_no, hid, waits=()):
         obs_rows = obs_all[frame_no].reshape(owners, 1, image)
-        return owned_patches(columns, slabs, own, span, places, obs_rows, hid, ends_turned)
+        return owned_patches(
+            columns, slabs, own, span, places, obs_rows, hid, ends_turned, waits
+        )
 
     states = jnp.stack([hidden_init[0, 0], cells_init[0, 0]])
     states = states.reshape(2, tile_rows * columns, blocks, width).transpose(2, 0, 1, 3)
@@ -724,47 +904,46 @@
     low = states[0].astype(BF)
     cells = states[1]
     patches = [None] * frames
-    patches[0] = patches_of(0, all_tiles(spread(low.T, "dp")))
 
     def whole_hidden(values):
         got = lax.all_gather(values, "tile").reshape(slabs, blocks, pixels, width)
         return got.transpose(0, 2, 1, 3).reshape(image, hidden_dim)
 
-    weight, patches[0] = lax.optimization_barrier((weight, patches[0]))
+    heads = [h.reshape(1, 1) for h in (head_bias, head_moment, head_second)]
+    hid = whole_hidden(low)
+    parts = [lax.all_gather(local, "dp", axis=0, tiled=True)]
+    where = jnp.zeros((1,), I32)
+    patches[0] = patches_of(0, all_tiles(spread(low.T, "dp")))
     first = jnp.reshape(first_row, (1,)).astype(I32)
     kept, seen, turns = [], [], [None] * frames
     for frame_no in range(frames):
         obs_column = mine[0, frame_no].reshape(image, 1)
-        gates, cells_next, hidden, low_next, turned, seen_part = forward_frame(
-            owners, columns, first, obs_column, whole_hidden(low), ends, weight, cells, norms, head
+        gates, cells_next, hidden, low_next, turned, seen_part, *ordered = forward_frame(
+            owners,
+            columns,
+            first,
+            where,
+            obs_column,
+            hid,
+            ends,
+            parts,
+            cells,
+            norms,
+            head,
+            [patches[0], looks] + heads if frame_no == 0 else [],
         )
+        if ordered:
+            parts, where = ordered, jnp.zeros((1,), I32)
         kept.append((gates, cells))
-        cells, low = cells_next, low_next
+        cells = cells_next
         seen.append(seen_part[0])
         if frame_no + 1 < frames:
             turns[frame_no + 1] = lax.all_to_all(turned, "dp", 0, 0)
+            hid = whole_hidden(low_next)
     seen = lax.all_gather(jnp.stack(seen), "tile", axis_index_groups=groups)
     seen, turns[1:] = lax.optimization_barrier((seen, turns[1:]))
     turns[1:] = [all_tiles(t) for t in turns[1:]]
     scalars = jnp.stack([head_bias[0], count])
-
-    padded = jnp.pad(
-        jnp.stack([mine[0, :, 0], jnp.ones_like(mine[0, :, 0])], axis=1).reshape(
-            frames, 2, height, columns
-        ),
-        ((0, 0), (0, 0), (MARGIN, MARGIN), (MARGIN, MARGIN)),
-    )
-    padded = lax.dynamic_slice_in_dim(padded, first_row, rows + 2 * MARGIN, 2)
-    looks = jnp.stack(
-        [
-            padded[:, :, a : a + rows, b : b + columns].reshape(frames, 2, pixels)
-            for a in range(KERNEL)
-            for b in range(KERNEL)
-        ],
-        axis=2,
-    )
-    looks = jnp.pad(looks, ((0, 0), (0, 0), (0, ONES_ROW - TAPS), (0, 0)))
-    looks = looks.reshape(frames, 2 * ONES_ROW, pixels)
 
     sums = jnp.zeros((8, gate), F32)
     echo = jnp.zeros((2 * ONES_ROW, gate), F32)
@@ -801,7 +980,7 @@
                 sides = (above, below)
             pieces = list(
                 hidden_gradient(
-                    columns, blocks, jnp.reshape(block, (1,)).astype(I32), sides, lows, weight
+                    columns, blocks, jnp.reshape(block, (1,)).astype(I32), where, sides, lows, parts
                 )
             )
             for k in range(1, blocks):
@@ -815,27 +994,9 @@
         for frame_no in reversed(range(1, frames)):
             part = patch_gradient(patches[frame_no], [parcels[frame_no]])[0]
             own_grad = part if frame_no == frames - 1 else own_grad + part
-    echo = after(echo, own_grad)
-    lift_kernel = weight[:, :hidden_dim]
-    echoes = echo.reshape(2, ONES_ROW, gate)[:, :TAPS]
-    lift_grads = sum(
-        jnp.einsum("ktg,tcg->kc", part, lift_kernel, preferred_element_type=F32)
-        for part in split_low(echoes)
-    )
-
+    lift_grads = lift_gradients(where, echo, parts, [own_grad])
     pieces = [None] + [all_tiles(p, [own_grad, lift_grads]) for p in parcels[1:]]
 
-    states = after(jnp.stack([hidden, cells]), own_grad)
-    states = states.reshape(2, blocks, tile_rows * columns, width)
-    final = []
-    for k in range(blocks):
-        part = lax.dynamic_slice_in_dim(states, jnp.bitwise_xor(block, k), 1, 1)
-        if k:
-            part = lax.ppermute(part, "tile", [(j, j ^ k) for j in range(tiles)])
-        final.append(part)
-    final = jnp.concatenate(final, axis=1)
-    final = jnp.take(final, jnp.bitwise_xor(jnp.arange(blocks), block), axis=1)
-    final = final.transpose(0, 2, 1, 3).reshape(2, 1, 1, tile_rows, columns, hidden_dim)
     once = (block == 0).astype(F32)
     norm_part = jnp.zeros((2, 4, hidden_dim), F32)
     norm_part = lax.dynamic_update_slice_in_dim(
@@ -854,15 +1015,25 @@
     )
     lanes = 2 * GROUP_SIZE
     packed = jnp.pad(packed, (0, -packed.shape[0] % lanes)).reshape(-1, lanes)
+    my_block = jnp.reshape(block, (1,)).astype(I32)
+
+    def final_states(parts, between):
+        for k in range(1, blocks):
+            parts[k] = lax.ppermute(parts[k], "tile", [(j, j ^ k) for j in range(tiles)])
+        got = join_states(my_block, parts, between)
+        return list(got)
+
     devices = owners * tiles
     if slabs == 1:
-        own_grad, square = patch_gradient(patches[0], [parcels[0]], own_grad, waits=[final])
+        own_grad, square = patch_gradient(patches[0], [parcels[0]], own_grad)
         packed = jnp.broadcast_to(jnp.concatenate([packed, square])[None], (devices, packed.shape[0] + 1, lanes))
+        parts = split_states(my_block, blocks, hidden, cells, [square])
         bases = [0.0] * (blocks - 1)
         for frame_no in reversed(range(1, frames)):
-            got = patch_gradient(patches[frame_no], pieces[frame_no][1:], waits=[packed])
+            got = patch_gradient(patches[frame_no], pieces[frame_no][1:], waits=[packed, parts[0]])
             bases = [b + g for b, g in zip(bases, got)]
         everyone = lax.all_to_all(packed, ("dp", "tile"), 0, 0)
+        final = final_states(parts, [bases[-1]])
         pieces[0] = all_tiles(parcels[0], [everyone] + bases)
         bases, late = [own_grad] + bases, [patches[0]] + pieces[0][1:]
     else:
@@ -880,11 +1051,11 @@
             own_grad = jnp.where(block == b, bases[b], own_grad)
         square = jnp.sum(own_grad * own_grad, axis=0, keepdims=True) * (slab == 0).astype(F32)
         square = square[:, : 2 * GROUP_SIZE] + square[:, 2 * GROUP_SIZE :]
+        final = final_states(split_states(my_block, blocks, hidden, cells, []), [])
         packed = jnp.broadcast_to(jnp.concatenate([packed, square])[None], (devices, packed.shape[0] + 1, lanes))
         everyone = lax.all_to_all(packed, ("dp", "tile"), 0, 0)
     correction = 1.0 - jnp.power(0.5, step_count[0].astype(F32))
     kernel_rate = (TAPS * IN_DIM) ** (-0.5)
-    heads = [h.reshape(1, 1) for h in (head_bias, head_moment, head_second)]
     smalls = [norm_params, norm_moment, norm_second, end_params, end_moment, end_second] + heads
     out = last_update(
         me,
@@ -901,7 +1072,7 @@
         + tuple(k[None] for k in out[:3])
         + tuple(out[5:11])
         + tuple(h.reshape(1) for h in out[11:14])
-        + (final[0], final[1])
+        + tuple(g.reshape(1, 1, tile_rows, columns, hidden_dim) for g in final)
     )
 
 

time: 299 us -> 302 us (1.010)
  Pallas kernels: 94.2 us -> 104 us
  waiting for transfers between devices: 80.1 us -> 86.2 us
  local copies, waits for them, and re-layouts: 27.8 us -> 21.9 us
  matrix products: 5.89 us -> 0 us
    pallas_call x0 -> x4, Pallas kernels: none -> 9.55 us  [the longest x1 4.7 us: lift_gradients(): pl.pallas_call(body, out_shape=shape((16, hidden_dim), F32), grid_spec=pl...]
    dot_general x2 -> x0, matrix products: 5.89 us -> none  [per_device(): jnp.einsum('ktg,tcg->kc', part, lift_kernel, preferred_element_type=F32)]
    unnamed x93 -> x63, local copies, waits for them, and re-layouts: 9.14 us -> 8.03 us
  transfers between devices with their start and end apart: 26 -> 26, of which waited for: 13 -> 12; matrix products, arithmetic and copies ran while one was open for 12% -> 8% of each run, Pallas kernels for 18% -> 22%
where the time goes in v3:
time: 302 us; the launch traced here: 299 us
  Pallas kernels  104 us (34%)
  waiting for transfers between devices  86.2 us (29%)
  starting transfers between devices  41.5 us (14%)
  local copies, waits for them, and re-layouts  21.9 us (7%)
  between operations  18.7 us (6%)
  blocking collectives  16.6 us (5%)
  other arithmetic  10.2 us (3%)
    all_gather x1, waiting for transfers between devices, per_device(): parts = [lax.all_gather(local, 'dp', axis=0, tiled=True)]  40.2 us
    pallas_call x1, Pallas kernels, last_update(): pl.pallas_call(body, out_shape=tuple([shape((own, gate_dim), F32)] * 3 +...  25 us
    pallas_call x3, Pallas kernels, patch_gradient(): pl.pallas_call(body, out_shape=tuple(outs), grid=(own // step,), in_specs...  20.3 us
    pallas_call x2, Pallas kernels, owned_patches(): pl.pallas_call(body, out_shape=shape((own, owners * image), BF), grid_spe...  18.1 us
    all_to_all x2, waiting for transfers between devices, spread(): return lax.all_to_all(jnp.broadcast_to(x[None], (n,) + x.shape), axes, 0, 0)  17.6 us
    pallas_call x2, Pallas kernels, forward_frame(): pl.pallas_call(body, out_shape=outs, grid_spec=pltpu.PrefetchScalarGridSp...  14 us
    all_gather x2, blocking collectives, whole_hidden(): got = lax.all_gather(values, 'tile').reshape(slabs, blocks, pixels, width)  11.4 us
    all_to_all x2, starting transfers between devices, per_device(): parcels[frame_no] = lax.all_to_all(lows, 'dp', 0, 0)  9.58 us
  transfers between devices with their start and end apart: 26, of which 12 were waited for; matrix products, arithmetic and copies ran while one was open for 8% of the time, Pallas kernels for 22%

profile of v3, /device:TPU:0, one launch (start us, length us, event | category | flops | bytes accessed | tf_op | source)
XLA Modules:
  0.0 299.3 jit_solution(7799172399432316381)
XLA Ops:
  7.9 3.8 %columns.1 = bf16[1600,256]{1,0:T(8,128)(2,1)} custom-call(s32[2]{0:T(128)} %pad_add_fusion.place, f32[1600,1024]{1,0:T(8,128)} %bitcast.97, f32[1600,1024]{1,0:T(8,128)} %bitcast.98, f32[1600,1024]{1,0:T(8,128)} %bitcast.99, f32[1600,1024]{1,0:T(8,128)} %bitcast.100), custom_call_target="tpu_custom_call" | custom-call | tf_op jit(solution)/shard_map/columns/pallas_call | solution.py:85
  12.9 4.3 %all-to-all-start.1 = ((f32[4,1,8192]{2,1,0:T(1,128)}), f32[4,1,8192]{2,1,0:T(1,128)S(1)}, u32[]{:S(2)}, u32[]{:S(2)}) async-start(f32[4,1,8192]{2,1,0:T(1,128)} %reshape.189), calls=%async_computation.1 | async-start | bytes 262144 | tf_op jit(solution)/shard_map/all_to_all | solution.py:902
  18.9 2.9 all-to-all-done.1
  21.8 5.4 %all-to-all-start = ((f32[32,1,384]{2,1,0:T(1,128)}), f32[32,1,384]{2,1,0:T(1,128)S(1)}, u32[]{:S(2)}, u32[]{:S(2)}) async-start(f32[32,1,384]{2,1,0:T(1,128)} %reshape.187), calls=%async_computation | async-start | bytes 98304 | tf_op jit(solution)/shard_map/all_to_all | solution.py:27
  27.7 1.0 reduce.3
  29.0 6.2 %all-to-all-done = f32[32,1,384]{2,1,0:T(1,128)S(1)} async-done(((f32[32,1,384]{2,1,0:T(1,128)}), f32[32,1,384]{2,1,0:T(1,128)S(1)}, u32[]{:S(2)}, u32[]{:S(2)}) %all-to-all-start) | async-done | bytes 49184 | tf_op jit(solution)/shard_map/all_to_all | solution.py:27
  36.0 3.4 %all-to-all-start.2 = ((bf16[8,64,256]{2,1,0:T(8,128)(2,1)}), bf16[8,64,256]{2,1,0:T(8,128)(2,1)S(1)}, u32[]{:S(2)}, u32[]{:S(2)}) async-start(bf16[8,64,256]{2,1,0:T(8,128)(2,1)} %broadcast_in_dim.47), calls=%async_computation.2 | async-start | bytes 524288 | tf_op jit(solution)/shard_map/all_to_all | solution.py:27
  45.1 11.4 %all-to-all-done.2.refs_3_ = bf16[8,64,256]{2,1,0:T(8,128)(2,1)S(1)} async-done(((bf16[8,64,256]{2,1,0:T(8,128)(2,1)}), bf16[8,64,256]{2,1,0:T(8,128)(2,1)S(1)}, u32[]{:S(2)}, u32[]{:S(2)}) %all-to-all-start.2) | async-done | bytes 262176 | tf_op jit(solution)/shard_map/all_to_all | solution.py:27
  58.4 1.5 looks.1.refs_10_
  61.3 3.1 %collective-permute-done.1.refs_5_ = bf16[8,64,256]{2,1,0:T(8,128)(2,1)S(1)} collective-permute-done((bf16[8,64,256]{2,1,0:T(8,128)(2,1)S(1)}, bf16[8,64,256]{2,1,0:T(8,128)(2,1)S(1)}, u32[]{:S(2)}, u32[]{:S(2)}) %collective-permute-start.1) | collective-permute-done | bytes 262176 | tf_op jit(solution)/shard_map/ppermute | solution.py:880
  64.4 1.6 slice_bitcast_fusion.1
  66.8 5.4 %all_gather.19 = bf16[4,256,64]{1,2,0:T(8,128)(2,1)S(1)} all-gather(bf16[1,256,64]{1,2,0:T(8,128)(2,1)S(1)} %copy.72), channel_id=1, replica_groups=mesh['tile'=4,'dp'=8] {'tile'}, dimensions={0}, use_global_device_ids=true | all-gather | bytes 163840 | tf_op jit(solution)/shard_map/all_gather | solution.py:909
  73.8 9.1 %owned_patches.2.refs_9_.refs_0_.refs_16_ = bf16[1600,2048]{1,0:T(8,128)(2,1)} custom-call(s32[10]{0:T(128)} %stack.87.refs_0_, f32[8,1,256]{2,1,0:T(1,128)} %reshape_squeeze.17.refs_1_, f32[256,2]{1,0:T(8,128)} %bitcast.117, bf16[8,64,256]{2,1,0:T(8,128)(2,1)} %copy-done.6, bf16[8,64,256]{2,1,0:T(8,128)(2,1)} %copy-done.23, bf16[8,64,256]{2,1,0:T(8,128)(2,1)} %copy-done.22, ...), custom_call_target="tpu_custom_call" | custom-call | flops 3150000128 | bytes 9450000 | tf_op jit(solution)/shard_map/owned_patches/pallas_call | solution.py:521
  82.9 40.2 %all-gather.5.cloned.1.call-done.refs_8_.refs_1_.refs_0_ = bf16[12800,256]{1,0:T(8,128)(2,1)} async-done(((bf16[1600,256]{1,0:T(8,128)(2,1)}), bf16[12800,256]{1,0:T(8,128)(2,1)}) %all-gather.5.cloned.1.call-update) | async-done | bytes 6553616 | tf_op jit(solution)/shard_map/all_gather | solution.py:914
  123.7 7.0 %forward_frame.2 = (f32[256,256]{1,0:T(8,128)}, f32[256,64]{1,0:T(8,128)}, f32[256,64]{1,0:T(8,128)}, bf16[256,64]{1,0:T(8,128)(2,1)}, bf16[8,64,256]{2,1,0:T(8,128)(2,1)}, /*index=5*/f32[1,256]{1,0:T(1,128)}) custom-call(s32[1]{0:T(128)} %bitcast.4.refs_0_, s32[1]{0:T(128)} %constant.115.clone.1.refs_1_.where_ref, f32[256,1]{1,0:T(8,128)} %copy.75.refs_2_, ...), custom_call_target="tpu_custom_call" | custom-call | flops 1400000000 | bytes 4200000 | tf_op jit(solution)/shard_map/forward_frame/pallas_call | solution.py:256
  130.7 3.4 %all-to-all-start.3 = ((bf16[8,64,256]{2,1,0:T(8,128)(2,1)}), bf16[8,64,256]{2,1,0:T(8,128)(2,1)S(1)}, u32[]{:S(2)}, u32[]{:S(2)}) async-start(bf16[8,64,256]{2,1,0:T(8,128)(2,1)} %get-tuple-element.71), calls=%async_computation.3 | async-start | bytes 524288 | tf_op jit(solution)/shard_map/all_to_all | solution.py:941
  136.8 6.0 %all-gather = bf16[1024,64]{1,0:T(8,128)(2,1)S(1)} all-gather(bf16[256,64]{1,0:T(8,128)(2,1)} %get-tuple-element.68), channel_id=2, replica_groups=mesh['tile'=4,'dp'=8] {'tile'}, dimensions={0}, use_global_device_ids=true | all-gather | bytes 163840 | tf_op jit(solution)/shard_map/all_gather | solution.py:909
  143.7 7.0 %forward_frame.3 = (f32[256,256]{1,0:T(8,128)}, f32[256,64]{1,0:T(8,128)}, f32[256,64]{1,0:T(8,128)}, bf16[256,64]{1,0:T(8,128)(2,1)}, bf16[8,64,256]{2,1,0:T(8,128)(2,1)}, /*index=5*/f32[1,256]{1,0:T(1,128)}) custom-call(s32[1]{0:T(128)} %bitcast.4.refs_0_, s32[1]{0:T(128)} %constant.115.clone.1.refs_1_.where_ref, f32[256,1]{1,0:T(8,128)} %copy.79.refs_2_, ...), custom_call_target="tpu_custom_call" | custom-call | flops 1400000000 | bytes 4200000 | tf_op jit(solution)/shard_map/forward_frame/pallas_call | solution.py:256
  151.4 5.2 %all-gather.2 = f32[4,2,256]{2,1,0:T(2,128)S(1)} all-gather(f32[1,2,256]{2,1,0:T(2,128)S(1)} %maximum_bitcast_fusion.1), channel_id=3, replica_groups=mesh['tile'=4,'dp'=8] {'tile'}, dimensions={0}, use_global_device_ids=true | all-gather | bytes 10240 | tf_op jit(solution)/shard_map/all_gather | solution.py:943
  157.2 4.0 %backward_cell.2 = (bf16[8,256,256]{2,1,0:T(8,128)(2,1)}, f32[256,64]{1,0:T(8,128)}, f32[8,256]{1,0:T(8,128)}, f32[64,256]{1,0:T(8,128)}, f32[8,256]{1,0:T(8,128)}, /*index=5*/f32[8,64]{1,0:T(8,128)}) custom-call(f32[2]{0:T(128)} %pad_maximum_fusion.4.refs_0_, f32[4,256]{1,0:T(4,128)} %get-tuple-element.130.refs_1_, f32[1,256]{1,0:T(1,128)} %get-tuple-element.124.refs_2_, ...), custom_call_target="tpu_custom_call" | custom-call | flops 1400000000 | bytes 4200000 | tf_op jit(solution)/shard_map/backward_cell/pallas_call | solution.py:339
  161.2 5.9 %all-to-all-start.4 = ((bf16[8,256,256]{2,1,0:T(8,128)(2,1)}), bf16[8,256,256]{2,1,0:T(8,128)(2,1)S(1)}, u32[]{:S(2)}, u32[]{:S(2)}) async-start(bf16[8,256,256]{2,1,0:T(8,128)(2,1)} %get-tuple-element.77.refs_0_), calls=%async_computation.4 | async-start | bytes 2097152 | tf_op jit(solution)/shard_map/all_to_all | solution.py:969
  167.2 5.2 %hidden_gradient.1 = (f32[256,64]{1,0:T(8,128)}, f32[256,64]{1,0:T(8,128)}, f32[256,64]{1,0:T(8,128)}, f32[256,64]{1,0:T(8,128)}) custom-call(s32[1]{0:T(128)} %bitcast.me_ref.refs_0_, s32[1]{0:T(128)} %constant.115.clone.1.refs_1_.where_ref, bf16[8,256,256]{2,1,0:T(8,128)(2,1)} %get-tuple-element.77.refs_0_, ...), custom_call_target="tpu_custom_call" | custom-call | flops 1400000000 | bytes 4200000 | tf_op jit(solution)/shard_map/hidden_gradient/pallas_call | solution.py:408
  172.5 1.5 collective-permute-start.4
  174.3 1.5 collective-permute-start.7
  175.8 3.3 %collective-permute-done.4.refs_12_ = f32[256,64]{1,0:T(8,128)S(1)} collective-permute-done((f32[256,64]{1,0:T(8,128)}, f32[256,64]{1,0:T(8,128)S(1)}, u32[]{:S(2)}, u32[]{:S(2)}) %collective-permute-start.4) | collective-permute-done | bytes 65568 | tf_op jit(solution)/shard_map/ppermute | solution.py:988
  179.1 1.9 collective-permute-done.5.refs_13_
  181.6 4.2 %backward_cell.3 = (bf16[8,256,256]{2,1,0:T(8,128)(2,1)}, f32[256,64]{1,0:T(8,128)}, f32[8,256]{1,0:T(8,128)}, f32[64,256]{1,0:T(8,128)}, f32[8,256]{1,0:T(8,128)}, /*index=5*/f32[8,64]{1,0:T(8,128)}) custom-call(f32[2]{0:T(128)} %pad_maximum_fusion.4.refs_0_, f32[4,256]{1,0:T(4,128)} %get-tuple-element.131.refs_1_, f32[1,256]{1,0:T(1,128)} %get-tuple-element.123.refs_2_, ...), custom_call_target="tpu_custom_call" | custom-call | flops 1400000000 | bytes 4200000 | tf_op jit(solution)/shard_map/backward_cell/pallas_call | solution.py:339
  185.9 7.6 %all-to-all-done.4.refs_1_ = bf16[8,256,256]{2,1,0:T(8,128)(2,1)S(1)} async-done(((bf16[8,256,256]{2,1,0:T(8,128)(2,1)}), bf16[8,256,256]{2,1,0:T(8,128)(2,1)S(1)}, u32[]{:S(2)}, u32[]{:S(2)}) %all-to-all-start.4) | async-done | bytes 1048608 | tf_op jit(solution)/shard_map/all_to_all | solution.py:969
  193.5 3.6 %all-to-all-start.5 = ((bf16[8,256,256]{2,1,0:T(8,128)(2,1)}), bf16[8,256,256]{2,1,0:T(8,128)(2,1)S(1)}, u32[]{:S(2)}, u32[]{:S(2)}) async-start(bf16[8,256,256]{2,1,0:T(8,128)(2,1)} %get-tuple-element.90), calls=%async_computation.5 | async-start | bytes 2097152 | tf_op jit(solution)/shard_map/all_to_all | solution.py:969
  199.9 1.5 collective-permute-start.10
  201.6 1.5 add.90.echo_ref
  203.1 9.0 %owned_patches.3.refs_0_ = bf16[1600,2048]{1,0:T(8,128)(2,1)} custom-call(s32[10]{0:T(128)} %stack.87.refs_0_, f32[8,1,256]{2,1,0:T(1,128)} %reshape_squeeze.19.refs_1_, f32[256,2]{1,0:T(8,128)} %bitcast.118, bf16[8,64,256]{2,1,0:T(8,128)(2,1)} %copy-done.7, bf16[8,64,256]{2,1,0:T(8,128)(2,1)} %collective-permute-done.6.refs_4_, ...), custom_call_target="tpu_custom_call" | custom-call | flops 3150000128 | bytes 9450000 | tf_op jit(solution)/shard_map/owned_patches/pallas_call | solution.py:521
  212.2 5.1 %patch_gradient.3.refs_1_.refs_2_ = f32[1600,256]{1,0:T(8,128)} custom-call(bf16[1600,2048]{1,0:T(8,128)(2,1)} %owned_patches.3.refs_0_, bf16[8,256,256]{2,1,0:T(8,128)(2,1)} %copy-done.2), custom_call_target="tpu_custom_call" | custom-call | flops 1750000000 | bytes 5250000 | tf_op jit(solution)/shard_map/patch_gradient/pallas_call | solution.py:603
  217.3 4.7 %lift_gradients.1 = f32[16,256]{1,0:T(8,128)} custom-call(s32[1]{0:T(128)} %constant.115.clone.1.refs_1_.where_ref, f32[64,256]{1,0:T(8,128)} %add.90.echo_ref, bf16[12800,256]{1,0:T(8,128)(2,1)} %all-gather.5.cloned.1.call-done.refs_8_.refs_1_.refs_0_, f32[1600,256]{1,0:T(8,128)} %patch_gradient.3.refs_1_.refs_2_), custom_call_target="tpu_custom_call" | custom-call | flops 1750000000 | bytes 5250000 | tf_op jit(solution)/shard_map/lift_gradients/pallas_call | solution.py:463
  223.5 1.5 collective-permute-done.10.refs_0_
  225.0 1.0 copy-done.5
  226.0 1.5 collective-permute-start.13
  227.5 5.7 %patch_gradient.4 = (f32[1600,256]{1,0:T(8,128)}, f32[1,128]{1,0:T(1,128)}) custom-call(bf16[1600,2048]{1,0:T(8,128)(2,1)} %owned_patches.2.refs_9_.refs_0_.refs_16_, bf16[8,256,256]{2,1,0:T(8,128)(2,1)} %copy-done.1, f32[1600,256]{1,0:T(8,128)} %patch_gradient.3.refs_1_.refs_2_), custom_call_target="tpu_custom_call" | custom-call | flops 1750000000 | bytes 5250000 | tf_op jit(solution)/shard_map/patch_gradient/pallas_call | solution.py:603
  234.7 5.5 %all-to-all-start.6 = ((f32[32,24,128]{2,1,0:T(8,128)}), f32[32,24,128]{2,1,0:T(8,128)S(1)}, u32[]{:S(2)}, u32[]{:S(2)}) async-start(f32[32,24,128]{2,1,0:T(8,128)} %broadcast_in_dim.49.refs_4_), calls=%async_computation.6 | async-start | bytes 786432 | tf_op jit(solution)/shard_map/all_to_all | solution.py:1035
  240.2 1.7 split_states.1
  242.1 9.5 %patch_gradient.5 = (f32[1600,256]{1,0:T(8,128)}, f32[1600,256]{1,0:T(8,128)}, f32[1600,256]{1,0:T(8,128)}) custom-call(bf16[1600,2048]{1,0:T(8,128)(2,1)} %owned_patches.3.refs_0_, bf16[8,256,256]{2,1,0:T(8,128)(2,1)} %collective-permute-done.9.refs_1_, bf16[8,256,256]{2,1,0:T(8,128)(2,1)} %after.2.refs_2_, ...), custom_call_target="tpu_custom_call" | custom-call | flops 3150000128 | bytes 9450000 | tf_op jit(solution)/shard_map/patch_gradient/pallas_call | solution.py:603
  251.6 4.1 %all-to-all-done.6.refs_1_.refs_2_ = f32[32,24,128]{2,1,0:T(8,128)S(1)} async-done(((f32[32,24,128]{2,1,0:T(8,128)}), f32[32,24,128]{2,1,0:T(8,128)S(1)}, u32[]{:S(2)}, u32[]{:S(2)}) %all-to-all-start.6) | async-done | bytes 393248 | tf_op jit(solution)/shard_map/all_to_all | solution.py:1035
  258.1 1.5 collective-permute-start.16
  260.2 2.3 collective-permute-done.16.refs_2_
  262.6 1.6 collective-permute-done.17.refs_3_
  264.8 1.7 join_states.1
  266.5 1.0 copy-done.4
  267.5 25.0 %last_update.1 = (f32[1600,1024]{1,0:T(8,128)}, f32[1600,1024]{1,0:T(8,128)}, f32[1600,1024]{1,0:T(8,128)}, f32[1,1]{1,0:T(1,128)}, f32[1,1]{1,0:T(1,128)}, /*in...) custom-call(s32[1]{0:T(128)} %bitcast.me_ref.refs_0_, ...), custom_call_target="tpu_custom_call" | custom-call | flops 7699999744 | bytes 23100000 | tf_op jit(solution)/shard_map/last_update/pallas_call | solution.py:698
  (149 shorter events, 28.6 us)
Async XLA Ops:
  7.2 115.9 %all-gather.5.cloned.1.call-start = ((), (), s32[]{:S(2)}) async-start(), calls=%async_computation.7 | async-start | bytes 7372800 | tf_op jit(solution)/shard_map/all_gather | solution.py:914
  7.9 3.9 %copy-start.8 = (f32[1,1,2,32,256]{4,3,2,1,0:T(8,128)S(1)}, f32[1,1,2,32,256]{4,3,2,1,0:T(8,128)}, u32[]{:S(2)}) copy-start(f32[1,1,2,32,256]{4,3,2,1,0:T(8,128)} %param.36) | copy-start | bytes 196612
  7.9 4.0 %copy-start.9 = (f32[1,1,2,32,256]{4,3,2,1,0:T(8,128)S(1)}, f32[1,1,2,32,256]{4,3,2,1,0:T(8,128)}, u32[]{:S(2)}) copy-start(f32[1,1,2,32,256]{4,3,2,1,0:T(8,128)} %param.37) | copy-start | bytes 196612
  7.9 10.0 %copy-start.18 = (s32[1,2,2,32]{3,2,1,0:T(2,128)S(1)}, s32[1,2,2,32]{3,2,1,0:T(2,128)}, u32[]{:S(2)}) copy-start(s32[1,2,2,32]{3,2,1,0:T(2,128)} %param.21) | copy-start | bytes 1540
  7.9 10.1 %copy-start.19 = (f32[1,2,2,32]{3,2,1,0:T(2,128)S(1)}, f32[1,2,2,32]{3,2,1,0:T(2,128)}, u32[]{:S(2)}) copy-start(f32[1,2,2,32]{3,2,1,0:T(2,128)} %param.20) | copy-start | bytes 1540
  7.9 10.1 %copy-start.20 = (f32[1,2,2,32]{3,2,1,0:T(2,128)S(1)}, f32[1,2,2,32]{3,2,1,0:T(2,128)}, u32[]{:S(2)}) copy-start(f32[1,2,2,32]{3,2,1,0:T(2,128)} %param.19) | copy-start | bytes 1540
  7.9 31.6 %copy-start.16 = (f32[3,256]{1,0:T(4,128)S(1)}, f32[3,256]{1,0:T(4,128)}, u32[]{:S(2)}) copy-start(f32[3,256]{1,0:T(4,128)} %refs_6_.1) | copy-start | bytes 9220
  7.9 33.7 %copy-start.15 = (f32[2,1,1024]{2,1,0:T(1,128)S(1)}, f32[2,1,1024]{2,1,0:T(1,128)}, u32[]{:S(2)}) copy-start(f32[2,1,1024]{2,1,0:T(1,128)} %refs_3_.1) | copy-start | bytes 24580
  12.9 8.9 %all-to-all-start.1 = ((f32[4,1,8192]{2,1,0:T(1,128)}), f32[4,1,8192]{2,1,0:T(1,128)S(1)}, u32[]{:S(2)}, u32[]{:S(2)}) async-start(f32[4,1,8192]{2,1,0:T(1,128)} %reshape.189), calls=%async_computation.1 | async-start | bytes 262144 | tf_op jit(solution)/shard_map/all_to_all | solution.py:902
  21.8 13.4 %all-to-all-start = ((f32[32,1,384]{2,1,0:T(1,128)}), f32[32,1,384]{2,1,0:T(1,128)S(1)}, u32[]{:S(2)}, u32[]{:S(2)}) async-start(f32[32,1,384]{2,1,0:T(1,128)} %reshape.187), calls=%async_computation | async-start | bytes 98304 | tf_op jit(solution)/shard_map/all_to_all | solution.py:27
  36.0 20.5 %all-to-all-start.2 = ((bf16[8,64,256]{2,1,0:T(8,128)(2,1)}), bf16[8,64,256]{2,1,0:T(8,128)(2,1)S(1)}, u32[]{:S(2)}, u32[]{:S(2)}) async-start(bf16[8,64,256]{2,1,0:T(8,128)(2,1)} %broadcast_in_dim.47), calls=%async_computation.2 | async-start | bytes 524288 | tf_op jit(solution)/shard_map/all_to_all | solution.py:27
  39.5 43.4 %copy-start.14 = (f32[2,256]{1,0:T(2,128)}, f32[2,256]{1,0:T(2,128)S(1)}, u32[]{:S(2)}) copy-start(f32[2,256]{1,0:T(2,128)S(1)} %slice.87.refs_4_) | copy-start | bytes 6148
  56.5 16.6 %copy-start.6 = (bf16[8,64,256]{2,1,0:T(8,128)(2,1)}, bf16[8,64,256]{2,1,0:T(8,128)(2,1)S(1)}, u32[]{:S(2)}) copy-start(bf16[8,64,256]{2,1,0:T(8,128)(2,1)S(1)} %all-to-all-done.2.refs_3_) | copy-start | bytes 786436
  56.5 8.0 %collective-permute-start.1 = (bf16[8,64,256]{2,1,0:T(8,128)(2,1)S(1)}, bf16[8,64,256]{2,1,0:T(8,128)(2,1)S(1)}, u32[]{:S(2)}, u32[]{:S(2)}) collective-permute-start(bf16[8,64,256]{2,1,0:T(8,128)(2,1)S(1)} %all-to-all-done.2.refs_3_), channel_id=1, source_target_pairs={{0,16},{8,24},{16,0},{24,8},{1,17},{9,25},{17,1},{25,9},{2,18},{10... | collective-permute-start | bytes 786440 | tf_op jit(solution)/shard_map/ppermute | solution.py:880
  61.3 11.7 %collective-permute-start = (bf16[8,64,256]{2,1,0:T(8,128)(2,1)S(1)}, bf16[8,64,256]{2,1,0:T(8,128)(2,1)S(1)}, u32[]{:S(2)}, u32[]{:S(2)}) collective-permute-start(bf16[8,64,256]{2,1,0:T(8,128)(2,1)S(1)} %all-to-all-done.2.refs_3_), channel_id=1, source_target_pairs={{0,8},{8,0},{16,24},{24,16},{1,9},{9,1},{17,25},{25,17},{2,10},{10... | collective-permute-start | bytes 786440 | tf_op jit(solution)/shard_map/ppermute | solution.py:880
  64.4 8.6 %copy-start.22 = (bf16[8,64,256]{2,1,0:T(8,128)(2,1)}, bf16[8,64,256]{2,1,0:T(8,128)(2,1)S(1)}, u32[]{:S(2)}) copy-start(bf16[8,64,256]{2,1,0:T(8,128)(2,1)S(1)} %collective-permute-done.1.refs_5_) | copy-start | bytes 786436
  64.4 8.6 %collective-permute-start.2 = (bf16[8,64,256]{2,1,0:T(8,128)(2,1)S(1)}, bf16[8,64,256]{2,1,0:T(8,128)(2,1)S(1)}, u32[]{:S(2)}, u32[]{:S(2)}) collective-permute-start(bf16[8,64,256]{2,1,0:T(8,128)(2,1)S(1)} %collective-permute-done.1.refs_5_), channel_id=1, source_target_pairs={{0,8},{8,0},{16,24},{24,16},{1,9},{9,1},{17,25},{25,17},{2,10},{10... | collective-permute-start | bytes 786440 | tf_op jit(solution)/shard_map/ppermute | solution.py:880
  130.7 20.0 %copy-start.21 = (f32[1,256]{1,0:T(1,128)S(1)}, f32[1,256]{1,0:T(1,128)}, u32[]{:S(2)}) copy-start(f32[1,256]{1,0:T(1,128)} %get-tuple-element.67) | copy-start | bytes 3076
  130.7 25.8 %all-to-all-start.3 = ((bf16[8,64,256]{2,1,0:T(8,128)(2,1)}), bf16[8,64,256]{2,1,0:T(8,128)(2,1)S(1)}, u32[]{:S(2)}, u32[]{:S(2)}) async-start(bf16[8,64,256]{2,1,0:T(8,128)(2,1)} %get-tuple-element.71), calls=%async_computation.3 | async-start | bytes 524288 | tf_op jit(solution)/shard_map/all_to_all | solution.py:941
  156.6 41.2 %copy-start.7 = (bf16[8,64,256]{2,1,0:T(8,128)(2,1)}, bf16[8,64,256]{2,1,0:T(8,128)(2,1)S(1)}, u32[]{:S(2)}) copy-start(bf16[8,64,256]{2,1,0:T(8,128)(2,1)S(1)} %all-to-all-done.3.refs_3_) | copy-start | bytes 786436
  161.2 32.2 %all-to-all-start.4 = ((bf16[8,256,256]{2,1,0:T(8,128)(2,1)}), bf16[8,256,256]{2,1,0:T(8,128)(2,1)S(1)}, u32[]{:S(2)}, u32[]{:S(2)}) async-start(bf16[8,256,256]{2,1,0:T(8,128)(2,1)} %get-tuple-element.77.refs_0_), calls=%async_computation.4 | async-start | bytes 2097152 | tf_op jit(solution)/shard_map/all_to_all | solution.py:969
  167.2 32.0 %copy-start.17 = (f32[8,64]{1,0:T(8,128)S(1)}, f32[8,64]{1,0:T(8,128)}, u32[]{:S(2)}) copy-start(f32[8,64]{1,0:T(8,128)} %get-tuple-element.86) | copy-start | bytes 6148
  167.2 34.5 %copy-start.10 = (f32[64,256]{1,0:T(8,128)S(1)}, f32[64,256]{1,0:T(8,128)}, u32[]{:S(2)}) copy-start(f32[64,256]{1,0:T(8,128)} %get-tuple-element.83) | copy-start | bytes 196612
  172.4 3.4 %collective-permute-start.3 = (f32[256,64]{1,0:T(8,128)}, f32[256,64]{1,0:T(8,128)S(1)}, u32[]{:S(2)}, u32[]{:S(2)}) collective-permute-start(f32[256,64]{1,0:T(8,128)} %get-tuple-element.79), channel_id=1, source_target_pairs={{0,8},{8,0},{16,24},{24,16},{1,9},{9,1},{17,25},{25,17},{2,10},{10... | collective-permute-start | bytes 196616 | tf_op jit(solution)/shard_map/ppermute | solution.py:988
  172.5 6.6 %collective-permute-start.4 = (f32[256,64]{1,0:T(8,128)}, f32[256,64]{1,0:T(8,128)S(1)}, u32[]{:S(2)}, u32[]{:S(2)}) collective-permute-start(f32[256,64]{1,0:T(8,128)} %get-tuple-element.80), channel_id=1, source_target_pairs={{0,16},{8,24},{16,0},{24,8},{1,17},{9,25},{17,1},{25,9},{2,18},{10... | collective-permute-start | bytes 196616 | tf_op jit(solution)/shard_map/ppermute | solution.py:988
  174.0 7.0 %collective-permute-start.5 = (f32[256,64]{1,0:T(8,128)}, f32[256,64]{1,0:T(8,128)S(1)}, u32[]{:S(2)}, u32[]{:S(2)}) collective-permute-start(f32[256,64]{1,0:T(8,128)} %get-tuple-element.81), channel_id=1, source_target_pairs={{0,24},{8,16},{16,8},{24,0},{1,25},{9,17},{17,9},{25,1},{2,26},{10... | collective-permute-start | bytes 196616 | tf_op jit(solution)/shard_map/ppermute | solution.py:988
  174.3 23.5 %collective-permute-start.7 = (bf16[8,64,256]{2,1,0:T(8,128)(2,1)S(1)}, bf16[8,64,256]{2,1,0:T(8,128)(2,1)}, u32[]{:S(2)}, u32[]{:S(2)}) collective-permute-start(bf16[8,64,256]{2,1,0:T(8,128)(2,1)S(1)} %all-to-all-done.3.refs_3_), channel_id=1, source_target_pairs={{0,16},{8,24},{16,0},{24,8},{1,17},{9,25},{17,1},{25,9},{2,18},{10... | collective-permute-start | bytes 786440 | tf_op jit(solution)/shard_map/ppermute | solution.py:880
  175.8 5.2 %copy-start.25 = (f32[256,64]{1,0:T(8,128)}, f32[256,64]{1,0:T(8,128)S(1)}, u32[]{:S(2)}) copy-start(f32[256,64]{1,0:T(8,128)S(1)} %collective-permute-done.3.refs_11_) | copy-start | bytes 196612
  179.1 1.9 copy-start.26
  193.5 18.7 %copy-start.2 = (bf16[8,256,256]{2,1,0:T(8,128)(2,1)}, bf16[8,256,256]{2,1,0:T(8,128)(2,1)S(1)}, u32[]{:S(2)}) copy-start(bf16[8,256,256]{2,1,0:T(8,128)(2,1)S(1)} %all-to-all-done.4.refs_1_) | copy-start | bytes 3145732
  193.5 32.5 %all-to-all-start.5 = ((bf16[8,256,256]{2,1,0:T(8,128)(2,1)}), bf16[8,256,256]{2,1,0:T(8,128)(2,1)S(1)}, u32[]{:S(2)}, u32[]{:S(2)}) async-start(bf16[8,256,256]{2,1,0:T(8,128)(2,1)} %get-tuple-element.90), calls=%async_computation.5 | async-start | bytes 2097152 | tf_op jit(solution)/shard_map/all_to_all | solution.py:969
  197.8 5.4 %collective-permute-start.6 = (bf16[8,64,256]{2,1,0:T(8,128)(2,1)S(1)}, bf16[8,64,256]{2,1,0:T(8,128)(2,1)}, u32[]{:S(2)}, u32[]{:S(2)}) collective-permute-start(bf16[8,64,256]{2,1,0:T(8,128)(2,1)S(1)} %all-to-all-done.3.refs_3_), channel_id=1, source_target_pairs={{0,8},{8,0},{16,24},{24,16},{1,9},{9,1},{17,25},{25,17},{2,10},{10... | collective-permute-start | bytes 786440 | tf_op jit(solution)/shard_map/ppermute | solution.py:880
  197.8 5.3 %collective-permute-start.8 = (bf16[8,64,256]{2,1,0:T(8,128)(2,1)}, bf16[8,64,256]{2,1,0:T(8,128)(2,1)}, u32[]{:S(2)}, u32[]{:S(2)}) collective-permute-start(bf16[8,64,256]{2,1,0:T(8,128)(2,1)} %collective-permute-done.7.refs_5_), channel_id=1, source_target_pairs={{0,8},{8,0},{16,24},{24,16},{1,9},{9,1},{17,25},{25,17},{2,10},{10... | collective-permute-start | bytes 786440 | tf_op jit(solution)/shard_map/ppermute | solution.py:880
  199.9 25.1 %collective-permute-start.10 = (bf16[8,256,256]{2,1,0:T(8,128)(2,1)S(1)}, bf16[8,256,256]{2,1,0:T(8,128)(2,1)S(1)}, u32[]{:S(2)}, u32[]{:S(2)}) collective-permute-start(bf16[8,256,256]{2,1,0:T(8,128)(2,1)S(1)} %all-to-all-done.4.refs_1_), channel_id=1, source_target_pairs={{0,16},{8,24},{16,0},{24,8},{1,17},{9,25},{17,1},{25,9},{2,18},{10... | collective-permute-start | bytes 3145736 | tf_op jit(solution)/shard_map/ppermute | solution.py:880
  212.1 30.0 %collective-permute-start.9 = (bf16[8,256,256]{2,1,0:T(8,128)(2,1)S(1)}, bf16[8,256,256]{2,1,0:T(8,128)(2,1)}, u32[]{:S(2)}, u32[]{:S(2)}) collective-permute-start(bf16[8,256,256]{2,1,0:T(8,128)(2,1)S(1)} %all-to-all-done.4.refs_1_), channel_id=1, source_target_pairs={{0,8},{8,0},{16,24},{24,16},{1,9},{9,1},{17,25},{25,17},{2,10},{10... | collective-permute-start | bytes 3145736 | tf_op jit(solution)/shard_map/ppermute | solution.py:880
  226.0 16.1 %collective-permute-start.11 = (bf16[8,256,256]{2,1,0:T(8,128)(2,1)}, bf16[8,256,256]{2,1,0:T(8,128)(2,1)}, u32[]{:S(2)}, u32[]{:S(2)}) collective-permute-start(bf16[8,256,256]{2,1,0:T(8,128)(2,1)} %after.2.refs_2_), channel_id=1, source_target_pairs={{0,8},{8,0},{16,24},{24,16},{1,9},{9,1},{17,25},{25,17},{2,10},{10... | collective-permute-start | bytes 3145736 | tf_op jit(solution)/shard_map/ppermute | solution.py:880
  226.0 1.6 copy-start.1
  226.0 29.7 %collective-permute-start.13 = (bf16[8,256,256]{2,1,0:T(8,128)(2,1)S(1)}, bf16[8,256,256]{2,1,0:T(8,128)(2,1)S(1)}, u32[]{:S(2)}, u32[]{:S(2)}) collective-permute-start(bf16[8,256,256]{2,1,0:T(8,128)(2,1)S(1)} %all-to-all-done.5.refs_1_), channel_id=1, source_target_pairs={{0,16},{8,24},{16,0},{24,8},{1,17},{9,25},{17,1},{25,9},{2,18},{10... | collective-permute-start | bytes 3145736 | tf_op jit(solution)/shard_map/ppermute | solution.py:880
  234.7 21.0 %all-to-all-start.6 = ((f32[32,24,128]{2,1,0:T(8,128)}), f32[32,24,128]{2,1,0:T(8,128)S(1)}, u32[]{:S(2)}, u32[]{:S(2)}) async-start(f32[32,24,128]{2,1,0:T(8,128)} %broadcast_in_dim.49.refs_4_), calls=%async_computation.6 | async-start | bytes 786432 | tf_op jit(solution)/shard_map/all_to_all | solution.py:1035
  241.8 24.6 %collective-permute-start.12 = (bf16[8,256,256]{2,1,0:T(8,128)(2,1)}, bf16[8,256,256]{2,1,0:T(8,128)(2,1)}, u32[]{:S(2)}, u32[]{:S(2)}) collective-permute-start(bf16[8,256,256]{2,1,0:T(8,128)(2,1)} %copy-done.1), channel_id=1, source_target_pairs={{0,8},{8,0},{16,24},{24,16},{1,9},{9,1},{17,25},{25,17},{2,10},{10... | collective-permute-start | bytes 3145736 | tf_op jit(solution)/shard_map/ppermute | solution.py:880
  255.7 1.1 copy-start
  256.8 9.7 %collective-permute-start.14 = (bf16[8,256,256]{2,1,0:T(8,128)(2,1)}, bf16[8,256,256]{2,1,0:T(8,128)(2,1)S(1)}, u32[]{:S(2)}, u32[]{:S(2)}) collective-permute-start(bf16[8,256,256]{2,1,0:T(8,128)(2,1)} %after.3.refs_18_), channel_id=1, source_target_pairs={{0,8},{8,0},{16,24},{24,16},{1,9},{9,1},{17,25},{25,17},{2,10},{10... | collective-permute-start | bytes 3145736 | tf_op jit(solution)/shard_map/ppermute | solution.py:880
  257.6 2.6 collective-permute-start.15
  258.1 4.5 %collective-permute-start.16 = (f32[2,64,64]{2,1,0:T(8,128)}, f32[2,64,64]{2,1,0:T(8,128)S(1)}, u32[]{:S(2)}, u32[]{:S(2)}) collective-permute-start(f32[2,64,64]{2,1,0:T(8,128)} %get-tuple-element.114), channel_id=1, source_target_pairs={{0,16},{8,24},{16,0},{24,8},{1,17},{9,25},{17,1},{25,9},{2,18},{10... | collective-permute-start | bytes 98312 | tf_op jit(solution)/shard_map/ppermute | solution.py:1022
  259.5 4.6 %collective-permute-start.17 = (f32[2,64,64]{2,1,0:T(8,128)}, f32[2,64,64]{2,1,0:T(8,128)S(1)}, u32[]{:S(2)}, u32[]{:S(2)}) collective-permute-start(f32[2,64,64]{2,1,0:T(8,128)} %get-tuple-element.115), channel_id=1, source_target_pairs={{0,24},{8,16},{16,8},{24,0},{1,25},{9,17},{17,9},{25,1},{2,26},{10... | collective-permute-start | bytes 98312 | tf_op jit(solution)/shard_map/ppermute | solution.py:1022
  260.2 3.9 %copy-start.11 = (f32[2,64,64]{2,1,0:T(8,128)}, f32[2,64,64]{2,1,0:T(8,128)S(1)}, u32[]{:S(2)}) copy-start(f32[2,64,64]{2,1,0:T(8,128)S(1)} %collective-permute-done.15.refs_1_) | copy-start | bytes 98308
  262.5 1.6 copy-start.12
  266.5 1.0 copy-start.4
  (6 other events, 4.5 us)
Sparse Core Ops, SparseCore 0:
  11.9 111.1 all-gather.4

commit v4 on v2

--- a/solution.py
+++ b/solution.py
@@ -450,7 +450,7 @@
 
 
 def rows_at_once(own):
-    return 16 * math.gcd(own // 16, 20)
+    return 16 * math.gcd(own // 16, 25)
 
 
 def patch_dot(patch, pieces):

time: 299 us -> 297 us (level)
  no operation moved by 1% of the time
where the time goes in v4:
time: 297 us; the launch traced here: 294 us
  Pallas kernels  92.3 us (31%)
  waiting for transfers between devices  80.1 us (27%)
  starting transfers between devices  43.2 us (15%)
  local copies, waits for them, and re-layouts  27.8 us (9%)
  between operations  18.9 us (6%)
  blocking collectives  16.6 us (6%)
  other arithmetic  9.57 us (3%)
  matrix products  5.89 us (2%)
    all_gather x1, waiting for transfers between devices, per_device(): lax.all_gather(own_kernel_columns(kernels[0], block), 'dp', axis=0, tiled...  38.9 us
    pallas_call x1, Pallas kernels, last_update(): pl.pallas_call(body, out_shape=tuple([shape((own, gate_dim), F32)] * 3 +...  23.1 us
    pallas_call x3, Pallas kernels, patch_gradient(): pl.pallas_call(body, out_shape=tuple(outs), grid=(own // step,), in_specs...  20.3 us
    all_to_all x2, waiting for transfers between devices, spread(): return lax.all_to_all(jnp.broadcast_to(x[None], (n,) + x.shape), axes, 0, 0)  18.8 us
    pallas_call x2, Pallas kernels, owned_patches(): pl.pallas_call(body, out_shape=shape((own, owners * image), BF), grid_spe...  18 us
    pallas_call x2, Pallas kernels, forward_frame(): pl.pallas_call(body, out_shape=outs, grid_spec=pltpu.PrefetchScalarGridSp...  14 us
    all_gather x2, blocking collectives, whole_hidden(): got = lax.all_gather(values, 'tile').reshape(slabs, blocks, pixels, width)  11.5 us
    all_to_all x2, starting transfers between devices, spread(): return lax.all_to_all(jnp.broadcast_to(x[None], (n,) + x.shape), axes, 0, 0)  10.7 us
  transfers between devices with their start and end apart: 26, of which 13 were waited for; matrix products, arithmetic and copies ran while one was open for 12% of the time, Pallas kernels for 18%

profile of v4, /device:TPU:0, one launch (start us, length us, event | category | flops | bytes accessed | tf_op | source)
XLA Modules:
  0.0 294.3 jit_solution(13722386057743450757)
XLA Ops:
  7.9 3.8 %columns.1 = bf16[1600,256]{1,0:T(8,128)(2,1)} custom-call(s32[2]{0:T(128)} %pad_add_fusion.place, f32[1600,1024]{1,0:T(8,128)} %bitcast.157, f32[1600,1024]{1,0:T(8,128)} %bitcast.158, f32[1600,1024]{1,0:T(8,128)} %bitcast.159, f32[1600,1024]{1,0:T(8,128)} %bitcast.160), custom_call_target="tpu_custom_call" | custom-call | tf_op jit(solution)/shard_map/columns/pallas_call | solution.py:85
  13.4 7.3 %all-to-all-start = ((f32[32,1,384]{2,1,0:T(1,128)}), f32[32,1,384]{2,1,0:T(1,128)S(1)}, u32[]{:S(2)}, u32[]{:S(2)}) async-start(f32[32,1,384]{2,1,0:T(1,128)} %reshape.248), calls=%async_computation | async-start | bytes 98304 | tf_op jit(solution)/shard_map/all_to_all | solution.py:27
  23.6 0.8 reshape.250
  25.1 2.9 all-to-all-done
  28.1 3.3 %all-to-all-start.1 = ((f32[4,1,8192]{2,1,0:T(1,128)}), f32[4,1,8192]{2,1,0:T(1,128)S(1)}, u32[]{:S(2)}, u32[]{:S(2)}) async-start(f32[4,1,8192]{2,1,0:T(1,128)} %reshape.250), calls=%async_computation.1 | async-start | bytes 262144 | tf_op jit(solution)/shard_map/all_to_all | solution.py:722
  36.0 1.0 reduce.3
  38.0 3.4 %all-to-all-start.2 = ((bf16[8,64,256]{2,1,0:T(8,128)(2,1)}), bf16[8,64,256]{2,1,0:T(8,128)(2,1)S(1)}, u32[]{:S(2)}, u32[]{:S(2)}) async-start(bf16[8,64,256]{2,1,0:T(8,128)(2,1)} %broadcast_in_dim.55), calls=%async_computation.2 | async-start | bytes 524288 | tf_op jit(solution)/shard_map/all_to_all | solution.py:27
  42.2 15.9 %all-to-all-done.2.refs_3_ = bf16[8,64,256]{2,1,0:T(8,128)(2,1)S(1)} async-done(((bf16[8,64,256]{2,1,0:T(8,128)(2,1)}), bf16[8,64,256]{2,1,0:T(8,128)(2,1)S(1)}, u32[]{:S(2)}, u32[]{:S(2)}) %all-to-all-start.2) | async-done | bytes 262176 | tf_op jit(solution)/shard_map/all_to_all | solution.py:27
  58.1 1.5 collective-permute-start.1
  61.4 4.7 %collective-permute-done.1.refs_5_ = bf16[8,64,256]{2,1,0:T(8,128)(2,1)S(1)} collective-permute-done((bf16[8,64,256]{2,1,0:T(8,128)(2,1)S(1)}, bf16[8,64,256]{2,1,0:T(8,128)(2,1)S(1)}, u32[]{:S(2)}, u32[]{:S(2)}) %collective-permute-start.1) | collective-permute-done | bytes 262176 | tf_op jit(solution)/shard_map/ppermute | solution.py:702
  67.0 5.5 %all_gather.19 = bf16[4,256,64]{1,2,0:T(8,128)(2,1)S(1)} all-gather(bf16[1,256,64]{1,2,0:T(8,128)(2,1)S(1)} %copy.103), channel_id=1, replica_groups=mesh['tile'=4,'dp'=8] {'tile'}, dimensions={0}, use_global_device_ids=true | all-gather | bytes 163840 | tf_op jit(solution)/shard_map/all_gather | solution.py:730
  74.0 9.1 %owned_patches.2.refs_0_.refs_16_ = bf16[1600,2048]{1,0:T(8,128)(2,1)} custom-call(s32[10]{0:T(128)} %stack.97.refs_0_, f32[8,1,256]{2,1,0:T(1,128)} %reshape_squeeze.16.refs_1_, f32[256,2]{1,0:T(8,128)} %bitcast.185, bf16[8,64,256]{2,1,0:T(8,128)(2,1)} %copy-done.7, bf16[8,64,256]{2,1,0:T(8,128)(2,1)} %copy-done.26, bf16[8,64,256]{2,1,0:T(8,128)(2,1)} %copy-done.24, ...), custom_call_target="tpu_custom_call" | custom-call | flops 3150000128 | bytes 9450000 | tf_op jit(solution)/shard_map/owned_patches/pallas_call | solution.py:422
  83.1 38.9 %all-gather.5.cloned.1.call-done = bf16[12800,256]{1,0:T(8,128)(2,1)} async-done(((bf16[1600,256]{1,0:T(8,128)(2,1)}), bf16[12800,256]{1,0:T(8,128)(2,1)}) %all-gather.5.cloned.1.call-update) | async-done | bytes 6553616 | tf_op jit(solution)/shard_map/all_gather | solution.py:668
  122.7 7.0 %forward_frame.2 = (f32[256,256]{1,0:T(8,128)}, f32[256,64]{1,0:T(8,128)}, f32[256,64]{1,0:T(8,128)}, bf16[256,64]{1,0:T(8,128)(2,1)}, bf16[8,64,256]{2,1,0:T(8,128)(2,1)}, /*index=5*/f32[1,256]{1,0:T(1,128)}) custom-call(s32[1]{0:T(128)} %bitcast.4.refs_0_, f32[256,1]{1,0:T(8,128)} %copy.106.refs_1_, bf16[256,256]{1,0:T(8,128)(2,1)} %copy.107.refs_2_, ...), custom_call_target="tpu_custom_call" | custom-call | flops 1400000000 | bytes 4200000 | tf_op jit(solution)/shard_map/forward_frame/pallas_call | solution.py:190
  129.7 3.4 %all-to-all-start.3 = ((bf16[8,64,256]{2,1,0:T(8,128)(2,1)}), bf16[8,64,256]{2,1,0:T(8,128)(2,1)S(1)}, u32[]{:S(2)}, u32[]{:S(2)}) async-start(bf16[8,64,256]{2,1,0:T(8,128)(2,1)} %get-tuple-element.68), calls=%async_computation.3 | async-start | bytes 524288 | tf_op jit(solution)/shard_map/all_to_all | solution.py:745
  136.4 6.0 %all-gather = bf16[1024,64]{1,0:T(8,128)(2,1)S(1)} all-gather(bf16[256,64]{1,0:T(8,128)(2,1)} %get-tuple-element.65), channel_id=2, replica_groups=mesh['tile'=4,'dp'=8] {'tile'}, dimensions={0}, use_global_device_ids=true | all-gather | bytes 163840 | tf_op jit(solution)/shard_map/all_gather | solution.py:730
  143.3 7.0 %forward_frame.3 = (f32[256,256]{1,0:T(8,128)}, f32[256,64]{1,0:T(8,128)}, f32[256,64]{1,0:T(8,128)}, bf16[256,64]{1,0:T(8,128)(2,1)}, bf16[8,64,256]{2,1,0:T(8,128)(2,1)}, /*index=5*/f32[1,256]{1,0:T(1,128)}) custom-call(s32[1]{0:T(128)} %bitcast.4.refs_0_, f32[256,1]{1,0:T(8,128)} %copy.110.refs_1_, bf16[256,256]{1,0:T(8,128)(2,1)} %copy.111.refs_2_, ...), custom_call_target="tpu_custom_call" | custom-call | flops 1400000000 | bytes 4200000 | tf_op jit(solution)/shard_map/forward_frame/pallas_call | solution.py:190
  151.0 5.2 %all-gather.2 = f32[4,2,256]{2,1,0:T(2,128)S(1)} all-gather(f32[1,2,256]{2,1,0:T(2,128)S(1)} %maximum_bitcast_fusion.1), channel_id=3, replica_groups=mesh['tile'=4,'dp'=8] {'tile'}, dimensions={0}, use_global_device_ids=true | all-gather | bytes 10240 | tf_op jit(solution)/shard_map/all_gather | solution.py:746
  156.8 4.0 %backward_cell.2 = (bf16[8,256,256]{2,1,0:T(8,128)(2,1)}, f32[256,64]{1,0:T(8,128)}, f32[8,256]{1,0:T(8,128)}, f32[64,256]{1,0:T(8,128)}, f32[8,256]{1,0:T(8,128)}, /*index=5*/f32[8,64]{1,0:T(8,128)}) custom-call(f32[2]{0:T(128)} %pad_maximum_fusion.5.refs_0_, f32[4,256]{1,0:T(4,128)} %get-tuple-element.150.refs_1_, f32[1,256]{1,0:T(1,128)} %get-tuple-element.122.refs_2_, ...), custom_call_target="tpu_custom_call" | custom-call | flops 1400000000 | bytes 4200000 | tf_op jit(solution)/shard_map/backward_cell/pallas_call | solution.py:289
  160.9 5.9 %all-to-all-start.4 = ((bf16[8,256,256]{2,1,0:T(8,128)(2,1)}), bf16[8,256,256]{2,1,0:T(8,128)(2,1)}, u32[]{:S(2)}, u32[]{:S(2)}) async-start(bf16[8,256,256]{2,1,0:T(8,128)(2,1)} %get-tuple-element.74.refs_0_), calls=%async_computation.4 | async-start | bytes 2097152 | tf_op jit(solution)/shard_map/all_to_all | solution.py:790
  168.2 4.8 %hidden_gradient.1 = (f32[256,64]{1,0:T(8,128)}, f32[256,64]{1,0:T(8,128)}, f32[256,64]{1,0:T(8,128)}, f32[256,64]{1,0:T(8,128)}) custom-call(s32[1]{0:T(128)} %bitcast.me_ref.refs_0_, bf16[8,256,256]{2,1,0:T(8,128)(2,1)} %get-tuple-element.74.refs_0_, bf16[25,2,256,256]{3,2,1,0:T(8,128)(2,1)} %bitcast.164), custom_call_target="tpu_custom_call" | custom-call | flops 1400000000 | bytes 4200000 | tf_op jit(solution)/shard_map/hidden_gradient/pallas_call | solution.py:361
  173.1 1.5 collective-permute-start.4
  175.7 1.5 collective-permute-start.7
  177.2 2.5 collective-permute-done.4.refs_12_
  179.7 1.9 collective-permute-done.5.refs_13_
  182.3 4.2 %backward_cell.3 = (bf16[8,256,256]{2,1,0:T(8,128)(2,1)}, f32[256,64]{1,0:T(8,128)}, f32[8,256]{1,0:T(8,128)}, f32[64,256]{1,0:T(8,128)}, f32[8,256]{1,0:T(8,128)}, /*index=5*/f32[8,64]{1,0:T(8,128)}) custom-call(f32[2]{0:T(128)} %pad_maximum_fusion.5.refs_0_, f32[4,256]{1,0:T(4,128)} %get-tuple-element.151.refs_1_, f32[1,256]{1,0:T(1,128)} %get-tuple-element.121.refs_2_, ...), custom_call_target="tpu_custom_call" | custom-call | flops 1400000000 | bytes 4200000 | tf_op jit(solution)/shard_map/backward_cell/pallas_call | solution.py:289
  186.5 0.9 fusion.15
  187.6 1.0 collective-permute-start.8
  188.6 4.6 %all-to-all-done.4.refs_1_ = bf16[8,256,256]{2,1,0:T(8,128)(2,1)} async-done(((bf16[8,256,256]{2,1,0:T(8,128)(2,1)}), bf16[8,256,256]{2,1,0:T(8,128)(2,1)}, u32[]{:S(2)}, u32[]{:S(2)}) %all-to-all-start.4) | async-done | bytes 1048608 | tf_op jit(solution)/shard_map/all_to_all | solution.py:790
  193.2 3.6 %all-to-all-start.5 = ((bf16[8,256,256]{2,1,0:T(8,128)(2,1)}), bf16[8,256,256]{2,1,0:T(8,128)(2,1)S(1)}, u32[]{:S(2)}, u32[]{:S(2)}) async-start(bf16[8,256,256]{2,1,0:T(8,128)(2,1)} %get-tuple-element.88), calls=%async_computation.5 | async-start | bytes 2097152 | tf_op jit(solution)/shard_map/all_to_all | solution.py:790
  197.8 1.5 add.119.refs_0_
  199.3 1.5 collective-permute-start.13
  202.2 8.9 %owned_patches.3.refs_0_ = bf16[1600,2048]{1,0:T(8,128)(2,1)} custom-call(s32[10]{0:T(128)} %stack.97.refs_0_, f32[8,1,256]{2,1,0:T(1,128)} %reshape_squeeze.19.refs_1_, f32[256,2]{1,0:T(8,128)} %bitcast.186, bf16[8,64,256]{2,1,0:T(8,128)(2,1)} %copy-done.6, bf16[8,64,256]{2,1,0:T(8,128)(2,1)} %copy-done.23, bf16[8,64,256]{2,1,0:T(8,128)(2,1)} %copy-done.22, ...), custom_call_target="tpu_custom_call" | custom-call | flops 3150000128 | bytes 9450000 | tf_op jit(solution)/shard_map/owned_patches/pallas_call | solution.py:422
  211.1 5.1 %patch_gradient.3.refs_1_.refs_2_ = f32[1600,256]{1,0:T(8,128)} custom-call(bf16[1600,2048]{1,0:T(8,128)(2,1)} %owned_patches.3.refs_0_, bf16[8,256,256]{2,1,0:T(8,128)(2,1)} %all-to-all-done.4.refs_1_), custom_call_target="tpu_custom_call" | custom-call | flops 1750000000 | bytes 5250000 | tf_op jit(solution)/shard_map/patch_gradient/pallas_call | solution.py:503
  216.2 2.9 fusion.7
  219.2 3.0 %fusion.10.refs_2_ = f32[2,256]{1,0:T(2,128)S(1)} fusion(f32[2,256]{1,0:T(2,128)S(1)} %fusion.7, bf16[25,512,256]{2,1,0:T(8,128)(2,1)} %bitcast.166, f32[2,25,256]{2,1,0:T(8,128)} %bitcast.177), kind=kOutput, calls=%fused_computation.7 | convolution fusion | flops 6554112 | bytes 3346432 | tf_op jit(solution)/shard_map/ktg,tcg->kc/dot_general | solution.py:822
  222.3 1.3 collective-permute-start.10
  224.6 1.0 copy-done.4
  225.7 1.0 collective-permute-done.11
  226.7 1.2 collective-permute-done.10
  228.5 1.0 collective-permute-start.16
  229.8 0.9 reshape.222.refs_3_
  230.7 5.7 %patch_gradient.4 = (f32[1600,256]{1,0:T(8,128)}, f32[1,128]{1,0:T(1,128)}) custom-call(bf16[1600,2048]{1,0:T(8,128)(2,1)} %owned_patches.2.refs_0_.refs_16_, bf16[8,256,256]{2,1,0:T(8,128)(2,1)} %copy-done.1, f32[1600,256]{1,0:T(8,128)} %patch_gradient.3.refs_1_.refs_2_, f32[2,1,1,2,32,256]{5,4,3,2,1,0:T(8,128)} %reshape.222.refs_3_), custom_call_target="tpu_custom_call" | custom-call | flops 1750000000 | bytes 5250000 | tf_op jit(solution)/shard_map/patch_gradient/pallas_call | solution.py:503
  237.8 5.3 %all-to-all-start.6 = ((f32[32,24,128]{2,1,0:T(8,128)}), f32[32,24,128]{2,1,0:T(8,128)S(1)}, u32[]{:S(2)}, u32[]{:S(2)}) async-start(f32[32,24,128]{2,1,0:T(8,128)} %broadcast_in_dim.61.refs_4_), calls=%async_computation.6 | async-start | bytes 786432 | tf_op jit(solution)/shard_map/all_to_all | solution.py:865
  243.2 9.5 %patch_gradient.5 = (f32[1600,256]{1,0:T(8,128)}, f32[1600,256]{1,0:T(8,128)}, f32[1600,256]{1,0:T(8,128)}) custom-call(bf16[1600,2048]{1,0:T(8,128)(2,1)} %owned_patches.3.refs_0_, bf16[8,256,256]{2,1,0:T(8,128)(2,1)} %collective-permute-done.12.refs_1_, bf16[8,256,256]{2,1,0:T(8,128)(2,1)} %after.6.refs_2_, ...), custom_call_target="tpu_custom_call" | custom-call | flops 3150000128 | bytes 9450000 | tf_op jit(solution)/shard_map/patch_gradient/pallas_call | solution.py:503
  252.6 5.2 %all-to-all-done.6.refs_1_.refs_2_ = f32[32,24,128]{2,1,0:T(8,128)S(1)} async-done(((f32[32,24,128]{2,1,0:T(8,128)}), f32[32,24,128]{2,1,0:T(8,128)S(1)}, u32[]{:S(2)}, u32[]{:S(2)}) %all-to-all-start.6) | async-done | bytes 393248 | tf_op jit(solution)/shard_map/all_to_all | solution.py:865
  263.4 1.0 copy-done.5
  264.4 23.1 %last_update.1 = (f32[1600,1024]{1,0:T(8,128)}, f32[1600,1024]{1,0:T(8,128)}, f32[1600,1024]{1,0:T(8,128)}, f32[1,1]{1,0:T(1,128)}, f32[1,1]{1,0:T(1,128)}, /*in...) custom-call(s32[1]{0:T(128)} %bitcast.me_ref.refs_0_, ...), custom_call_target="tpu_custom_call" | custom-call | flops 7699999744 | bytes 23100000 | tf_op jit(solution)/shard_map/last_update/pallas_call | solution.py:598
  (223 shorter events, 33.2 us)
Async XLA Ops:
  7.2 114.9 %all-gather.5.cloned.1.call-start = ((), (), s32[]{:S(2)}) async-start(), calls=%async_computation.7 | async-start | bytes 7372800 | tf_op jit(solution)/shard_map/all_gather | solution.py:668
  7.9 4.5 %copy-start.18 = (s32[1,2,2,32]{3,2,1,0:T(2,128)S(1)}, s32[1,2,2,32]{3,2,1,0:T(2,128)}, u32[]{:S(2)}) copy-start(s32[1,2,2,32]{3,2,1,0:T(2,128)} %param.21) | copy-start | bytes 1540
  7.9 4.6 %copy-start.19 = (f32[1,2,2,32]{3,2,1,0:T(2,128)S(1)}, f32[1,2,2,32]{3,2,1,0:T(2,128)}, u32[]{:S(2)}) copy-start(f32[1,2,2,32]{3,2,1,0:T(2,128)} %param.20) | copy-start | bytes 1540
  7.9 4.6 %copy-start.20 = (f32[1,2,2,32]{3,2,1,0:T(2,128)S(1)}, f32[1,2,2,32]{3,2,1,0:T(2,128)}, u32[]{:S(2)}) copy-start(f32[1,2,2,32]{3,2,1,0:T(2,128)} %param.19) | copy-start | bytes 1540
  7.9 13.0 %copy-start.16 = (f32[3,256]{1,0:T(4,128)S(1)}, f32[3,256]{1,0:T(4,128)}, u32[]{:S(2)}) copy-start(f32[3,256]{1,0:T(4,128)} %refs_6_.1) | copy-start | bytes 9220
  7.9 13.8 %copy-start.14 = (f32[2,1,1024]{2,1,0:T(1,128)S(1)}, f32[2,1,1024]{2,1,0:T(1,128)}, u32[]{:S(2)}) copy-start(f32[2,1,1024]{2,1,0:T(1,128)} %refs_3_.1) | copy-start | bytes 24580
  7.9 15.4 %copy-start.10 = (f32[1,1,2,32,256]{4,3,2,1,0:T(8,128)S(1)}, f32[1,1,2,32,256]{4,3,2,1,0:T(8,128)}, u32[]{:S(2)}) copy-start(f32[1,1,2,32,256]{4,3,2,1,0:T(8,128)} %param.36) | copy-start | bytes 196612
  7.9 15.5 %copy-start.11 = (f32[1,1,2,32,256]{4,3,2,1,0:T(8,128)S(1)}, f32[1,1,2,32,256]{4,3,2,1,0:T(8,128)}, u32[]{:S(2)}) copy-start(f32[1,1,2,32,256]{4,3,2,1,0:T(8,128)} %param.37) | copy-start | bytes 196612
  13.4 14.7 %all-to-all-start = ((f32[32,1,384]{2,1,0:T(1,128)}), f32[32,1,384]{2,1,0:T(1,128)S(1)}, u32[]{:S(2)}, u32[]{:S(2)}) async-start(f32[32,1,384]{2,1,0:T(1,128)} %reshape.248), calls=%async_computation | async-start | bytes 98304 | tf_op jit(solution)/shard_map/all_to_all | solution.py:27
  20.9 62.3 %copy-start.13 = (f32[2,256]{1,0:T(2,128)}, f32[2,256]{1,0:T(2,128)S(1)}, u32[]{:S(2)}) copy-start(f32[2,256]{1,0:T(2,128)S(1)} %slice.164.refs_3_) | copy-start | bytes 6148
  28.1 7.9 %all-to-all-start.1 = ((f32[4,1,8192]{2,1,0:T(1,128)}), f32[4,1,8192]{2,1,0:T(1,128)S(1)}, u32[]{:S(2)}, u32[]{:S(2)}) async-start(f32[4,1,8192]{2,1,0:T(1,128)} %reshape.250), calls=%async_computation.1 | async-start | bytes 262144 | tf_op jit(solution)/shard_map/all_to_all | solution.py:722
  38.0 20.1 %all-to-all-start.2 = ((bf16[8,64,256]{2,1,0:T(8,128)(2,1)}), bf16[8,64,256]{2,1,0:T(8,128)(2,1)S(1)}, u32[]{:S(2)}, u32[]{:S(2)}) async-start(bf16[8,64,256]{2,1,0:T(8,128)(2,1)} %broadcast_in_dim.55), calls=%async_computation.2 | async-start | bytes 524288 | tf_op jit(solution)/shard_map/all_to_all | solution.py:27
  58.1 15.2 %copy-start.7 = (bf16[8,64,256]{2,1,0:T(8,128)(2,1)}, bf16[8,64,256]{2,1,0:T(8,128)(2,1)S(1)}, u32[]{:S(2)}) copy-start(bf16[8,64,256]{2,1,0:T(8,128)(2,1)S(1)} %all-to-all-done.2.refs_3_) | copy-start | bytes 786436
  58.1 8.1 %collective-permute-start.1 = (bf16[8,64,256]{2,1,0:T(8,128)(2,1)S(1)}, bf16[8,64,256]{2,1,0:T(8,128)(2,1)S(1)}, u32[]{:S(2)}, u32[]{:S(2)}) collective-permute-start(bf16[8,64,256]{2,1,0:T(8,128)(2,1)S(1)} %all-to-all-done.2.refs_3_), channel_id=1, source_target_pairs={{0,16},{8,24},{16,0},{24,8},{1,17},{9,25},{17,1},{25,9},{2,18},{10... | collective-permute-start | bytes 786440 | tf_op jit(solution)/shard_map/ppermute | solution.py:702
  61.3 11.9 %collective-permute-start = (bf16[8,64,256]{2,1,0:T(8,128)(2,1)S(1)}, bf16[8,64,256]{2,1,0:T(8,128)(2,1)S(1)}, u32[]{:S(2)}, u32[]{:S(2)}) collective-permute-start(bf16[8,64,256]{2,1,0:T(8,128)(2,1)S(1)} %all-to-all-done.2.refs_3_), channel_id=1, source_target_pairs={{0,8},{8,0},{16,24},{24,16},{1,9},{9,1},{17,25},{25,17},{2,10},{10... | collective-permute-start | bytes 786440 | tf_op jit(solution)/shard_map/ppermute | solution.py:702
  66.1 7.1 %copy-start.24 = (bf16[8,64,256]{2,1,0:T(8,128)(2,1)}, bf16[8,64,256]{2,1,0:T(8,128)(2,1)S(1)}, u32[]{:S(2)}) copy-start(bf16[8,64,256]{2,1,0:T(8,128)(2,1)S(1)} %collective-permute-done.1.refs_5_) | copy-start | bytes 786436
  66.1 7.1 %collective-permute-start.2 = (bf16[8,64,256]{2,1,0:T(8,128)(2,1)S(1)}, bf16[8,64,256]{2,1,0:T(8,128)(2,1)S(1)}, u32[]{:S(2)}, u32[]{:S(2)}) collective-permute-start(bf16[8,64,256]{2,1,0:T(8,128)(2,1)S(1)} %collective-permute-done.1.refs_5_), channel_id=1, source_target_pairs={{0,8},{8,0},{16,24},{24,16},{1,9},{9,1},{17,25},{25,17},{2,10},{10... | collective-permute-start | bytes 786440 | tf_op jit(solution)/shard_map/ppermute | solution.py:702
  129.7 20.6 %copy-start.21 = (f32[1,256]{1,0:T(1,128)S(1)}, f32[1,256]{1,0:T(1,128)}, u32[]{:S(2)}) copy-start(f32[1,256]{1,0:T(1,128)} %get-tuple-element.64) | copy-start | bytes 3076
  129.7 26.5 %all-to-all-start.3 = ((bf16[8,64,256]{2,1,0:T(8,128)(2,1)}), bf16[8,64,256]{2,1,0:T(8,128)(2,1)S(1)}, u32[]{:S(2)}, u32[]{:S(2)}) async-start(bf16[8,64,256]{2,1,0:T(8,128)(2,1)} %get-tuple-element.68), calls=%async_computation.3 | async-start | bytes 524288 | tf_op jit(solution)/shard_map/all_to_all | solution.py:745
  156.2 21.0 %copy-start.6 = (bf16[8,64,256]{2,1,0:T(8,128)(2,1)}, bf16[8,64,256]{2,1,0:T(8,128)(2,1)S(1)}, u32[]{:S(2)}) copy-start(bf16[8,64,256]{2,1,0:T(8,128)(2,1)S(1)} %all-to-all-done.3.refs_3_) | copy-start | bytes 786436
  156.8 18.1 %copy-start.8 = (f32[256,64]{1,0:T(8,128)S(1)}, f32[256,64]{1,0:T(8,128)}, u32[]{:S(2)}) copy-start(f32[256,64]{1,0:T(8,128)} %get-tuple-element.90) | copy-start | bytes 196612
  156.8 18.1 %copy-start.9 = (f32[256,64]{1,0:T(8,128)S(1)}, f32[256,64]{1,0:T(8,128)}, u32[]{:S(2)}) copy-start(f32[256,64]{1,0:T(8,128)} %get-tuple-element.89) | copy-start | bytes 196612
  160.9 32.3 %all-to-all-start.4 = ((bf16[8,256,256]{2,1,0:T(8,128)(2,1)}), bf16[8,256,256]{2,1,0:T(8,128)(2,1)}, u32[]{:S(2)}, u32[]{:S(2)}) async-start(bf16[8,256,256]{2,1,0:T(8,128)(2,1)} %get-tuple-element.74.refs_0_), calls=%async_computation.4 | async-start | bytes 2097152 | tf_op jit(solution)/shard_map/all_to_all | solution.py:790
  168.1 28.9 %copy-start.17 = (f32[8,64]{1,0:T(8,128)S(1)}, f32[8,64]{1,0:T(8,128)}, u32[]{:S(2)}) copy-start(f32[8,64]{1,0:T(8,128)} %get-tuple-element.83) | copy-start | bytes 6148
  168.1 29.6 %copy-start.12 = (f32[64,256]{1,0:T(8,128)S(1)}, f32[64,256]{1,0:T(8,128)}, u32[]{:S(2)}) copy-start(f32[64,256]{1,0:T(8,128)} %get-tuple-element.80) | copy-start | bytes 196612
  173.0 4.2 %collective-permute-start.3 = (f32[256,64]{1,0:T(8,128)}, f32[256,64]{1,0:T(8,128)S(1)}, u32[]{:S(2)}, u32[]{:S(2)}) collective-permute-start(f32[256,64]{1,0:T(8,128)} %get-tuple-element.76), channel_id=1, source_target_pairs={{0,8},{8,0},{16,24},{24,16},{1,9},{9,1},{17,25},{25,17},{2,10},{10... | collective-permute-start | bytes 196616 | tf_op jit(solution)/shard_map/ppermute | solution.py:809
  173.1 6.6 %collective-permute-start.4 = (f32[256,64]{1,0:T(8,128)}, f32[256,64]{1,0:T(8,128)S(1)}, u32[]{:S(2)}, u32[]{:S(2)}) collective-permute-start(f32[256,64]{1,0:T(8,128)} %get-tuple-element.77), channel_id=1, source_target_pairs={{0,16},{8,24},{16,0},{24,8},{1,17},{9,25},{17,1},{25,9},{2,18},{10... | collective-permute-start | bytes 196616 | tf_op jit(solution)/shard_map/ppermute | solution.py:809
  174.6 7.0 %collective-permute-start.5 = (f32[256,64]{1,0:T(8,128)}, f32[256,64]{1,0:T(8,128)S(1)}, u32[]{:S(2)}, u32[]{:S(2)}) collective-permute-start(f32[256,64]{1,0:T(8,128)} %get-tuple-element.78), channel_id=1, source_target_pairs={{0,24},{8,16},{16,8},{24,0},{1,25},{9,17},{17,9},{25,1},{2,26},{10... | collective-permute-start | bytes 196616 | tf_op jit(solution)/shard_map/ppermute | solution.py:809
  175.7 11.9 %collective-permute-start.7 = (bf16[8,64,256]{2,1,0:T(8,128)(2,1)S(1)}, bf16[8,64,256]{2,1,0:T(8,128)(2,1)S(1)}, u32[]{:S(2)}, u32[]{:S(2)}) collective-permute-start(bf16[8,64,256]{2,1,0:T(8,128)(2,1)S(1)} %all-to-all-done.3.refs_3_), channel_id=1, source_target_pairs={{0,16},{8,24},{16,0},{24,8},{1,17},{9,25},{17,1},{25,9},{2,18},{10... | collective-permute-start | bytes 786440 | tf_op jit(solution)/shard_map/ppermute | solution.py:702
  177.1 23.6 %collective-permute-start.6 = (bf16[8,64,256]{2,1,0:T(8,128)(2,1)S(1)}, bf16[8,64,256]{2,1,0:T(8,128)(2,1)S(1)}, u32[]{:S(2)}, u32[]{:S(2)}) collective-permute-start(bf16[8,64,256]{2,1,0:T(8,128)(2,1)S(1)} %all-to-all-done.3.refs_3_), channel_id=1, source_target_pairs={{0,8},{8,0},{16,24},{24,16},{1,9},{9,1},{17,25},{25,17},{2,10},{10... | collective-permute-start | bytes 786440 | tf_op jit(solution)/shard_map/ppermute | solution.py:702
  177.2 4.4 %copy-start.28 = (f32[256,64]{1,0:T(8,128)}, f32[256,64]{1,0:T(8,128)S(1)}, u32[]{:S(2)}) copy-start(f32[256,64]{1,0:T(8,128)S(1)} %collective-permute-done.3.refs_11_) | copy-start | bytes 196612
  179.7 1.9 copy-start.29
  187.6 13.2 %copy-start.22 = (bf16[8,64,256]{2,1,0:T(8,128)(2,1)}, bf16[8,64,256]{2,1,0:T(8,128)(2,1)S(1)}, u32[]{:S(2)}) copy-start(bf16[8,64,256]{2,1,0:T(8,128)(2,1)S(1)} %collective-permute-done.7.refs_5_) | copy-start | bytes 786436
  187.6 13.2 %collective-permute-start.8 = (bf16[8,64,256]{2,1,0:T(8,128)(2,1)S(1)}, bf16[8,64,256]{2,1,0:T(8,128)(2,1)S(1)}, u32[]{:S(2)}, u32[]{:S(2)}) collective-permute-start(bf16[8,64,256]{2,1,0:T(8,128)(2,1)S(1)} %collective-permute-done.7.refs_5_), channel_id=1, source_target_pairs={{0,8},{8,0},{16,24},{24,16},{1,9},{9,1},{17,25},{25,17},{2,10},{10... | collective-permute-start | bytes 786440 | tf_op jit(solution)/shard_map/ppermute | solution.py:702
  193.2 35.3 %all-to-all-start.5 = ((bf16[8,256,256]{2,1,0:T(8,128)(2,1)}), bf16[8,256,256]{2,1,0:T(8,128)(2,1)S(1)}, u32[]{:S(2)}, u32[]{:S(2)}) async-start(bf16[8,256,256]{2,1,0:T(8,128)(2,1)} %get-tuple-element.88), calls=%async_computation.5 | async-start | bytes 2097152 | tf_op jit(solution)/shard_map/all_to_all | solution.py:790
  199.3 25.3 %collective-permute-start.13 = (bf16[8,256,256]{2,1,0:T(8,128)(2,1)}, bf16[8,256,256]{2,1,0:T(8,128)(2,1)S(1)}, u32[]{:S(2)}, u32[]{:S(2)}) collective-permute-start(bf16[8,256,256]{2,1,0:T(8,128)(2,1)} %all-to-all-done.4.refs_1_), channel_id=1, source_target_pairs={{0,16},{8,24},{16,0},{24,8},{1,17},{9,25},{17,1},{25,9},{2,18},{10... | collective-permute-start | bytes 3145736 | tf_op jit(solution)/shard_map/ppermute | solution.py:702
  216.2 6.0 %copy-start.3 = (f32[2,256,64]{2,1,0:T(8,128)S(1)}, f32[2,256,64]{2,1,0:T(8,128)}, u32[]{:S(2)}) copy-start(f32[2,256,64]{2,1,0:T(8,128)} %after.5) | copy-start | bytes 393220
  222.1 2.5 copy-start.15
  222.2 4.5 %collective-permute-start.11 = (f32[2,1,64,64]{3,2,1,0:T(8,128)S(1)}, f32[2,1,64,64]{3,2,1,0:T(8,128)S(1)}, u32[]{:S(2)}, u32[]{:S(2)}) collective-permute-start(f32[2,1,64,64]{3,2,1,0:T(8,128)S(1)} %get-tuple-element.113), channel_id=1, source_target_pairs={{0,24},{8,16},{16,8},{24,0},{1,25},{9,17},{17,9},{25,1},{2,26},{10... | collective-permute-start | bytes 98312 | tf_op jit(solution)/shard_map/ppermute | solution.py:834
  222.3 5.6 %collective-permute-start.10 = (f32[2,1,64,64]{3,2,1,0:T(8,128)S(1)}, f32[2,1,64,64]{3,2,1,0:T(8,128)S(1)}, u32[]{:S(2)}, u32[]{:S(2)}) collective-permute-start(f32[2,1,64,64]{3,2,1,0:T(8,128)S(1)} %get-tuple-element.114), channel_id=1, source_target_pairs={{0,16},{8,24},{16,0},{24,8},{1,17},{9,25},{17,1},{25,9},{2,18},{10... | collective-permute-start | bytes 98312 | tf_op jit(solution)/shard_map/ppermute | solution.py:834
  223.6 4.2 %collective-permute-start.9 = (f32[2,1,64,64]{3,2,1,0:T(8,128)S(1)}, f32[2,1,64,64]{3,2,1,0:T(8,128)S(1)}, u32[]{:S(2)}, u32[]{:S(2)}) collective-permute-start(f32[2,1,64,64]{3,2,1,0:T(8,128)S(1)} %get-tuple-element.115), channel_id=1, source_target_pairs={{0,8},{8,0},{16,24},{24,16},{1,9},{9,1},{17,25},{25,17},{2,10},{10... | collective-permute-start | bytes 98312 | tf_op jit(solution)/shard_map/ppermute | solution.py:834
  224.2 19.0 %collective-permute-start.12 = (bf16[8,256,256]{2,1,0:T(8,128)(2,1)}, bf16[8,256,256]{2,1,0:T(8,128)(2,1)}, u32[]{:S(2)}, u32[]{:S(2)}) collective-permute-start(bf16[8,256,256]{2,1,0:T(8,128)(2,1)} %all-to-all-done.4.refs_1_), channel_id=1, source_target_pairs={{0,8},{8,0},{16,24},{24,16},{1,9},{9,1},{17,25},{25,17},{2,10},{10... | collective-permute-start | bytes 3145736 | tf_op jit(solution)/shard_map/ppermute | solution.py:702
  225.6 17.6 %collective-permute-start.14 = (bf16[8,256,256]{2,1,0:T(8,128)(2,1)}, bf16[8,256,256]{2,1,0:T(8,128)(2,1)}, u32[]{:S(2)}, u32[]{:S(2)}) collective-permute-start(bf16[8,256,256]{2,1,0:T(8,128)(2,1)} %after.6.refs_2_), channel_id=1, source_target_pairs={{0,8},{8,0},{16,24},{24,16},{1,9},{9,1},{17,25},{25,17},{2,10},{10... | collective-permute-start | bytes 3145736 | tf_op jit(solution)/shard_map/ppermute | solution.py:702
  228.5 2.2 copy-start.1
  228.5 29.3 %collective-permute-start.16 = (bf16[8,256,256]{2,1,0:T(8,128)(2,1)S(1)}, bf16[8,256,256]{2,1,0:T(8,128)(2,1)S(1)}, u32[]{:S(2)}, u32[]{:S(2)}) collective-permute-start(bf16[8,256,256]{2,1,0:T(8,128)(2,1)S(1)} %all-to-all-done.5.refs_1_), channel_id=1, source_target_pairs={{0,16},{8,24},{16,0},{24,8},{1,17},{9,25},{17,1},{25,9},{2,18},{10... | collective-permute-start | bytes 3145736 | tf_op jit(solution)/shard_map/ppermute | solution.py:702
  237.8 20.0 %all-to-all-start.6 = ((f32[32,24,128]{2,1,0:T(8,128)}), f32[32,24,128]{2,1,0:T(8,128)S(1)}, u32[]{:S(2)}, u32[]{:S(2)}) async-start(f32[32,24,128]{2,1,0:T(8,128)} %broadcast_in_dim.61.refs_4_), calls=%async_computation.6 | async-start | bytes 786432 | tf_op jit(solution)/shard_map/all_to_all | solution.py:865
  243.1 20.3 %collective-permute-start.15 = (bf16[8,256,256]{2,1,0:T(8,128)(2,1)}, bf16[8,256,256]{2,1,0:T(8,128)(2,1)}, u32[]{:S(2)}, u32[]{:S(2)}) collective-permute-start(bf16[8,256,256]{2,1,0:T(8,128)(2,1)} %copy-done.1), channel_id=1, source_target_pairs={{0,8},{8,0},{16,24},{24,16},{1,9},{9,1},{17,25},{25,17},{2,10},{10... | collective-permute-start | bytes 3145736 | tf_op jit(solution)/shard_map/ppermute | solution.py:702
  258.9 4.4 %collective-permute-start.17 = (bf16[8,256,256]{2,1,0:T(8,128)(2,1)}, bf16[8,256,256]{2,1,0:T(8,128)(2,1)S(1)}, u32[]{:S(2)}, u32[]{:S(2)}) collective-permute-start(bf16[8,256,256]{2,1,0:T(8,128)(2,1)} %after.7.refs_18_), channel_id=1, source_target_pairs={{0,8},{8,0},{16,24},{24,16},{1,9},{9,1},{17,25},{25,17},{2,10},{10... | collective-permute-start | bytes 3145736 | tf_op jit(solution)/shard_map/ppermute | solution.py:702
  (9 other events, 7.4 us)
Sparse Core Ops, SparseCore 0:
  11.9 110.1 all-gather.4
